TPU v7x, 32 devices: a whole 2x2x4 slice. The times are simulated.
32 devices in a mesh: gx: 4 (over z), gy: 4 (over y, core), gz: 2 (over x).
Axes of the slice: x: 2, y: 2, z: 4, core: 2. Of those that a mesh axis runs over, the one named last changes fastest.
Arguments:
- operator: bfloat16 [4, 4, 2, 1152, 1152], P('gx', 'gy', 'gz'), may hold values from -0.1875 to 0.1875
- lift: bfloat16 [4, 4, 2, 1152, 128], P('gx', 'gy', 'gz'), may hold values from -0.5 to 0.5
- source: bfloat16 [4, 4, 2, 128, 256], P('gx', 'gy', 'gz'), may hold values from -6 to 6
- traces_in: bfloat16 [4, 4, 2, 1152, 256], P('gx', 'gy', 'gz'), may hold values from -6 to 6
- depth: int32 [8], replicated, may hold values from 0 to 6
- direction: int32 [8], replicated, may hold values from 0 to 1
Outputs:
- traces_out: bfloat16 [4, 4, 2, 1152, 256], P('gx', 'gy', 'gz')
All inputs are finite; a program needn't handle non-finite values.
Results may differ from a plain program's by a relative error of at most 0.008.
Values may be sent and summed in bfloat16 or wider, within the bound.
No kernel may reach another device: no remote copies, remote signals or barrier semaphores. Data moves between devices by JAX's collectives and lax.ppermute only.
A program may use at most 64 MiB of HBM per device.

v0:
```python
import jax
import jax.numpy as jnp
from jax import lax
from jax.sharding import PartitionSpec as P

RB = 32
STEPS = 6


def with_halo(value, sides, width):
    for axis, dim in sides:
        size, length = (lax.axis_size(axis), value.shape[dim])
        up = [(i, (i + 1) % size) for i in range(size - 1)]
        down = [(j, i) for i, j in up]
        last = lax.slice_in_dim(value, length - width, length, axis=dim)
        leading = lax.slice_in_dim(value, 0, width, axis=dim)
        before = lax.ppermute(last, axis, up)
        after = lax.ppermute(leading, axis, down)
        value = jnp.concatenate([before, value, after], axis=dim)
    return value


def body(operator, lift, source, traces_in, depth, direction):
    matrix = operator[0, 0, 0]
    lifted = jnp.dot(lift[0, 0, 0], source[0, 0, 0], preferred_element_type=jnp.float32)
    backward = jnp.repeat(direction == 1, RB)
    state = traces_in[0, 0, 0]
    rows = state.shape[0] // 3
    for step in range(STEPS):
        gate = jnp.repeat(depth <= step, RB).astype(jnp.float32)
        outgoing = (
            jnp.dot(matrix, state, preferred_element_type=jnp.float32) + gate * lifted
        ).astype(jnp.bfloat16)
        pieces = [outgoing[0:rows], outgoing[rows : 2 * rows], outgoing[2 * rows :]]
        near_x = with_halo(pieces[0][None], (("gx", 0),), 1)
        near_y = with_halo(pieces[1][None], (("gy", 0),), 1)
        near_z = with_halo(pieces[2][None], (("gz", 0),), 1)
        face_x = jnp.where(backward, near_x[2], near_x[0])
        face_y = jnp.where(backward, near_y[2], near_y[0])
        face_z = jnp.where(backward, near_z[2], near_z[0])
        state = jnp.concatenate([face_x, face_y, face_z], axis=0)
    return state[None, None, None]


def solution(mesh):
    placed = (
        P("gx", "gy", "gz", None, None),
        P("gx", "gy", "gz", None, None),
        P("gx", "gy", "gz", None, None),
        P("gx", "gy", "gz", None, None),
        P(),
        P(),
    )
    return jax.shard_map(
        body, mesh=mesh, in_specs=placed, out_specs=P("gx", "gy", "gz", None, None), check_vma=False
    )
```

profile of v0, /device:TPU:1, one launch (start us, length us, event | category | flops | bytes accessed | tf_op | source)
XLA Modules:
  0.0 146.6 jit_solution(12659695463636110198)
XLA Ops:
  4.7 5.4 %collective-permute-start.1 = (bf16[1,384,256]{2,1,0:T(8,128)(2,1)S(1)}, bf16[1,384,256]{2,1,0:T(8,128)(2,1)}, u32[]{:S(2)}, u32[]{:S(2)}) collective-permute-start(bf16[1,384,256]{2,1,0:T(8,128)(2,1)S(1)} %get-tuple-element.20), channel_id=1, source_target_pairs={{0,8},{8,16},{16,24},{1,9},{9,17},{17,25},{2,10},{10,18},{18,26},{... | collective-permute-start | bytes 589832 | tf_op jit(solution)/shard_map/ppermute | solution.py:17
  10.0 2.9 %collective-permute-start.2 = (bf16[1,384,256]{2,1,0:T(8,128)(2,1)S(1)}, bf16[1,384,256]{2,1,0:T(8,128)(2,1)}, u32[]{:S(2)}, u32[]{:S(2)}) collective-permute-start(bf16[1,384,256]{2,1,0:T(8,128)(2,1)S(1)} %get-tuple-element.22), channel_id=1, source_target_pairs={{2,0},{4,2},{6,4},{3,1},{5,3},{7,5},{10,8},{12,10},{14,12},{11,9},... | collective-permute-start | bytes 589832 | tf_op jit(solution)/shard_map/ppermute | solution.py:18
  12.9 3.5 %collective-permute-start.3 = (bf16[1,384,256]{2,1,0:T(8,128)(2,1)S(1)}, bf16[1,384,256]{2,1,0:T(8,128)(2,1)}, u32[]{:S(2)}, u32[]{:S(2)}) collective-permute-start(bf16[1,384,256]{2,1,0:T(8,128)(2,1)S(1)} %get-tuple-element.22), channel_id=1, source_target_pairs={{0,2},{2,4},{4,6},{1,3},{3,5},{5,7},{8,10},{10,12},{12,14},{9,11},... | collective-permute-start | bytes 589832 | tf_op jit(solution)/shard_map/ppermute | solution.py:17
  17.7 5.3 %collective-permute-start.5 = (bf16[1,384,256]{2,1,0:T(8,128)(2,1)S(1)}, bf16[1,384,256]{2,1,0:T(8,128)(2,1)}, u32[]{:S(2)}, u32[]{:S(2)}) collective-permute-start(bf16[1,384,256]{2,1,0:T(8,128)(2,1)S(1)} %get-tuple-element.21), channel_id=1, source_target_pairs={{0,1},{2,3},{4,5},{6,7},{8,9},{10,11},{12,13},{14,15},{16,17},{18,... | collective-permute-start | bytes 589832 | tf_op jit(solution)/shard_map/ppermute | solution.py:17
  23.4 1.9 %collective-permute-done.4 = bf16[1,384,256]{2,1,0:T(8,128)(2,1)} collective-permute-done((bf16[1,384,256]{2,1,0:T(8,128)(2,1)S(1)}, bf16[1,384,256]{2,1,0:T(8,128)(2,1)}, u32[]{:S(2)}, u32[]{:S(2)}) %collective-permute-start.4) | collective-permute-done | bytes 196640 | tf_op jit(solution)/shard_map/ppermute | solution.py:18
  25.2 1.5 %collective-permute-done.5 = bf16[1,384,256]{2,1,0:T(8,128)(2,1)} collective-permute-done((bf16[1,384,256]{2,1,0:T(8,128)(2,1)S(1)}, bf16[1,384,256]{2,1,0:T(8,128)(2,1)}, u32[]{:S(2)}, u32[]{:S(2)}) %collective-permute-start.5) | collective-permute-done | bytes 196640 | tf_op jit(solution)/shard_map/ppermute | solution.py:17
  26.7 1.3 bitcast_select_fusion.17
  30.4 4.9 %collective-permute-start.11 = (bf16[1,384,256]{2,1,0:T(8,128)(2,1)S(1)}, bf16[1,384,256]{2,1,0:T(8,128)(2,1)}, u32[]{:S(2)}, u32[]{:S(2)}) collective-permute-start(bf16[1,384,256]{2,1,0:T(8,128)(2,1)S(1)} %get-tuple-element.18), channel_id=1, source_target_pairs={{0,1},{2,3},{4,5},{6,7},{8,9},{10,11},{12,13},{14,15},{16,17},{18,... | collective-permute-start | bytes 589832 | tf_op jit(solution)/shard_map/ppermute | solution.py:17
  36.6 4.7 %collective-permute-start.7 = (bf16[1,384,256]{2,1,0:T(8,128)(2,1)S(1)}, bf16[1,384,256]{2,1,0:T(8,128)(2,1)}, u32[]{:S(2)}, u32[]{:S(2)}) collective-permute-start(bf16[1,384,256]{2,1,0:T(8,128)(2,1)S(1)} %get-tuple-element.17), channel_id=1, source_target_pairs={{0,8},{8,16},{16,24},{1,9},{9,17},{17,25},{2,10},{10,18},{18,26},{... | collective-permute-start | bytes 589832 | tf_op jit(solution)/shard_map/ppermute | solution.py:17
  41.3 3.5 %collective-permute-start.8 = (bf16[1,384,256]{2,1,0:T(8,128)(2,1)S(1)}, bf16[1,384,256]{2,1,0:T(8,128)(2,1)}, u32[]{:S(2)}, u32[]{:S(2)}) collective-permute-start(bf16[1,384,256]{2,1,0:T(8,128)(2,1)S(1)} %get-tuple-element.19), channel_id=1, source_target_pairs={{2,0},{4,2},{6,4},{3,1},{5,3},{7,5},{10,8},{12,10},{14,12},{11,9},... | collective-permute-start | bytes 589832 | tf_op jit(solution)/shard_map/ppermute | solution.py:18
  44.8 2.0 %collective-permute-start.9 = (bf16[1,384,256]{2,1,0:T(8,128)(2,1)S(1)}, bf16[1,384,256]{2,1,0:T(8,128)(2,1)}, u32[]{:S(2)}, u32[]{:S(2)}) collective-permute-start(bf16[1,384,256]{2,1,0:T(8,128)(2,1)S(1)} %get-tuple-element.19), channel_id=1, source_target_pairs={{0,2},{2,4},{4,6},{1,3},{3,5},{5,7},{8,10},{10,12},{12,14},{9,11},... | collective-permute-start | bytes 589832 | tf_op jit(solution)/shard_map/ppermute | solution.py:17
  53.1 4.7 %collective-permute-start.13 = (bf16[1,384,256]{2,1,0:T(8,128)(2,1)S(1)}, bf16[1,384,256]{2,1,0:T(8,128)(2,1)}, u32[]{:S(2)}, u32[]{:S(2)}) collective-permute-start(bf16[1,384,256]{2,1,0:T(8,128)(2,1)S(1)} %get-tuple-element.14), channel_id=1, source_target_pairs={{0,8},{8,16},{16,24},{1,9},{9,17},{17,25},{2,10},{10,18},{18,26},{... | collective-permute-start | bytes 589832 | tf_op jit(solution)/shard_map/ppermute | solution.py:17
  57.8 1.9 %collective-permute-start.14 = (bf16[1,384,256]{2,1,0:T(8,128)(2,1)S(1)}, bf16[1,384,256]{2,1,0:T(8,128)(2,1)}, u32[]{:S(2)}, u32[]{:S(2)}) collective-permute-start(bf16[1,384,256]{2,1,0:T(8,128)(2,1)S(1)} %get-tuple-element.16), channel_id=1, source_target_pairs={{2,0},{4,2},{6,4},{3,1},{5,3},{7,5},{10,8},{12,10},{14,12},{11,9},... | collective-permute-start | bytes 589832 | tf_op jit(solution)/shard_map/ppermute | solution.py:18
  59.7 5.1 %collective-permute-start.15 = (bf16[1,384,256]{2,1,0:T(8,128)(2,1)S(1)}, bf16[1,384,256]{2,1,0:T(8,128)(2,1)}, u32[]{:S(2)}, u32[]{:S(2)}) collective-permute-start(bf16[1,384,256]{2,1,0:T(8,128)(2,1)S(1)} %get-tuple-element.16), channel_id=1, source_target_pairs={{0,2},{2,4},{4,6},{1,3},{3,5},{5,7},{8,10},{10,12},{12,14},{9,11},... | collective-permute-start | bytes 589832 | tf_op jit(solution)/shard_map/ppermute | solution.py:17
  66.1 5.3 %collective-permute-start.17 = (bf16[1,384,256]{2,1,0:T(8,128)(2,1)S(1)}, bf16[1,384,256]{2,1,0:T(8,128)(2,1)}, u32[]{:S(2)}, u32[]{:S(2)}) collective-permute-start(bf16[1,384,256]{2,1,0:T(8,128)(2,1)S(1)} %get-tuple-element.15), channel_id=1, source_target_pairs={{0,1},{2,3},{4,5},{6,7},{8,9},{10,11},{12,13},{14,15},{16,17},{18,... | collective-permute-start | bytes 589832 | tf_op jit(solution)/shard_map/ppermute | solution.py:17
  71.9 2.3 %collective-permute-done.17 = bf16[1,384,256]{2,1,0:T(8,128)(2,1)} collective-permute-done((bf16[1,384,256]{2,1,0:T(8,128)(2,1)S(1)}, bf16[1,384,256]{2,1,0:T(8,128)(2,1)}, u32[]{:S(2)}, u32[]{:S(2)}) %collective-permute-start.17) | collective-permute-done | bytes 196640 | tf_op jit(solution)/shard_map/ppermute | solution.py:17
  77.8 4.7 %collective-permute-start.19 = (bf16[1,384,256]{2,1,0:T(8,128)(2,1)S(1)}, bf16[1,384,256]{2,1,0:T(8,128)(2,1)}, u32[]{:S(2)}, u32[]{:S(2)}) collective-permute-start(bf16[1,384,256]{2,1,0:T(8,128)(2,1)S(1)} %get-tuple-element.11), channel_id=1, source_target_pairs={{0,8},{8,16},{16,24},{1,9},{9,17},{17,25},{2,10},{10,18},{18,26},{... | collective-permute-start | bytes 589832 | tf_op jit(solution)/shard_map/ppermute | solution.py:17
  82.5 1.9 %collective-permute-start.20 = (bf16[1,384,256]{2,1,0:T(8,128)(2,1)S(1)}, bf16[1,384,256]{2,1,0:T(8,128)(2,1)}, u32[]{:S(2)}, u32[]{:S(2)}) collective-permute-start(bf16[1,384,256]{2,1,0:T(8,128)(2,1)S(1)} %get-tuple-element.13), channel_id=1, source_target_pairs={{2,0},{4,2},{6,4},{3,1},{5,3},{7,5},{10,8},{12,10},{14,12},{11,9},... | collective-permute-start | bytes 589832 | tf_op jit(solution)/shard_map/ppermute | solution.py:18
  84.4 4.1 %collective-permute-start.21 = (bf16[1,384,256]{2,1,0:T(8,128)(2,1)S(1)}, bf16[1,384,256]{2,1,0:T(8,128)(2,1)}, u32[]{:S(2)}, u32[]{:S(2)}) collective-permute-start(bf16[1,384,256]{2,1,0:T(8,128)(2,1)S(1)} %get-tuple-element.13), channel_id=1, source_target_pairs={{0,2},{2,4},{4,6},{1,3},{3,5},{5,7},{8,10},{10,12},{12,14},{9,11},... | collective-permute-start | bytes 589832 | tf_op jit(solution)/shard_map/ppermute | solution.py:17
  89.9 5.6 %collective-permute-start.23 = (bf16[1,384,256]{2,1,0:T(8,128)(2,1)S(1)}, bf16[1,384,256]{2,1,0:T(8,128)(2,1)}, u32[]{:S(2)}, u32[]{:S(2)}) collective-permute-start(bf16[1,384,256]{2,1,0:T(8,128)(2,1)S(1)} %get-tuple-element.12), channel_id=1, source_target_pairs={{0,1},{2,3},{4,5},{6,7},{8,9},{10,11},{12,13},{14,15},{16,17},{18,... | collective-permute-start | bytes 589832 | tf_op jit(solution)/shard_map/ppermute | solution.py:17
  96.6 2.3 %collective-permute-done.23 = bf16[1,384,256]{2,1,0:T(8,128)(2,1)} collective-permute-done((bf16[1,384,256]{2,1,0:T(8,128)(2,1)S(1)}, bf16[1,384,256]{2,1,0:T(8,128)(2,1)}, u32[]{:S(2)}, u32[]{:S(2)}) %collective-permute-start.23) | collective-permute-done | bytes 196640 | tf_op jit(solution)/shard_map/ppermute | solution.py:17
  102.6 4.7 %collective-permute-start.25 = (bf16[1,384,256]{2,1,0:T(8,128)(2,1)S(1)}, bf16[1,384,256]{2,1,0:T(8,128)(2,1)}, u32[]{:S(2)}, u32[]{:S(2)}) collective-permute-start(bf16[1,384,256]{2,1,0:T(8,128)(2,1)S(1)} %get-tuple-element.8), channel_id=1, source_target_pairs={{0,8},{8,16},{16,24},{1,9},{9,17},{17,25},{2,10},{10,18},{18,26},{... | collective-permute-start | bytes 589832 | tf_op jit(solution)/shard_map/ppermute | solution.py:17
  107.3 2.3 %collective-permute-start.26 = (bf16[1,384,256]{2,1,0:T(8,128)(2,1)S(1)}, bf16[1,384,256]{2,1,0:T(8,128)(2,1)}, u32[]{:S(2)}, u32[]{:S(2)}) collective-permute-start(bf16[1,384,256]{2,1,0:T(8,128)(2,1)S(1)} %get-tuple-element.10), channel_id=1, source_target_pairs={{2,0},{4,2},{6,4},{3,1},{5,3},{7,5},{10,8},{12,10},{14,12},{11,9},... | collective-permute-start | bytes 589832 | tf_op jit(solution)/shard_map/ppermute | solution.py:18
  109.6 3.3 %collective-permute-start.27 = (bf16[1,384,256]{2,1,0:T(8,128)(2,1)S(1)}, bf16[1,384,256]{2,1,0:T(8,128)(2,1)}, u32[]{:S(2)}, u32[]{:S(2)}) collective-permute-start(bf16[1,384,256]{2,1,0:T(8,128)(2,1)S(1)} %get-tuple-element.10), channel_id=1, source_target_pairs={{0,2},{2,4},{4,6},{1,3},{3,5},{5,7},{8,10},{10,12},{12,14},{9,11},... | collective-permute-start | bytes 589832 | tf_op jit(solution)/shard_map/ppermute | solution.py:17
  114.2 5.4 %collective-permute-start.29 = (bf16[1,384,256]{2,1,0:T(8,128)(2,1)S(1)}, bf16[1,384,256]{2,1,0:T(8,128)(2,1)}, u32[]{:S(2)}, u32[]{:S(2)}) collective-permute-start(bf16[1,384,256]{2,1,0:T(8,128)(2,1)S(1)} %get-tuple-element.9), channel_id=1, source_target_pairs={{0,1},{2,3},{4,5},{6,7},{8,9},{10,11},{12,13},{14,15},{16,17},{18,... | collective-permute-start | bytes 589832 | tf_op jit(solution)/shard_map/ppermute | solution.py:17
  119.7 1.9 %collective-permute-done.28 = bf16[1,384,256]{2,1,0:T(8,128)(2,1)} collective-permute-done((bf16[1,384,256]{2,1,0:T(8,128)(2,1)S(1)}, bf16[1,384,256]{2,1,0:T(8,128)(2,1)}, u32[]{:S(2)}, u32[]{:S(2)}) %collective-permute-start.28) | collective-permute-done | bytes 196640 | tf_op jit(solution)/shard_map/ppermute | solution.py:18
  121.6 1.5 %collective-permute-done.29 = bf16[1,384,256]{2,1,0:T(8,128)(2,1)} collective-permute-done((bf16[1,384,256]{2,1,0:T(8,128)(2,1)S(1)}, bf16[1,384,256]{2,1,0:T(8,128)(2,1)}, u32[]{:S(2)}, u32[]{:S(2)}) %collective-permute-start.29) | collective-permute-done | bytes 196640 | tf_op jit(solution)/shard_map/ppermute | solution.py:17
  126.7 4.0 %collective-permute-start.31 = (bf16[1,384,256]{2,1,0:T(8,128)(2,1)S(1)}, bf16[1,384,256]{2,1,0:T(8,128)(2,1)S(1)}, u32[]{:S(2)}, u32[]{:S(2)}) collective-permute-start(bf16[1,384,256]{2,1,0:T(8,128)(2,1)S(1)} %get-tuple-element.5), channel_id=1, source_target_pairs={{0,8},{8,16},{16,24},{1,9},{9,17},{17,25},{2,10},{10,18},{18,26},{... | collective-permute-start | bytes 589832 | tf_op jit(solution)/shard_map/ppermute | solution.py:17
  130.7 3.4 %collective-permute-start.32 = (bf16[1,384,256]{2,1,0:T(8,128)(2,1)S(1)}, bf16[1,384,256]{2,1,0:T(8,128)(2,1)S(1)}, u32[]{:S(2)}, u32[]{:S(2)}) collective-permute-start(bf16[1,384,256]{2,1,0:T(8,128)(2,1)S(1)} %get-tuple-element.7), channel_id=1, source_target_pairs={{2,0},{4,2},{6,4},{3,1},{5,3},{7,5},{10,8},{12,10},{14,12},{11,9},... | collective-permute-start | bytes 589832 | tf_op jit(solution)/shard_map/ppermute | solution.py:18
  134.1 2.2 %collective-permute-start.33 = (bf16[1,384,256]{2,1,0:T(8,128)(2,1)S(1)}, bf16[1,384,256]{2,1,0:T(8,128)(2,1)S(1)}, u32[]{:S(2)}, u32[]{:S(2)}) collective-permute-start(bf16[1,384,256]{2,1,0:T(8,128)(2,1)S(1)} %get-tuple-element.7), channel_id=1, source_target_pairs={{0,2},{2,4},{4,6},{1,3},{3,5},{5,7},{8,10},{10,12},{12,14},{9,11},... | collective-permute-start | bytes 589832 | tf_op jit(solution)/shard_map/ppermute | solution.py:17
  137.6 4.2 %collective-permute-start.35 = (bf16[1,384,256]{2,1,0:T(8,128)(2,1)S(1)}, bf16[1,384,256]{2,1,0:T(8,128)(2,1)S(1)}, u32[]{:S(2)}, u32[]{:S(2)}) collective-permute-start(bf16[1,384,256]{2,1,0:T(8,128)(2,1)S(1)} %get-tuple-element.6), channel_id=1, source_target_pairs={{0,1},{2,3},{4,5},{6,7},{8,9},{10,11},{12,13},{14,15},{16,17},{18,... | collective-permute-start | bytes 589832 | tf_op jit(solution)/shard_map/ppermute | solution.py:17
  141.8 3.0 %collective-permute-done.34 = bf16[1,384,256]{2,1,0:T(8,128)(2,1)S(1)} collective-permute-done((bf16[1,384,256]{2,1,0:T(8,128)(2,1)S(1)}, bf16[1,384,256]{2,1,0:T(8,128)(2,1)S(1)}, u32[]{:S(2)}, u32[]{:S(2)}) %collective-permute-start.34) | collective-permute-done | bytes 196640 | tf_op jit(solution)/shard_map/ppermute | solution.py:18
  (94 shorter events, 35.6 us)
Async XLA Ops:
  3.4 14.3 %collective-permute-start = (bf16[1,384,256]{2,1,0:T(8,128)(2,1)S(1)}, bf16[1,384,256]{2,1,0:T(8,128)(2,1)S(1)}, u32[]{:S(2)}, u32[]{:S(2)}) collective-permute-start(bf16[1,384,256]{2,1,0:T(8,128)(2,1)S(1)} %get-tuple-element.20), channel_id=1, source_target_pairs={{8,0},{16,8},{24,16},{9,1},{17,9},{25,17},{10,2},{18,10},{26,18},{... | collective-permute-start | bytes 589832 | tf_op jit(solution)/shard_map/ppermute | solution.py:18
  4.7 18.7 %collective-permute-start.1 = (bf16[1,384,256]{2,1,0:T(8,128)(2,1)S(1)}, bf16[1,384,256]{2,1,0:T(8,128)(2,1)}, u32[]{:S(2)}, u32[]{:S(2)}) collective-permute-start(bf16[1,384,256]{2,1,0:T(8,128)(2,1)S(1)} %get-tuple-element.20), channel_id=1, source_target_pairs={{0,8},{8,16},{16,24},{1,9},{9,17},{17,25},{2,10},{10,18},{18,26},{... | collective-permute-start | bytes 589832 | tf_op jit(solution)/shard_map/ppermute | solution.py:17
  10.0 13.3 %collective-permute-start.2 = (bf16[1,384,256]{2,1,0:T(8,128)(2,1)S(1)}, bf16[1,384,256]{2,1,0:T(8,128)(2,1)}, u32[]{:S(2)}, u32[]{:S(2)}) collective-permute-start(bf16[1,384,256]{2,1,0:T(8,128)(2,1)S(1)} %get-tuple-element.22), channel_id=1, source_target_pairs={{2,0},{4,2},{6,4},{3,1},{5,3},{7,5},{10,8},{12,10},{14,12},{11,9},... | collective-permute-start | bytes 589832 | tf_op jit(solution)/shard_map/ppermute | solution.py:18
  12.9 10.5 %collective-permute-start.3 = (bf16[1,384,256]{2,1,0:T(8,128)(2,1)S(1)}, bf16[1,384,256]{2,1,0:T(8,128)(2,1)}, u32[]{:S(2)}, u32[]{:S(2)}) collective-permute-start(bf16[1,384,256]{2,1,0:T(8,128)(2,1)S(1)} %get-tuple-element.22), channel_id=1, source_target_pairs={{0,2},{2,4},{4,6},{1,3},{3,5},{5,7},{8,10},{10,12},{12,14},{9,11},... | collective-permute-start | bytes 589832 | tf_op jit(solution)/shard_map/ppermute | solution.py:17
  16.4 8.9 %collective-permute-start.4 = (bf16[1,384,256]{2,1,0:T(8,128)(2,1)S(1)}, bf16[1,384,256]{2,1,0:T(8,128)(2,1)}, u32[]{:S(2)}, u32[]{:S(2)}) collective-permute-start(bf16[1,384,256]{2,1,0:T(8,128)(2,1)S(1)} %get-tuple-element.21), channel_id=1, source_target_pairs={{1,0},{3,2},{5,4},{7,6},{9,8},{11,10},{13,12},{15,14},{17,16},{19,... | collective-permute-start | bytes 589832 | tf_op jit(solution)/shard_map/ppermute | solution.py:18
  17.7 9.0 %collective-permute-start.5 = (bf16[1,384,256]{2,1,0:T(8,128)(2,1)S(1)}, bf16[1,384,256]{2,1,0:T(8,128)(2,1)}, u32[]{:S(2)}, u32[]{:S(2)}) collective-permute-start(bf16[1,384,256]{2,1,0:T(8,128)(2,1)S(1)} %get-tuple-element.21), channel_id=1, source_target_pairs={{0,1},{2,3},{4,5},{6,7},{8,9},{10,11},{12,13},{14,15},{16,17},{18,... | collective-permute-start | bytes 589832 | tf_op jit(solution)/shard_map/ppermute | solution.py:17
  29.1 15.7 %collective-permute-start.10 = (bf16[1,384,256]{2,1,0:T(8,128)(2,1)S(1)}, bf16[1,384,256]{2,1,0:T(8,128)(2,1)S(1)}, u32[]{:S(2)}, u32[]{:S(2)}) collective-permute-start(bf16[1,384,256]{2,1,0:T(8,128)(2,1)S(1)} %get-tuple-element.18), channel_id=1, source_target_pairs={{1,0},{3,2},{5,4},{7,6},{9,8},{11,10},{13,12},{15,14},{17,16},{19,... | collective-permute-start | bytes 589832 | tf_op jit(solution)/shard_map/ppermute | solution.py:18
  30.4 16.6 %collective-permute-start.11 = (bf16[1,384,256]{2,1,0:T(8,128)(2,1)S(1)}, bf16[1,384,256]{2,1,0:T(8,128)(2,1)}, u32[]{:S(2)}, u32[]{:S(2)}) collective-permute-start(bf16[1,384,256]{2,1,0:T(8,128)(2,1)S(1)} %get-tuple-element.18), channel_id=1, source_target_pairs={{0,1},{2,3},{4,5},{6,7},{8,9},{10,11},{12,13},{14,15},{16,17},{18,... | collective-permute-start | bytes 589832 | tf_op jit(solution)/shard_map/ppermute | solution.py:17
  35.3 11.7 %collective-permute-start.6 = (bf16[1,384,256]{2,1,0:T(8,128)(2,1)S(1)}, bf16[1,384,256]{2,1,0:T(8,128)(2,1)}, u32[]{:S(2)}, u32[]{:S(2)}) collective-permute-start(bf16[1,384,256]{2,1,0:T(8,128)(2,1)S(1)} %get-tuple-element.17), channel_id=1, source_target_pairs={{8,0},{16,8},{24,16},{9,1},{17,9},{25,17},{10,2},{18,10},{26,18},{... | collective-permute-start | bytes 589832 | tf_op jit(solution)/shard_map/ppermute | solution.py:18
  36.6 10.4 %collective-permute-start.7 = (bf16[1,384,256]{2,1,0:T(8,128)(2,1)S(1)}, bf16[1,384,256]{2,1,0:T(8,128)(2,1)}, u32[]{:S(2)}, u32[]{:S(2)}) collective-permute-start(bf16[1,384,256]{2,1,0:T(8,128)(2,1)S(1)} %get-tuple-element.17), channel_id=1, source_target_pairs={{0,8},{8,16},{16,24},{1,9},{9,17},{17,25},{2,10},{10,18},{18,26},{... | collective-permute-start | bytes 589832 | tf_op jit(solution)/shard_map/ppermute | solution.py:17
  51.8 14.3 %collective-permute-start.12 = (bf16[1,384,256]{2,1,0:T(8,128)(2,1)S(1)}, bf16[1,384,256]{2,1,0:T(8,128)(2,1)S(1)}, u32[]{:S(2)}, u32[]{:S(2)}) collective-permute-start(bf16[1,384,256]{2,1,0:T(8,128)(2,1)S(1)} %get-tuple-element.14), channel_id=1, source_target_pairs={{8,0},{16,8},{24,16},{9,1},{17,9},{25,17},{10,2},{18,10},{26,18},{... | collective-permute-start | bytes 589832 | tf_op jit(solution)/shard_map/ppermute | solution.py:18
  53.1 18.5 %collective-permute-start.13 = (bf16[1,384,256]{2,1,0:T(8,128)(2,1)S(1)}, bf16[1,384,256]{2,1,0:T(8,128)(2,1)}, u32[]{:S(2)}, u32[]{:S(2)}) collective-permute-start(bf16[1,384,256]{2,1,0:T(8,128)(2,1)S(1)} %get-tuple-element.14), channel_id=1, source_target_pairs={{0,8},{8,16},{16,24},{1,9},{9,17},{17,25},{2,10},{10,18},{18,26},{... | collective-permute-start | bytes 589832 | tf_op jit(solution)/shard_map/ppermute | solution.py:17
  57.8 13.8 %collective-permute-start.14 = (bf16[1,384,256]{2,1,0:T(8,128)(2,1)S(1)}, bf16[1,384,256]{2,1,0:T(8,128)(2,1)}, u32[]{:S(2)}, u32[]{:S(2)}) collective-permute-start(bf16[1,384,256]{2,1,0:T(8,128)(2,1)S(1)} %get-tuple-element.16), channel_id=1, source_target_pairs={{2,0},{4,2},{6,4},{3,1},{5,3},{7,5},{10,8},{12,10},{14,12},{11,9},... | collective-permute-start | bytes 589832 | tf_op jit(solution)/shard_map/ppermute | solution.py:18
  59.7 11.9 %collective-permute-start.15 = (bf16[1,384,256]{2,1,0:T(8,128)(2,1)S(1)}, bf16[1,384,256]{2,1,0:T(8,128)(2,1)}, u32[]{:S(2)}, u32[]{:S(2)}) collective-permute-start(bf16[1,384,256]{2,1,0:T(8,128)(2,1)S(1)} %get-tuple-element.16), channel_id=1, source_target_pairs={{0,2},{2,4},{4,6},{1,3},{3,5},{5,7},{8,10},{10,12},{12,14},{9,11},... | collective-permute-start | bytes 589832 | tf_op jit(solution)/shard_map/ppermute | solution.py:17
  66.1 8.1 %collective-permute-start.17 = (bf16[1,384,256]{2,1,0:T(8,128)(2,1)S(1)}, bf16[1,384,256]{2,1,0:T(8,128)(2,1)}, u32[]{:S(2)}, u32[]{:S(2)}) collective-permute-start(bf16[1,384,256]{2,1,0:T(8,128)(2,1)S(1)} %get-tuple-element.15), channel_id=1, source_target_pairs={{0,1},{2,3},{4,5},{6,7},{8,9},{10,11},{12,13},{14,15},{16,17},{18,... | collective-permute-start | bytes 589832 | tf_op jit(solution)/shard_map/ppermute | solution.py:17
  76.5 13.4 %collective-permute-start.18 = (bf16[1,384,256]{2,1,0:T(8,128)(2,1)S(1)}, bf16[1,384,256]{2,1,0:T(8,128)(2,1)S(1)}, u32[]{:S(2)}, u32[]{:S(2)}) collective-permute-start(bf16[1,384,256]{2,1,0:T(8,128)(2,1)S(1)} %get-tuple-element.11), channel_id=1, source_target_pairs={{8,0},{16,8},{24,16},{9,1},{17,9},{25,17},{10,2},{18,10},{26,18},{... | collective-permute-start | bytes 589832 | tf_op jit(solution)/shard_map/ppermute | solution.py:18
  77.8 17.8 %collective-permute-start.19 = (bf16[1,384,256]{2,1,0:T(8,128)(2,1)S(1)}, bf16[1,384,256]{2,1,0:T(8,128)(2,1)}, u32[]{:S(2)}, u32[]{:S(2)}) collective-permute-start(bf16[1,384,256]{2,1,0:T(8,128)(2,1)S(1)} %get-tuple-element.11), channel_id=1, source_target_pairs={{0,8},{8,16},{16,24},{1,9},{9,17},{17,25},{2,10},{10,18},{18,26},{... | collective-permute-start | bytes 589832 | tf_op jit(solution)/shard_map/ppermute | solution.py:17
  82.5 13.1 %collective-permute-start.20 = (bf16[1,384,256]{2,1,0:T(8,128)(2,1)S(1)}, bf16[1,384,256]{2,1,0:T(8,128)(2,1)}, u32[]{:S(2)}, u32[]{:S(2)}) collective-permute-start(bf16[1,384,256]{2,1,0:T(8,128)(2,1)S(1)} %get-tuple-element.13), channel_id=1, source_target_pairs={{2,0},{4,2},{6,4},{3,1},{5,3},{7,5},{10,8},{12,10},{14,12},{11,9},... | collective-permute-start | bytes 589832 | tf_op jit(solution)/shard_map/ppermute | solution.py:18
  84.4 11.2 %collective-permute-start.21 = (bf16[1,384,256]{2,1,0:T(8,128)(2,1)S(1)}, bf16[1,384,256]{2,1,0:T(8,128)(2,1)}, u32[]{:S(2)}, u32[]{:S(2)}) collective-permute-start(bf16[1,384,256]{2,1,0:T(8,128)(2,1)S(1)} %get-tuple-element.13), channel_id=1, source_target_pairs={{0,2},{2,4},{4,6},{1,3},{3,5},{5,7},{8,10},{10,12},{12,14},{9,11},... | collective-permute-start | bytes 589832 | tf_op jit(solution)/shard_map/ppermute | solution.py:17
  88.6 8.0 %collective-permute-start.22 = (bf16[1,384,256]{2,1,0:T(8,128)(2,1)S(1)}, bf16[1,384,256]{2,1,0:T(8,128)(2,1)}, u32[]{:S(2)}, u32[]{:S(2)}) collective-permute-start(bf16[1,384,256]{2,1,0:T(8,128)(2,1)S(1)} %get-tuple-element.12), channel_id=1, source_target_pairs={{1,0},{3,2},{5,4},{7,6},{9,8},{11,10},{13,12},{15,14},{17,16},{19,... | collective-permute-start | bytes 589832 | tf_op jit(solution)/shard_map/ppermute | solution.py:18
  89.9 9.0 %collective-permute-start.23 = (bf16[1,384,256]{2,1,0:T(8,128)(2,1)S(1)}, bf16[1,384,256]{2,1,0:T(8,128)(2,1)}, u32[]{:S(2)}, u32[]{:S(2)}) collective-permute-start(bf16[1,384,256]{2,1,0:T(8,128)(2,1)S(1)} %get-tuple-element.12), channel_id=1, source_target_pairs={{0,1},{2,3},{4,5},{6,7},{8,9},{10,11},{12,13},{14,15},{16,17},{18,... | collective-permute-start | bytes 589832 | tf_op jit(solution)/shard_map/ppermute | solution.py:17
  101.3 12.9 %collective-permute-start.24 = (bf16[1,384,256]{2,1,0:T(8,128)(2,1)S(1)}, bf16[1,384,256]{2,1,0:T(8,128)(2,1)S(1)}, u32[]{:S(2)}, u32[]{:S(2)}) collective-permute-start(bf16[1,384,256]{2,1,0:T(8,128)(2,1)S(1)} %get-tuple-element.8), channel_id=1, source_target_pairs={{8,0},{16,8},{24,16},{9,1},{17,9},{25,17},{10,2},{18,10},{26,18},{... | collective-permute-start | bytes 589832 | tf_op jit(solution)/shard_map/ppermute | solution.py:18
  102.6 17.1 %collective-permute-start.25 = (bf16[1,384,256]{2,1,0:T(8,128)(2,1)S(1)}, bf16[1,384,256]{2,1,0:T(8,128)(2,1)}, u32[]{:S(2)}, u32[]{:S(2)}) collective-permute-start(bf16[1,384,256]{2,1,0:T(8,128)(2,1)S(1)} %get-tuple-element.8), channel_id=1, source_target_pairs={{0,8},{8,16},{16,24},{1,9},{9,17},{17,25},{2,10},{10,18},{18,26},{... | collective-permute-start | bytes 589832 | tf_op jit(solution)/shard_map/ppermute | solution.py:17
  107.3 12.4 %collective-permute-start.26 = (bf16[1,384,256]{2,1,0:T(8,128)(2,1)S(1)}, bf16[1,384,256]{2,1,0:T(8,128)(2,1)}, u32[]{:S(2)}, u32[]{:S(2)}) collective-permute-start(bf16[1,384,256]{2,1,0:T(8,128)(2,1)S(1)} %get-tuple-element.10), channel_id=1, source_target_pairs={{2,0},{4,2},{6,4},{3,1},{5,3},{7,5},{10,8},{12,10},{14,12},{11,9},... | collective-permute-start | bytes 589832 | tf_op jit(solution)/shard_map/ppermute | solution.py:18
  109.6 10.1 %collective-permute-start.27 = (bf16[1,384,256]{2,1,0:T(8,128)(2,1)S(1)}, bf16[1,384,256]{2,1,0:T(8,128)(2,1)}, u32[]{:S(2)}, u32[]{:S(2)}) collective-permute-start(bf16[1,384,256]{2,1,0:T(8,128)(2,1)S(1)} %get-tuple-element.10), channel_id=1, source_target_pairs={{0,2},{2,4},{4,6},{1,3},{3,5},{5,7},{8,10},{10,12},{12,14},{9,11},... | collective-permute-start | bytes 589832 | tf_op jit(solution)/shard_map/ppermute | solution.py:17
  112.8 8.7 %collective-permute-start.28 = (bf16[1,384,256]{2,1,0:T(8,128)(2,1)S(1)}, bf16[1,384,256]{2,1,0:T(8,128)(2,1)}, u32[]{:S(2)}, u32[]{:S(2)}) collective-permute-start(bf16[1,384,256]{2,1,0:T(8,128)(2,1)S(1)} %get-tuple-element.9), channel_id=1, source_target_pairs={{1,0},{3,2},{5,4},{7,6},{9,8},{11,10},{13,12},{15,14},{17,16},{19,... | collective-permute-start | bytes 589832 | tf_op jit(solution)/shard_map/ppermute | solution.py:18
  114.2 8.9 %collective-permute-start.29 = (bf16[1,384,256]{2,1,0:T(8,128)(2,1)S(1)}, bf16[1,384,256]{2,1,0:T(8,128)(2,1)}, u32[]{:S(2)}, u32[]{:S(2)}) collective-permute-start(bf16[1,384,256]{2,1,0:T(8,128)(2,1)S(1)} %get-tuple-element.9), channel_id=1, source_target_pairs={{0,1},{2,3},{4,5},{6,7},{8,9},{10,11},{12,13},{14,15},{16,17},{18,... | collective-permute-start | bytes 589832 | tf_op jit(solution)/shard_map/ppermute | solution.py:17
  125.4 12.2 %collective-permute-start.30 = (bf16[1,384,256]{2,1,0:T(8,128)(2,1)S(1)}, bf16[1,384,256]{2,1,0:T(8,128)(2,1)S(1)}, u32[]{:S(2)}, u32[]{:S(2)}) collective-permute-start(bf16[1,384,256]{2,1,0:T(8,128)(2,1)S(1)} %get-tuple-element.5), channel_id=1, source_target_pairs={{8,0},{16,8},{24,16},{9,1},{17,9},{25,17},{10,2},{18,10},{26,18},{... | collective-permute-start | bytes 589832 | tf_op jit(solution)/shard_map/ppermute | solution.py:18
  126.7 15.1 %collective-permute-start.31 = (bf16[1,384,256]{2,1,0:T(8,128)(2,1)S(1)}, bf16[1,384,256]{2,1,0:T(8,128)(2,1)S(1)}, u32[]{:S(2)}, u32[]{:S(2)}) collective-permute-start(bf16[1,384,256]{2,1,0:T(8,128)(2,1)S(1)} %get-tuple-element.5), channel_id=1, source_target_pairs={{0,8},{8,16},{16,24},{1,9},{9,17},{17,25},{2,10},{10,18},{18,26},{... | collective-permute-start | bytes 589832 | tf_op jit(solution)/shard_map/ppermute | solution.py:17
  130.7 11.1 %collective-permute-start.32 = (bf16[1,384,256]{2,1,0:T(8,128)(2,1)S(1)}, bf16[1,384,256]{2,1,0:T(8,128)(2,1)S(1)}, u32[]{:S(2)}, u32[]{:S(2)}) collective-permute-start(bf16[1,384,256]{2,1,0:T(8,128)(2,1)S(1)} %get-tuple-element.7), channel_id=1, source_target_pairs={{2,0},{4,2},{6,4},{3,1},{5,3},{7,5},{10,8},{12,10},{14,12},{11,9},... | collective-permute-start | bytes 589832 | tf_op jit(solution)/shard_map/ppermute | solution.py:18
  136.3 8.5 %collective-permute-start.34 = (bf16[1,384,256]{2,1,0:T(8,128)(2,1)S(1)}, bf16[1,384,256]{2,1,0:T(8,128)(2,1)S(1)}, u32[]{:S(2)}, u32[]{:S(2)}) collective-permute-start(bf16[1,384,256]{2,1,0:T(8,128)(2,1)S(1)} %get-tuple-element.6), channel_id=1, source_target_pairs={{1,0},{3,2},{5,4},{7,6},{9,8},{11,10},{13,12},{15,14},{17,16},{19,... | collective-permute-start | bytes 589832 | tf_op jit(solution)/shard_map/ppermute | solution.py:18
  137.6 8.2 %collective-permute-start.35 = (bf16[1,384,256]{2,1,0:T(8,128)(2,1)S(1)}, bf16[1,384,256]{2,1,0:T(8,128)(2,1)S(1)}, u32[]{:S(2)}, u32[]{:S(2)}) collective-permute-start(bf16[1,384,256]{2,1,0:T(8,128)(2,1)S(1)} %get-tuple-element.6), channel_id=1, source_target_pairs={{0,1},{2,3},{4,5},{6,7},{8,9},{10,11},{12,13},{14,15},{16,17},{18,... | collective-permute-start | bytes 589832 | tf_op jit(solution)/shard_map/ppermute | solution.py:17
  (13 other events, 73.6 us)
where the time goes:
time: 149 us; the launch traced here: 147 us
  starting transfers between devices  110 us (74%)
  waiting for transfers between devices  18.9 us (13%)
  other arithmetic  8.42 us (6%)
  matrix products  6.94 us (5%)
    ppermute x18, starting transfers between devices, with_halo(): before = lax.ppermute(last, axis, up)  79 us
    ppermute x18, starting transfers between devices, with_halo(): after = lax.ppermute(leading, axis, down)  31.4 us
    ppermute x18, waiting for transfers between devices, with_halo(): before = lax.ppermute(last, axis, up)  9.64 us
    ppermute x18, waiting for transfers between devices, with_halo(): after = lax.ppermute(leading, axis, down)  9.29 us
    select_n x6, other arithmetic, body(): face_x = jnp.where(backward, near_x[2], near_x[0])  6.76 us
    dot_general x6, matrix products, body(): jnp.dot(matrix, state, preferred_element_type=jnp.float32) + gate * lifted  5.65 us
  transfers between devices with their start and end apart: 36, of which 12 were waited for; matrix products, arithmetic and copies ran while one was open for 1% of the time, Pallas kernels for 0%

commit v1 on v0

v1 whole, which is shorter than its diff:
```python
import functools

import jax
import jax.numpy as jnp
from jax import lax
from jax.experimental import pallas as pl
from jax.experimental.pallas import tpu as pltpu
from jax.sharding import PartitionSpec as P

STEPS = 6
AXES = ("gx", "gy", "gz")
VMEM = pl.BlockSpec(memory_space=pltpu.VMEM)
SMEM = pl.BlockSpec(memory_space=pltpu.SMEM)


def swaps(axis):
    size = lax.axis_size(axis)
    sets = []
    for first in (0, 1):
        pairs = [(i, i + 1) for i in range(first, size - 1, 2)]
        sets.append(pairs + [(j, i) for i, j in pairs])
    return sets


def exchange(face, axis):
    return [lax.ppermute(face, axis, pairs) for pairs in swaps(axis) if pairs]


def per_column(values, width, rows):
    batches = values.shape[0]
    batch = lax.broadcasted_iota(jnp.int32, (rows, width), 1) // (width // batches)
    out = jnp.zeros((rows, width), jnp.int32)
    for b in range(batches):
        out = jnp.where(batch == b, values[b], out)
    return out


def choose(arrived, axis, direction, dtype):
    rows, width = arrived[0].shape
    even = 1 - lax.rem(lax.axis_index(axis), 2)
    first = per_column(direction, width, rows) == even
    other = arrived[1][...] if len(arrived) > 1 else jnp.zeros((rows, width), dtype)
    return jnp.where(first, arrived[0][...], other)


def step_kernel(step, counts, *refs):
    operator, lift, source, depth, direction = refs[:5]
    stack = refs[-1]
    faces = refs[-4:-1]
    arrived = refs[5:-4]
    order, width = operator.shape[0], source.shape[1]
    if step == 0:
        stack[:order, :] = arrived[0][...]
    else:
        rows = order // len(AXES)
        at = 0
        for n, axis in enumerate(AXES):
            stack[n * rows : (n + 1) * rows, :] = choose(arrived[at : at + counts[n]], axis, direction, stack.dtype)
            at += counts[n]
    injected = per_column(depth, width, source.shape[0]) <= step
    stack[order:, :] = jnp.where(injected, source[...], jnp.zeros_like(source[...]))
    rows = order // len(AXES)
    for n, face in enumerate(faces):
        total = jnp.dot(operator[n * rows : (n + 1) * rows, :], stack[:order, :], preferred_element_type=jnp.float32)
        total += jnp.dot(lift[n * rows : (n + 1) * rows, :], stack[order:, :], preferred_element_type=jnp.float32)
        face[...] = total.astype(face.dtype)


def last_kernel(counts, direction, *refs):
    out = refs[-1]
    rows = out.shape[0] // len(AXES)
    at = 0
    for n, axis in enumerate(AXES):
        out[n * rows : (n + 1) * rows, :] = choose(refs[at : at + counts[n]], axis, direction, out.dtype)
        at += counts[n]


def body(operator, lift, source, traces_in, depth, direction):
    shape = traces_in.shape
    operator, lift, source, state = operator[0, 0, 0], lift[0, 0, 0], source[0, 0, 0], traces_in[0, 0, 0]
    order, width = state.shape
    rows = order // len(AXES)
    face = jax.ShapeDtypeStruct((rows, width), state.dtype)
    counts = [sum(1 for pairs in swaps(axis) if pairs) for axis in AXES]
    params = pltpu.CompilerParams(vmem_limit_bytes=16 * 2**20)
    arrived = [state]
    for step in range(STEPS):
        faces = pl.pallas_call(
            functools.partial(step_kernel, step, counts),
            out_shape=[face] * 3,
            in_specs=[VMEM] * 3 + [SMEM] * 2 + [VMEM] * len(arrived),
            out_specs=[VMEM] * 3,
            scratch_shapes=[pltpu.VMEM((order + source.shape[0], width), state.dtype)],
            compiler_params=params,
            name=f"step{step}",
        )(operator, lift, source, depth, direction, *arrived)
        arrived = [piece for value, axis in zip(faces, AXES) for piece in exchange(value, axis)]
    state = pl.pallas_call(
        functools.partial(last_kernel, counts),
        out_shape=jax.ShapeDtypeStruct((order, width), state.dtype),
        in_specs=[SMEM] + [VMEM] * len(arrived),
        out_specs=VMEM,
        compiler_params=params,
        name="last",
    )(direction, *arrived)
    return state.reshape(shape)


def solution(mesh):
    placed = P("gx", "gy", "gz", None, None)
    return jax.shard_map(
        body,
        mesh=mesh,
        in_specs=(placed, placed, placed, placed, P(), P()),
        out_specs=placed,
        check_vma=False,
    )
```

time: 149 us -> 86.9 us (0.58); the launches traced: 147 us -> 86.3 us
  starting transfers between devices: 110 us -> 49.4 us
  Pallas kernels: 0 us -> 11.2 us
  other arithmetic: 8.42 us -> 0 us
  matrix products: 6.94 us -> 0 us
  local copies, waits for them, and re-layouts: 1.44 us -> 5.92 us
    ppermute x36 -> x30, starting transfers between devices: 110 us -> 49.4 us  [exchange(): return [lax.ppermute(face, axis, pairs) for pairs in swaps(axis) if pairs]]
    pallas_call x0 -> x7, Pallas kernels: none -> 11.2 us  [the longest x6 9.78 us: body(): pl.pallas_call(functools.partial(step_kernel, step, counts), out_shape=[f...]
    dot_general x7 -> x0, matrix products: 6.94 us -> none  [the longest x6 5.65 us: body(): jnp.dot(matrix, state, preferred_element_type=jnp.float32) + gate * lifted]
    select_n x6 -> x0, other arithmetic: 6.76 us -> none  [body(): face_x = jnp.where(backward, near_x[2], near_x[0])]
    unnamed x18 -> x12, local copies, waits for them, and re-layouts: 0.13 us -> 5.92 us
    ppermute x36 -> x30, waiting for transfers between devices: 18.9 us -> 19.5 us  [exchange(): return [lax.ppermute(face, axis, pairs) for pairs in swaps(axis) if pairs]]
  transfers between devices with their start and end apart: 36 -> 30, of which waited for: 12 -> 11; matrix products, arithmetic and copies ran while one was open for 1% -> 0% of each run, Pallas kernels for 0% -> 0%
where the time goes in v1:
time: 86.9 us; the launch traced here: 86.3 us
  starting transfers between devices  49.4 us (57%)
  waiting for transfers between devices  19.5 us (22%)
  Pallas kernels  11.2 us (13%)
  local copies, waits for them, and re-layouts  5.92 us (7%)
    ppermute x30, starting transfers between devices, exchange(): return [lax.ppermute(face, axis, pairs) for pairs in swaps(axis) if pairs]  49.4 us
    ppermute x30, waiting for transfers between devices, exchange(): return [lax.ppermute(face, axis, pairs) for pairs in swaps(axis) if pairs]  19.5 us
    pallas_call x6, Pallas kernels, body(): pl.pallas_call(functools.partial(step_kernel, step, counts), out_shape=[f...  9.78 us
    unnamed x12, local copies, waits for them, and re-layouts  5.92 us
  transfers between devices with their start and end apart: 30, of which 11 were waited for; matrix products, arithmetic and copies ran while one was open for 0% of the time, Pallas kernels for 0%

profile of v1, /device:TPU:1, one launch (start us, length us, event | category | flops | bytes accessed | tf_op | source)
XLA Modules:
  0.0 86.3 jit_solution(14127666647267772957)
XLA Ops:
  0.0 1.7 %copy-done = bf16[1,1,1,1152,1152]{4,3,2,1,0:T(8,128)(2,1)S(1)} copy-done((bf16[1,1,1,1152,1152]{4,3,2,1,0:T(8,128)(2,1)S(1)}, bf16[1,1,1,1152,1152]{4,3,2,1,0:T(8,128)(2,1)}, u32[]{:S(2)}) %copy-start) | copy-done | bytes 2654232
  1.8 1.0 %copy-done.1 = bf16[1,1,1,1152,128]{4,3,2,1,0:T(8,128)(2,1)S(1)} copy-done((bf16[1,1,1,1152,128]{4,3,2,1,0:T(8,128)(2,1)S(1)}, bf16[1,1,1,1152,128]{4,3,2,1,0:T(8,128)(2,1)}, u32[]{:S(2)}) %copy-start.1) | copy-done | bytes 294936
  3.6 1.1 %copy-done.3 = bf16[1,1,1,1152,256]{4,3,2,1,0:T(8,128)(2,1)S(1)} copy-done((bf16[1,1,1,1152,256]{4,3,2,1,0:T(8,128)(2,1)S(1)}, bf16[1,1,1,1152,256]{4,3,2,1,0:T(8,128)(2,1)}, u32[]{:S(2)}) %copy-start.3) | copy-done | bytes 589848
  5.9 1.7 %step0.1 = (bf16[384,256]{1,0:T(8,128)(2,1)S(1)}, bf16[384,256]{1,0:T(8,128)(2,1)S(1)}, bf16[384,256]{1,0:T(8,128)(2,1)S(1)}) custom-call(bf16[1152,1152]{1,0:T(8,128)(2,1)S(1)} %bitcast.5, bf16[1152,128]{1,0:T(8,128)(2,1)S(1)} %bitcast.11, bf16[128,256]{1,0:T(8,128)(2,1)S(1)} %bitcast.17, s32[8]{0:T(128)S(1)} %copy-done.5, s32[8]{0:T(128)S(1)} %copy-done.4, ...), custom_call_target="tpu_custom_call" | custom-call | tf_op jit(solution)/shard_map/step0/pallas_call | solution.py:88
  7.6 2.1 %collective-permute-start.4 = (bf16[384,256]{1,0:T(8,128)(2,1)S(1)}, bf16[384,256]{1,0:T(8,128)(2,1)S(1)}, u32[]{:S(2)}, u32[]{:S(2)}) collective-permute-start(bf16[384,256]{1,0:T(8,128)(2,1)S(1)} %get-tuple-element.25), channel_id=1, source_target_pairs={{0,1},{1,0},{2,3},{3,2},{4,5},{5,4},{6,7},{7,6},{8,9},{9,8},{10,11... | collective-permute-start | bytes 589832 | tf_op jit(solution)/shard_map/ppermute | solution.py:26
  10.4 3.9 %collective-permute-start = (bf16[384,256]{1,0:T(8,128)(2,1)S(1)}, bf16[384,256]{1,0:T(8,128)(2,1)S(1)}, u32[]{:S(2)}, u32[]{:S(2)}) collective-permute-start(bf16[384,256]{1,0:T(8,128)(2,1)S(1)} %get-tuple-element.23), channel_id=1, source_target_pairs={{0,8},{16,24},{8,0},{24,16},{1,9},{17,25},{9,1},{25,17},{2,10},{18... | collective-permute-start | bytes 589832 | tf_op jit(solution)/shard_map/ppermute | solution.py:26
  14.2 4.5 %collective-permute-start.3 = (bf16[384,256]{1,0:T(8,128)(2,1)S(1)}, bf16[384,256]{1,0:T(8,128)(2,1)S(1)}, u32[]{:S(2)}, u32[]{:S(2)}) collective-permute-start(bf16[384,256]{1,0:T(8,128)(2,1)S(1)} %get-tuple-element.24), channel_id=1, source_target_pairs={{2,4},{4,2},{3,5},{5,3},{10,12},{12,10},{11,13},{13,11},{18,20},{2... | collective-permute-start | bytes 589832 | tf_op jit(solution)/shard_map/ppermute | solution.py:26
  18.9 3.2 %collective-permute-done.3.refs_8_ = bf16[384,256]{1,0:T(8,128)(2,1)S(1)} collective-permute-done((bf16[384,256]{1,0:T(8,128)(2,1)S(1)}, bf16[384,256]{1,0:T(8,128)(2,1)S(1)}, u32[]{:S(2)}, u32[]{:S(2)}) %collective-permute-start.3) | collective-permute-done | bytes 196640 | tf_op jit(solution)/shard_map/ppermute | solution.py:26
  22.1 1.6 %step1.1 = (bf16[384,256]{1,0:T(8,128)(2,1)S(1)}, bf16[384,256]{1,0:T(8,128)(2,1)S(1)}, bf16[384,256]{1,0:T(8,128)(2,1)S(1)}) custom-call(bf16[1152,1152]{1,0:T(8,128)(2,1)S(1)} %bitcast.6, bf16[1152,128]{1,0:T(8,128)(2,1)S(1)} %bitcast.12, bf16[128,256]{1,0:T(8,128)(2,1)S(1)} %bitcast.18, s32[8]{0:T(128)S(1)} %copy-done.5, s32[8]{0:T(128)S(1)} %copy-done.4, ...), custom_call_target="tpu_custom_call" | custom-call | tf_op jit(solution)/shard_map/step1/pallas_call | solution.py:88
  24.8 1.2 %collective-permute-start.5 = (bf16[384,256]{1,0:T(8,128)(2,1)S(1)}, bf16[384,256]{1,0:T(8,128)(2,1)S(1)}, u32[]{:S(2)}, u32[]{:S(2)}) collective-permute-start(bf16[384,256]{1,0:T(8,128)(2,1)S(1)} %get-tuple-element.26), channel_id=1, source_target_pairs={{0,8},{16,24},{8,0},{24,16},{1,9},{17,25},{9,1},{25,17},{2,10},{18... | collective-permute-start | bytes 589832 | tf_op jit(solution)/shard_map/ppermute | solution.py:26
  26.0 4.5 %collective-permute-start.8 = (bf16[384,256]{1,0:T(8,128)(2,1)S(1)}, bf16[384,256]{1,0:T(8,128)(2,1)S(1)}, u32[]{:S(2)}, u32[]{:S(2)}) collective-permute-start(bf16[384,256]{1,0:T(8,128)(2,1)S(1)} %get-tuple-element.27), channel_id=1, source_target_pairs={{2,4},{4,2},{3,5},{5,3},{10,12},{12,10},{11,13},{13,11},{18,20},{2... | collective-permute-start | bytes 589832 | tf_op jit(solution)/shard_map/ppermute | solution.py:26
  30.5 1.1 %collective-permute-done.5.refs_5_ = bf16[384,256]{1,0:T(8,128)(2,1)S(1)} collective-permute-done((bf16[384,256]{1,0:T(8,128)(2,1)S(1)}, bf16[384,256]{1,0:T(8,128)(2,1)S(1)}, u32[]{:S(2)}, u32[]{:S(2)}) %collective-permute-start.5) | collective-permute-done | bytes 196640 | tf_op jit(solution)/shard_map/ppermute | solution.py:26
  31.6 2.2 %collective-permute-done.8.refs_8_ = bf16[384,256]{1,0:T(8,128)(2,1)S(1)} collective-permute-done((bf16[384,256]{1,0:T(8,128)(2,1)S(1)}, bf16[384,256]{1,0:T(8,128)(2,1)S(1)}, u32[]{:S(2)}, u32[]{:S(2)}) %collective-permute-start.8) | collective-permute-done | bytes 196640 | tf_op jit(solution)/shard_map/ppermute | solution.py:26
  33.8 1.6 %step2.1 = (bf16[384,256]{1,0:T(8,128)(2,1)S(1)}, bf16[384,256]{1,0:T(8,128)(2,1)S(1)}, bf16[384,256]{1,0:T(8,128)(2,1)S(1)}) custom-call(bf16[1152,1152]{1,0:T(8,128)(2,1)S(1)} %bitcast.7, bf16[1152,128]{1,0:T(8,128)(2,1)S(1)} %bitcast.13, bf16[128,256]{1,0:T(8,128)(2,1)S(1)} %bitcast.19, s32[8]{0:T(128)S(1)} %copy-done.5, s32[8]{0:T(128)S(1)} %copy-done.4, ...), custom_call_target="tpu_custom_call" | custom-call | tf_op jit(solution)/shard_map/step2/pallas_call | solution.py:88
  35.4 1.3 %collective-permute-start.14 = (bf16[384,256]{1,0:T(8,128)(2,1)S(1)}, bf16[384,256]{1,0:T(8,128)(2,1)S(1)}, u32[]{:S(2)}, u32[]{:S(2)}) collective-permute-start(bf16[384,256]{1,0:T(8,128)(2,1)S(1)} %get-tuple-element.31), channel_id=1, source_target_pairs={{0,1},{1,0},{2,3},{3,2},{4,5},{5,4},{6,7},{7,6},{8,9},{9,8},{10,11... | collective-permute-start | bytes 589832 | tf_op jit(solution)/shard_map/ppermute | solution.py:26
  37.4 2.3 %collective-permute-start.10 = (bf16[384,256]{1,0:T(8,128)(2,1)S(1)}, bf16[384,256]{1,0:T(8,128)(2,1)S(1)}, u32[]{:S(2)}, u32[]{:S(2)}) collective-permute-start(bf16[384,256]{1,0:T(8,128)(2,1)S(1)} %get-tuple-element.29), channel_id=1, source_target_pairs={{0,8},{16,24},{8,0},{24,16},{1,9},{17,25},{9,1},{25,17},{2,10},{18... | collective-permute-start | bytes 589832 | tf_op jit(solution)/shard_map/ppermute | solution.py:26
  39.7 4.5 %collective-permute-start.13 = (bf16[384,256]{1,0:T(8,128)(2,1)S(1)}, bf16[384,256]{1,0:T(8,128)(2,1)S(1)}, u32[]{:S(2)}, u32[]{:S(2)}) collective-permute-start(bf16[384,256]{1,0:T(8,128)(2,1)S(1)} %get-tuple-element.30), channel_id=1, source_target_pairs={{2,4},{4,2},{3,5},{5,3},{10,12},{12,10},{11,13},{13,11},{18,20},{2... | collective-permute-start | bytes 589832 | tf_op jit(solution)/shard_map/ppermute | solution.py:26
  44.7 2.9 %collective-permute-done.13.refs_8_ = bf16[384,256]{1,0:T(8,128)(2,1)S(1)} collective-permute-done((bf16[384,256]{1,0:T(8,128)(2,1)S(1)}, bf16[384,256]{1,0:T(8,128)(2,1)S(1)}, u32[]{:S(2)}, u32[]{:S(2)}) %collective-permute-start.13) | collective-permute-done | bytes 196640 | tf_op jit(solution)/shard_map/ppermute | solution.py:26
  47.5 1.6 %step3.1 = (bf16[384,256]{1,0:T(8,128)(2,1)S(1)}, bf16[384,256]{1,0:T(8,128)(2,1)S(1)}, bf16[384,256]{1,0:T(8,128)(2,1)S(1)}) custom-call(bf16[1152,1152]{1,0:T(8,128)(2,1)S(1)} %bitcast.8, bf16[1152,128]{1,0:T(8,128)(2,1)S(1)} %bitcast.14, bf16[128,256]{1,0:T(8,128)(2,1)S(1)} %bitcast.20, s32[8]{0:T(128)S(1)} %copy-done.5, s32[8]{0:T(128)S(1)} %copy-done.4, ...), custom_call_target="tpu_custom_call" | custom-call | tf_op jit(solution)/shard_map/step3/pallas_call | solution.py:88
  50.2 1.5 %collective-permute-start.15 = (bf16[384,256]{1,0:T(8,128)(2,1)S(1)}, bf16[384,256]{1,0:T(8,128)(2,1)S(1)}, u32[]{:S(2)}, u32[]{:S(2)}) collective-permute-start(bf16[384,256]{1,0:T(8,128)(2,1)S(1)} %get-tuple-element.32), channel_id=1, source_target_pairs={{0,8},{16,24},{8,0},{24,16},{1,9},{17,25},{9,1},{25,17},{2,10},{18... | collective-permute-start | bytes 589832 | tf_op jit(solution)/shard_map/ppermute | solution.py:26
  51.7 4.5 %collective-permute-start.18 = (bf16[384,256]{1,0:T(8,128)(2,1)S(1)}, bf16[384,256]{1,0:T(8,128)(2,1)S(1)}, u32[]{:S(2)}, u32[]{:S(2)}) collective-permute-start(bf16[384,256]{1,0:T(8,128)(2,1)S(1)} %get-tuple-element.33), channel_id=1, source_target_pairs={{2,4},{4,2},{3,5},{5,3},{10,12},{12,10},{11,13},{13,11},{18,20},{2... | collective-permute-start | bytes 589832 | tf_op jit(solution)/shard_map/ppermute | solution.py:26
  56.7 2.8 %collective-permute-done.18.refs_8_ = bf16[384,256]{1,0:T(8,128)(2,1)S(1)} collective-permute-done((bf16[384,256]{1,0:T(8,128)(2,1)S(1)}, bf16[384,256]{1,0:T(8,128)(2,1)S(1)}, u32[]{:S(2)}, u32[]{:S(2)}) %collective-permute-start.18) | collective-permute-done | bytes 196640 | tf_op jit(solution)/shard_map/ppermute | solution.py:26
  59.5 1.6 %step4.1 = (bf16[384,256]{1,0:T(8,128)(2,1)S(1)}, bf16[384,256]{1,0:T(8,128)(2,1)S(1)}, bf16[384,256]{1,0:T(8,128)(2,1)S(1)}) custom-call(bf16[1152,1152]{1,0:T(8,128)(2,1)S(1)} %bitcast.9, bf16[1152,128]{1,0:T(8,128)(2,1)S(1)} %bitcast.15, bf16[128,256]{1,0:T(8,128)(2,1)S(1)} %bitcast.21, s32[8]{0:T(128)S(1)} %copy-done.5, s32[8]{0:T(128)S(1)} %copy-done.4, ...), custom_call_target="tpu_custom_call" | custom-call | tf_op jit(solution)/shard_map/step4/pallas_call | solution.py:88
  61.1 1.3 %collective-permute-start.24 = (bf16[384,256]{1,0:T(8,128)(2,1)S(1)}, bf16[384,256]{1,0:T(8,128)(2,1)S(1)}, u32[]{:S(2)}, u32[]{:S(2)}) collective-permute-start(bf16[384,256]{1,0:T(8,128)(2,1)S(1)} %get-tuple-element.37), channel_id=1, source_target_pairs={{0,1},{1,0},{2,3},{3,2},{4,5},{5,4},{6,7},{7,6},{8,9},{9,8},{10,11... | collective-permute-start | bytes 589832 | tf_op jit(solution)/shard_map/ppermute | solution.py:26
  63.1 2.1 %collective-permute-start.20 = (bf16[384,256]{1,0:T(8,128)(2,1)S(1)}, bf16[384,256]{1,0:T(8,128)(2,1)S(1)}, u32[]{:S(2)}, u32[]{:S(2)}) collective-permute-start(bf16[384,256]{1,0:T(8,128)(2,1)S(1)} %get-tuple-element.35), channel_id=1, source_target_pairs={{0,8},{16,24},{8,0},{24,16},{1,9},{17,25},{9,1},{25,17},{2,10},{18... | collective-permute-start | bytes 589832 | tf_op jit(solution)/shard_map/ppermute | solution.py:26
  65.1 4.5 %collective-permute-start.23 = (bf16[384,256]{1,0:T(8,128)(2,1)S(1)}, bf16[384,256]{1,0:T(8,128)(2,1)S(1)}, u32[]{:S(2)}, u32[]{:S(2)}) collective-permute-start(bf16[384,256]{1,0:T(8,128)(2,1)S(1)} %get-tuple-element.36), channel_id=1, source_target_pairs={{2,4},{4,2},{3,5},{5,3},{10,12},{12,10},{11,13},{13,11},{18,20},{2... | collective-permute-start | bytes 589832 | tf_op jit(solution)/shard_map/ppermute | solution.py:26
  70.1 2.9 %collective-permute-done.23.refs_8_ = bf16[384,256]{1,0:T(8,128)(2,1)S(1)} collective-permute-done((bf16[384,256]{1,0:T(8,128)(2,1)S(1)}, bf16[384,256]{1,0:T(8,128)(2,1)S(1)}, u32[]{:S(2)}, u32[]{:S(2)}) %collective-permute-start.23) | collective-permute-done | bytes 196640 | tf_op jit(solution)/shard_map/ppermute | solution.py:26
  72.9 1.6 %step5.1 = (bf16[384,256]{1,0:T(8,128)(2,1)S(1)}, bf16[384,256]{1,0:T(8,128)(2,1)S(1)}, bf16[384,256]{1,0:T(8,128)(2,1)S(1)}) custom-call(bf16[1152,1152]{1,0:T(8,128)(2,1)S(1)} %bitcast.10, bf16[1152,128]{1,0:T(8,128)(2,1)S(1)} %bitcast.16, bf16[128,256]{1,0:T(8,128)(2,1)S(1)} %bitcast.22, s32[8]{0:T(128)S(1)} %copy-done.5, s32[8]{0:T(128)S(1)} %copy-done.4, ...), custom_call_target="tpu_custom_call" | custom-call | tf_op jit(solution)/shard_map/step5/pallas_call | solution.py:88
  75.5 1.5 %collective-permute-start.25 = (bf16[384,256]{1,0:T(8,128)(2,1)S(1)}, bf16[384,256]{1,0:T(8,128)(2,1)S(1)}, u32[]{:S(2)}, u32[]{:S(2)}) collective-permute-start(bf16[384,256]{1,0:T(8,128)(2,1)S(1)} %get-tuple-element.38), channel_id=1, source_target_pairs={{0,8},{16,24},{8,0},{24,16},{1,9},{17,25},{9,1},{25,17},{2,10},{18... | collective-permute-start | bytes 589832 | tf_op jit(solution)/shard_map/ppermute | solution.py:26
  77.1 4.5 %collective-permute-start.28 = (bf16[384,256]{1,0:T(8,128)(2,1)S(1)}, bf16[384,256]{1,0:T(8,128)(2,1)S(1)}, u32[]{:S(2)}, u32[]{:S(2)}) collective-permute-start(bf16[384,256]{1,0:T(8,128)(2,1)S(1)} %get-tuple-element.39), channel_id=1, source_target_pairs={{2,4},{4,2},{3,5},{5,3},{10,12},{12,10},{11,13},{13,11},{18,20},{2... | collective-permute-start | bytes 589832 | tf_op jit(solution)/shard_map/ppermute | solution.py:26
  82.1 2.8 %collective-permute-done.28.refs_3_ = bf16[384,256]{1,0:T(8,128)(2,1)S(1)} collective-permute-done((bf16[384,256]{1,0:T(8,128)(2,1)S(1)}, bf16[384,256]{1,0:T(8,128)(2,1)S(1)}, u32[]{:S(2)}, u32[]{:S(2)}) %collective-permute-start.28) | collective-permute-done | bytes 196640 | tf_op jit(solution)/shard_map/ppermute | solution.py:26
  84.9 1.4 %last.1 = bf16[1152,256]{1,0:T(8,128)(2,1)} custom-call(s32[8]{0:T(128)S(1)} %copy-done.4, bf16[384,256]{1,0:T(8,128)(2,1)S(1)} %collective-permute-done.25.refs_0_, bf16[384,256]{1,0:T(8,128)(2,1)S(1)} %collective-permute-done.26.refs_1_, bf16[384,256]{1,0:T(8,128)(2,1)S(1)} %collective-permute-done.27.refs_2_, ...), custom_call_target="tpu_custom_call" | custom-call | tf_op jit(solution)/shard_map/last/pallas_call | solution.py:98
  (47 shorter events, 9.2 us)
Async XLA Ops:
  0.0 1.7 %copy-start = (bf16[1,1,1,1152,1152]{4,3,2,1,0:T(8,128)(2,1)S(1)}, bf16[1,1,1,1152,1152]{4,3,2,1,0:T(8,128)(2,1)}, u32[]{:S(2)}) copy-start(bf16[1,1,1,1152,1152]{4,3,2,1,0:T(8,128)(2,1)} %param.6) | copy-start | bytes 7962628
  3.6 1.1 %copy-start.3 = (bf16[1,1,1,1152,256]{4,3,2,1,0:T(8,128)(2,1)S(1)}, bf16[1,1,1,1152,256]{4,3,2,1,0:T(8,128)(2,1)}, u32[]{:S(2)}) copy-start(bf16[1,1,1,1152,256]{4,3,2,1,0:T(8,128)(2,1)} %param.9) | copy-start | bytes 1769476
  7.6 11.3 %collective-permute-start.4 = (bf16[384,256]{1,0:T(8,128)(2,1)S(1)}, bf16[384,256]{1,0:T(8,128)(2,1)S(1)}, u32[]{:S(2)}, u32[]{:S(2)}) collective-permute-start(bf16[384,256]{1,0:T(8,128)(2,1)S(1)} %get-tuple-element.25), channel_id=1, source_target_pairs={{0,1},{1,0},{2,3},{3,2},{4,5},{5,4},{6,7},{7,6},{8,9},{9,8},{10,11... | collective-permute-start | bytes 589832 | tf_op jit(solution)/shard_map/ppermute | solution.py:26
  9.7 9.2 %collective-permute-start.1 = (bf16[384,256]{1,0:T(8,128)(2,1)S(1)}, bf16[384,256]{1,0:T(8,128)(2,1)S(1)}, u32[]{:S(2)}, u32[]{:S(2)}) collective-permute-start(bf16[384,256]{1,0:T(8,128)(2,1)S(1)} %get-tuple-element.23), channel_id=1, source_target_pairs={{8,16},{16,8},{9,17},{17,9},{10,18},{18,10},{11,19},{19,11},{12,20... | collective-permute-start | bytes 589832 | tf_op jit(solution)/shard_map/ppermute | solution.py:26
  10.4 8.5 %collective-permute-start = (bf16[384,256]{1,0:T(8,128)(2,1)S(1)}, bf16[384,256]{1,0:T(8,128)(2,1)S(1)}, u32[]{:S(2)}, u32[]{:S(2)}) collective-permute-start(bf16[384,256]{1,0:T(8,128)(2,1)S(1)} %get-tuple-element.23), channel_id=1, source_target_pairs={{0,8},{16,24},{8,0},{24,16},{1,9},{17,25},{9,1},{25,17},{2,10},{18... | collective-permute-start | bytes 589832 | tf_op jit(solution)/shard_map/ppermute | solution.py:26
  14.2 7.9 %collective-permute-start.3 = (bf16[384,256]{1,0:T(8,128)(2,1)S(1)}, bf16[384,256]{1,0:T(8,128)(2,1)S(1)}, u32[]{:S(2)}, u32[]{:S(2)}) collective-permute-start(bf16[384,256]{1,0:T(8,128)(2,1)S(1)} %get-tuple-element.24), channel_id=1, source_target_pairs={{2,4},{4,2},{3,5},{5,3},{10,12},{12,10},{11,13},{13,11},{18,20},{2... | collective-permute-start | bytes 589832 | tf_op jit(solution)/shard_map/ppermute | solution.py:26
  18.8 3.3 %collective-permute-start.2 = (bf16[384,256]{1,0:T(8,128)(2,1)S(1)}, bf16[384,256]{1,0:T(8,128)(2,1)S(1)}, u32[]{:S(2)}, u32[]{:S(2)}) collective-permute-start(bf16[384,256]{1,0:T(8,128)(2,1)S(1)} %get-tuple-element.24), channel_id=1, source_target_pairs={{0,2},{4,6},{2,0},{6,4},{1,3},{5,7},{3,1},{7,5},{8,10},{12,14},{10... | collective-permute-start | bytes 589832 | tf_op jit(solution)/shard_map/ppermute | solution.py:26
  23.8 6.8 %collective-permute-start.9 = (bf16[384,256]{1,0:T(8,128)(2,1)S(1)}, bf16[384,256]{1,0:T(8,128)(2,1)S(1)}, u32[]{:S(2)}, u32[]{:S(2)}) collective-permute-start(bf16[384,256]{1,0:T(8,128)(2,1)S(1)} %get-tuple-element.28), channel_id=1, source_target_pairs={{0,1},{1,0},{2,3},{3,2},{4,5},{5,4},{6,7},{7,6},{8,9},{9,8},{10,11... | collective-permute-start | bytes 589832 | tf_op jit(solution)/shard_map/ppermute | solution.py:26
  24.1 6.5 %collective-permute-start.6 = (bf16[384,256]{1,0:T(8,128)(2,1)S(1)}, bf16[384,256]{1,0:T(8,128)(2,1)S(1)}, u32[]{:S(2)}, u32[]{:S(2)}) collective-permute-start(bf16[384,256]{1,0:T(8,128)(2,1)S(1)} %get-tuple-element.26), channel_id=1, source_target_pairs={{8,16},{16,8},{9,17},{17,9},{10,18},{18,10},{11,19},{19,11},{12,20... | collective-permute-start | bytes 589832 | tf_op jit(solution)/shard_map/ppermute | solution.py:26
  24.8 6.9 %collective-permute-start.5 = (bf16[384,256]{1,0:T(8,128)(2,1)S(1)}, bf16[384,256]{1,0:T(8,128)(2,1)S(1)}, u32[]{:S(2)}, u32[]{:S(2)}) collective-permute-start(bf16[384,256]{1,0:T(8,128)(2,1)S(1)} %get-tuple-element.26), channel_id=1, source_target_pairs={{0,8},{16,24},{8,0},{24,16},{1,9},{17,25},{9,1},{25,17},{2,10},{18... | collective-permute-start | bytes 589832 | tf_op jit(solution)/shard_map/ppermute | solution.py:26
  26.0 7.8 %collective-permute-start.8 = (bf16[384,256]{1,0:T(8,128)(2,1)S(1)}, bf16[384,256]{1,0:T(8,128)(2,1)S(1)}, u32[]{:S(2)}, u32[]{:S(2)}) collective-permute-start(bf16[384,256]{1,0:T(8,128)(2,1)S(1)} %get-tuple-element.27), channel_id=1, source_target_pairs={{2,4},{4,2},{3,5},{5,3},{10,12},{12,10},{11,13},{13,11},{18,20},{2... | collective-permute-start | bytes 589832 | tf_op jit(solution)/shard_map/ppermute | solution.py:26
  30.4 3.3 %collective-permute-start.7 = (bf16[384,256]{1,0:T(8,128)(2,1)S(1)}, bf16[384,256]{1,0:T(8,128)(2,1)S(1)}, u32[]{:S(2)}, u32[]{:S(2)}) collective-permute-start(bf16[384,256]{1,0:T(8,128)(2,1)S(1)} %get-tuple-element.27), channel_id=1, source_target_pairs={{0,2},{4,6},{2,0},{6,4},{1,3},{5,7},{3,1},{7,5},{8,10},{12,14},{10... | collective-permute-start | bytes 589832 | tf_op jit(solution)/shard_map/ppermute | solution.py:26
  35.4 8.8 %collective-permute-start.14 = (bf16[384,256]{1,0:T(8,128)(2,1)S(1)}, bf16[384,256]{1,0:T(8,128)(2,1)S(1)}, u32[]{:S(2)}, u32[]{:S(2)}) collective-permute-start(bf16[384,256]{1,0:T(8,128)(2,1)S(1)} %get-tuple-element.31), channel_id=1, source_target_pairs={{0,1},{1,0},{2,3},{3,2},{4,5},{5,4},{6,7},{7,6},{8,9},{9,8},{10,11... | collective-permute-start | bytes 589832 | tf_op jit(solution)/shard_map/ppermute | solution.py:26
  36.7 7.6 %collective-permute-start.11 = (bf16[384,256]{1,0:T(8,128)(2,1)S(1)}, bf16[384,256]{1,0:T(8,128)(2,1)S(1)}, u32[]{:S(2)}, u32[]{:S(2)}) collective-permute-start(bf16[384,256]{1,0:T(8,128)(2,1)S(1)} %get-tuple-element.29), channel_id=1, source_target_pairs={{8,16},{16,8},{9,17},{17,9},{10,18},{18,10},{11,19},{19,11},{12,20... | collective-permute-start | bytes 589832 | tf_op jit(solution)/shard_map/ppermute | solution.py:26
  37.4 7.3 %collective-permute-start.10 = (bf16[384,256]{1,0:T(8,128)(2,1)S(1)}, bf16[384,256]{1,0:T(8,128)(2,1)S(1)}, u32[]{:S(2)}, u32[]{:S(2)}) collective-permute-start(bf16[384,256]{1,0:T(8,128)(2,1)S(1)} %get-tuple-element.29), channel_id=1, source_target_pairs={{0,8},{16,24},{8,0},{24,16},{1,9},{17,25},{9,1},{25,17},{2,10},{18... | collective-permute-start | bytes 589832 | tf_op jit(solution)/shard_map/ppermute | solution.py:26
  39.7 7.8 %collective-permute-start.13 = (bf16[384,256]{1,0:T(8,128)(2,1)S(1)}, bf16[384,256]{1,0:T(8,128)(2,1)S(1)}, u32[]{:S(2)}, u32[]{:S(2)}) collective-permute-start(bf16[384,256]{1,0:T(8,128)(2,1)S(1)} %get-tuple-element.30), channel_id=1, source_target_pairs={{2,4},{4,2},{3,5},{5,3},{10,12},{12,10},{11,13},{13,11},{18,20},{2... | collective-permute-start | bytes 589832 | tf_op jit(solution)/shard_map/ppermute | solution.py:26
  44.2 3.3 %collective-permute-start.12 = (bf16[384,256]{1,0:T(8,128)(2,1)S(1)}, bf16[384,256]{1,0:T(8,128)(2,1)S(1)}, u32[]{:S(2)}, u32[]{:S(2)}) collective-permute-start(bf16[384,256]{1,0:T(8,128)(2,1)S(1)} %get-tuple-element.30), channel_id=1, source_target_pairs={{0,2},{4,6},{2,0},{6,4},{1,3},{5,7},{3,1},{7,5},{8,10},{12,14},{10... | collective-permute-start | bytes 589832 | tf_op jit(solution)/shard_map/ppermute | solution.py:26
  49.2 7.1 %collective-permute-start.19 = (bf16[384,256]{1,0:T(8,128)(2,1)S(1)}, bf16[384,256]{1,0:T(8,128)(2,1)S(1)}, u32[]{:S(2)}, u32[]{:S(2)}) collective-permute-start(bf16[384,256]{1,0:T(8,128)(2,1)S(1)} %get-tuple-element.34), channel_id=1, source_target_pairs={{0,1},{1,0},{2,3},{3,2},{4,5},{5,4},{6,7},{7,6},{8,9},{9,8},{10,11... | collective-permute-start | bytes 589832 | tf_op jit(solution)/shard_map/ppermute | solution.py:26
  49.5 6.7 %collective-permute-start.16 = (bf16[384,256]{1,0:T(8,128)(2,1)S(1)}, bf16[384,256]{1,0:T(8,128)(2,1)S(1)}, u32[]{:S(2)}, u32[]{:S(2)}) collective-permute-start(bf16[384,256]{1,0:T(8,128)(2,1)S(1)} %get-tuple-element.32), channel_id=1, source_target_pairs={{8,16},{16,8},{9,17},{17,9},{10,18},{18,10},{11,19},{19,11},{12,20... | collective-permute-start | bytes 589832 | tf_op jit(solution)/shard_map/ppermute | solution.py:26
  50.2 6.5 %collective-permute-start.15 = (bf16[384,256]{1,0:T(8,128)(2,1)S(1)}, bf16[384,256]{1,0:T(8,128)(2,1)S(1)}, u32[]{:S(2)}, u32[]{:S(2)}) collective-permute-start(bf16[384,256]{1,0:T(8,128)(2,1)S(1)} %get-tuple-element.32), channel_id=1, source_target_pairs={{0,8},{16,24},{8,0},{24,16},{1,9},{17,25},{9,1},{25,17},{2,10},{18... | collective-permute-start | bytes 589832 | tf_op jit(solution)/shard_map/ppermute | solution.py:26
  51.7 7.8 %collective-permute-start.18 = (bf16[384,256]{1,0:T(8,128)(2,1)S(1)}, bf16[384,256]{1,0:T(8,128)(2,1)S(1)}, u32[]{:S(2)}, u32[]{:S(2)}) collective-permute-start(bf16[384,256]{1,0:T(8,128)(2,1)S(1)} %get-tuple-element.33), channel_id=1, source_target_pairs={{2,4},{4,2},{3,5},{5,3},{10,12},{12,10},{11,13},{13,11},{18,20},{2... | collective-permute-start | bytes 589832 | tf_op jit(solution)/shard_map/ppermute | solution.py:26
  56.1 3.3 %collective-permute-start.17 = (bf16[384,256]{1,0:T(8,128)(2,1)S(1)}, bf16[384,256]{1,0:T(8,128)(2,1)S(1)}, u32[]{:S(2)}, u32[]{:S(2)}) collective-permute-start(bf16[384,256]{1,0:T(8,128)(2,1)S(1)} %get-tuple-element.33), channel_id=1, source_target_pairs={{0,2},{4,6},{2,0},{6,4},{1,3},{5,7},{3,1},{7,5},{8,10},{12,14},{10... | collective-permute-start | bytes 589832 | tf_op jit(solution)/shard_map/ppermute | solution.py:26
  61.1 8.6 %collective-permute-start.24 = (bf16[384,256]{1,0:T(8,128)(2,1)S(1)}, bf16[384,256]{1,0:T(8,128)(2,1)S(1)}, u32[]{:S(2)}, u32[]{:S(2)}) collective-permute-start(bf16[384,256]{1,0:T(8,128)(2,1)S(1)} %get-tuple-element.37), channel_id=1, source_target_pairs={{0,1},{1,0},{2,3},{3,2},{4,5},{5,4},{6,7},{7,6},{8,9},{9,8},{10,11... | collective-permute-start | bytes 589832 | tf_op jit(solution)/shard_map/ppermute | solution.py:26
  62.4 7.3 %collective-permute-start.21 = (bf16[384,256]{1,0:T(8,128)(2,1)S(1)}, bf16[384,256]{1,0:T(8,128)(2,1)S(1)}, u32[]{:S(2)}, u32[]{:S(2)}) collective-permute-start(bf16[384,256]{1,0:T(8,128)(2,1)S(1)} %get-tuple-element.35), channel_id=1, source_target_pairs={{8,16},{16,8},{9,17},{17,9},{10,18},{18,10},{11,19},{19,11},{12,20... | collective-permute-start | bytes 589832 | tf_op jit(solution)/shard_map/ppermute | solution.py:26
  63.1 7.0 %collective-permute-start.20 = (bf16[384,256]{1,0:T(8,128)(2,1)S(1)}, bf16[384,256]{1,0:T(8,128)(2,1)S(1)}, u32[]{:S(2)}, u32[]{:S(2)}) collective-permute-start(bf16[384,256]{1,0:T(8,128)(2,1)S(1)} %get-tuple-element.35), channel_id=1, source_target_pairs={{0,8},{16,24},{8,0},{24,16},{1,9},{17,25},{9,1},{25,17},{2,10},{18... | collective-permute-start | bytes 589832 | tf_op jit(solution)/shard_map/ppermute | solution.py:26
  65.1 7.8 %collective-permute-start.23 = (bf16[384,256]{1,0:T(8,128)(2,1)S(1)}, bf16[384,256]{1,0:T(8,128)(2,1)S(1)}, u32[]{:S(2)}, u32[]{:S(2)}) collective-permute-start(bf16[384,256]{1,0:T(8,128)(2,1)S(1)} %get-tuple-element.36), channel_id=1, source_target_pairs={{2,4},{4,2},{3,5},{5,3},{10,12},{12,10},{11,13},{13,11},{18,20},{2... | collective-permute-start | bytes 589832 | tf_op jit(solution)/shard_map/ppermute | solution.py:26
  69.6 3.3 %collective-permute-start.22 = (bf16[384,256]{1,0:T(8,128)(2,1)S(1)}, bf16[384,256]{1,0:T(8,128)(2,1)S(1)}, u32[]{:S(2)}, u32[]{:S(2)}) collective-permute-start(bf16[384,256]{1,0:T(8,128)(2,1)S(1)} %get-tuple-element.36), channel_id=1, source_target_pairs={{0,2},{4,6},{2,0},{6,4},{1,3},{5,7},{3,1},{7,5},{8,10},{12,14},{10... | collective-permute-start | bytes 589832 | tf_op jit(solution)/shard_map/ppermute | solution.py:26
  74.6 7.1 %collective-permute-start.29 = (bf16[384,256]{1,0:T(8,128)(2,1)S(1)}, bf16[384,256]{1,0:T(8,128)(2,1)S(1)}, u32[]{:S(2)}, u32[]{:S(2)}) collective-permute-start(bf16[384,256]{1,0:T(8,128)(2,1)S(1)} %get-tuple-element.40), channel_id=1, source_target_pairs={{0,1},{1,0},{2,3},{3,2},{4,5},{5,4},{6,7},{7,6},{8,9},{9,8},{10,11... | collective-permute-start | bytes 589832 | tf_op jit(solution)/shard_map/ppermute | solution.py:26
  74.9 6.7 %collective-permute-start.26 = (bf16[384,256]{1,0:T(8,128)(2,1)S(1)}, bf16[384,256]{1,0:T(8,128)(2,1)S(1)}, u32[]{:S(2)}, u32[]{:S(2)}) collective-permute-start(bf16[384,256]{1,0:T(8,128)(2,1)S(1)} %get-tuple-element.38), channel_id=1, source_target_pairs={{8,16},{16,8},{9,17},{17,9},{10,18},{18,10},{11,19},{19,11},{12,20... | collective-permute-start | bytes 589832 | tf_op jit(solution)/shard_map/ppermute | solution.py:26
  75.5 6.5 %collective-permute-start.25 = (bf16[384,256]{1,0:T(8,128)(2,1)S(1)}, bf16[384,256]{1,0:T(8,128)(2,1)S(1)}, u32[]{:S(2)}, u32[]{:S(2)}) collective-permute-start(bf16[384,256]{1,0:T(8,128)(2,1)S(1)} %get-tuple-element.38), channel_id=1, source_target_pairs={{0,8},{16,24},{8,0},{24,16},{1,9},{17,25},{9,1},{25,17},{2,10},{18... | collective-permute-start | bytes 589832 | tf_op jit(solution)/shard_map/ppermute | solution.py:26
  77.1 7.8 %collective-permute-start.28 = (bf16[384,256]{1,0:T(8,128)(2,1)S(1)}, bf16[384,256]{1,0:T(8,128)(2,1)S(1)}, u32[]{:S(2)}, u32[]{:S(2)}) collective-permute-start(bf16[384,256]{1,0:T(8,128)(2,1)S(1)} %get-tuple-element.39), channel_id=1, source_target_pairs={{2,4},{4,2},{3,5},{5,3},{10,12},{12,10},{11,13},{13,11},{18,20},{2... | collective-permute-start | bytes 589832 | tf_op jit(solution)/shard_map/ppermute | solution.py:26
  81.5 3.3 %collective-permute-start.27 = (bf16[384,256]{1,0:T(8,128)(2,1)S(1)}, bf16[384,256]{1,0:T(8,128)(2,1)S(1)}, u32[]{:S(2)}, u32[]{:S(2)}) collective-permute-start(bf16[384,256]{1,0:T(8,128)(2,1)S(1)} %get-tuple-element.39), channel_id=1, source_target_pairs={{0,2},{4,6},{2,0},{6,4},{1,3},{5,7},{3,1},{7,5},{8,10},{12,14},{10... | collective-permute-start | bytes 589832 | tf_op jit(solution)/shard_map/ppermute | solution.py:26
  (4 other events, 3.1 us)

commit v2 on v1

v2 whole, which is shorter than its diff:
```python
import functools

import jax
import jax.numpy as jnp
from jax import lax
from jax.experimental import pallas as pl
from jax.experimental.pallas import tpu as pltpu
from jax.sharding import PartitionSpec as P

STEPS = 6
AXES = ("gx", "gy", "gz")
FILL = {"gx": "gy", "gy": "gz", "gz": "gy"}
TILE = 16
VMEM = pl.BlockSpec(memory_space=pltpu.VMEM)
HBM = pl.BlockSpec(memory_space=pltpu.HBM)


def device(position):
    at = 0
    for axis in AXES:
        at = at * lax.axis_size(axis) + position[axis]
    return at


def devices():
    positions = [{}]
    for axis in AXES:
        positions = [dict(p, **{axis: i}) for p in positions for i in range(lax.axis_size(axis))]
    return positions


def swapped(position, axis, first):
    i = position[axis]
    j = i + 1 if (i - first) % 2 == 0 else i - 1
    return dict(position, **{axis: j}) if first <= min(i, j) and max(i, j) < lax.axis_size(axis) else None


def exchange(face, axis, first):
    pairs = []
    for position in devices():
        partner = swapped(position, axis, first) or swapped(position, FILL[axis], 0)
        if partner is not None:
            pairs.append((device(position), device(partner)))
    return lax.ppermute(face, AXES, pairs)


def sets(axis):
    return [first for first in (0, 1) if lax.axis_size(axis) > 1 + first]


def arrivals(faces):
    pieces = {}
    for axis, first in [("gx", 0), ("gx", 1), ("gz", 0), ("gz", 1), ("gy", 1), ("gy", 0)]:
        if first in sets(axis):
            pieces[axis, first] = exchange(faces[AXES.index(axis)], axis, first)
    return [pieces[axis, first] for axis in AXES for first in sets(axis)]


def choose(arrived, axis, direction):
    size, at = lax.axis_size(axis), lax.axis_index(axis)
    shape, dtype = arrived[0].shape, arrived[0].dtype
    even = (1 - lax.rem(at, 2)).astype(jnp.float32)
    toward = direction[...].astype(jnp.float32)
    first = toward * even + (1.0 - toward) * (1.0 - even)
    zeros = jnp.zeros(shape, dtype)

    def where(row, value, other):
        mask = jnp.broadcast_to(row.astype(dtype)[:1], shape)
        return jnp.where(mask > 0, value, other)

    paired = (at + (1 - 2 * lax.rem(at, 2)) < size).astype(jnp.float32)
    if len(arrived) == 1:
        return where(first * paired, arrived[0][...], zeros)
    inner = jnp.where((at > 0) & (at + 2 * lax.rem(at, 2) - 1 < size), 1.0, 0.0)
    return where(first * paired, arrived[0][...], where((1.0 - first) * inner, arrived[1][...], zeros))


def inject(source, depth, step):
    mask = jnp.broadcast_to(depth[...][:1], source.shape)
    return jnp.where(mask <= step, source[...], jnp.zeros_like(source[...]))


def multiply(operator, lift, stack, faces):
    order = operator.shape[1]
    rows = order // len(AXES)
    for n, face in enumerate(faces):
        total = jnp.dot(operator[n * rows : (n + 1) * rows, :], stack[:order, :], preferred_element_type=jnp.float32)
        total += jnp.dot(lift[n * rows : (n + 1) * rows, :], stack[order:, :], preferred_element_type=jnp.float32)
        face[...] = total.astype(face.dtype)


def row_of(values, shape):
    batches, width = values.shape[0], shape[1]
    batch = lax.broadcasted_iota(jnp.int32, shape, 1) // (width // batches)
    out = jnp.zeros(shape, jnp.int32)
    for b in range(batches):
        out = jnp.where(batch == b, values[b], out)
    return out.astype(jnp.float32)


def first_kernel(*refs):
    inputs, (face_x, face_y, face_z, operator, lift, source, depth, direction) = refs[:6], refs[6:14]
    stack, depth_s, direction_s, sems = refs[14:]
    order = operator.shape[0]
    targets = (operator, lift, source, stack.at[:order, :], depth_s, direction_s)
    copies = [pltpu.make_async_copy(a, b, sems.at[n]) for n, (a, b) in enumerate(zip(inputs, targets))]
    for copy in reversed(copies):
        copy.start()
    for copy in reversed(copies[1:]):
        copy.wait()
    depth[...] = row_of(depth_s, depth.shape).astype(depth.dtype)
    direction[...] = row_of(direction_s, direction.shape).astype(direction.dtype)
    stack[order:, :] = inject(source, depth, 0)
    copies[0].wait()
    multiply(operator, lift, stack, (face_x, face_y, face_z))


def step_kernel(step, counts, operator, lift, source, depth, direction, *refs):
    arrived, faces, stack = refs[:-4], refs[-4:-1], refs[-1]
    order = operator.shape[0]
    assemble(counts, arrived, direction, stack.at[:order, :])
    stack[order:, :] = inject(source, depth, step)
    multiply(operator, lift, stack, faces)


def assemble(counts, arrived, direction, out):
    rows = out.shape[0] // len(AXES)
    at = 0
    for n, axis in enumerate(AXES):
        if counts[n]:
            out[n * rows : (n + 1) * rows, :] = choose(arrived[at : at + counts[n]], axis, direction)
        else:
            out[n * rows : (n + 1) * rows, :] = jnp.zeros((rows, out.shape[1]), out.dtype)
        at += counts[n]


def last_kernel(counts, direction, *refs):
    assemble(counts, refs[:-1], direction, refs[-1])


def body(operator, lift, source, traces_in, depth, direction):
    shape = traces_in.shape
    operator, lift, source, state = operator[0, 0, 0], lift[0, 0, 0], source[0, 0, 0], traces_in[0, 0, 0]
    order, width = state.shape
    like = lambda value: jax.ShapeDtypeStruct(value.shape, value.dtype)
    face = jax.ShapeDtypeStruct((order // len(AXES), width), state.dtype)
    row = jax.ShapeDtypeStruct((TILE, width), state.dtype)
    stack = pltpu.VMEM((order + source.shape[0], width), state.dtype)
    counts = [len(sets(axis)) for axis in AXES]
    params = pltpu.CompilerParams(vmem_limit_bytes=16 * 2**20)
    *faces, operator, lift, source, depth, direction = pl.pallas_call(
        first_kernel,
        out_shape=[face] * 3 + [like(operator), like(lift), like(source), row, row],
        in_specs=[HBM] * 6,
        out_specs=[VMEM] * 8,
        scratch_shapes=[
            stack,
            pltpu.SMEM(depth.shape, depth.dtype),
            pltpu.SMEM(direction.shape, direction.dtype),
            pltpu.SemaphoreType.DMA((6,)),
        ],
        compiler_params=params,
        name="first",
    )(*[pltpu.with_memory_space_constraint(value, pltpu.HBM) for value in (operator, lift, source, state, depth, direction)])
    for step in range(1, STEPS):
        arrived = arrivals(faces)
        faces = pl.pallas_call(
            functools.partial(step_kernel, step, counts),
            out_shape=[face] * 3,
            in_specs=[VMEM] * (5 + len(arrived)),
            out_specs=[VMEM] * 3,
            scratch_shapes=[stack],
            compiler_params=params,
            name=f"step{step}",
        )(operator, lift, source, depth, direction, *arrived)
    arrived = arrivals(faces)
    state = pl.pallas_call(
        functools.partial(last_kernel, counts),
        out_shape=like(state),
        in_specs=[VMEM] * (1 + len(arrived)),
        out_specs=VMEM,
        compiler_params=params,
        name="last",
    )(direction, *arrived)
    return state.reshape(shape)


def solution(mesh):
    placed = P("gx", "gy", "gz", None, None)
    return jax.shard_map(
        body,
        mesh=mesh,
        in_specs=(placed, placed, placed, placed, P(), P()),
        out_specs=placed,
        check_vma=False,
    )
```

time: 86.9 us -> 64.7 us (0.74)
  starting transfers between devices: 49.4 us -> 32.8 us
  local copies, waits for them, and re-layouts: 5.92 us -> 0 us
  waiting for transfers between devices: 19.5 us -> 21.2 us
  Pallas kernels: 11.2 us -> 9.57 us
    ppermute x30, starting transfers between devices: 49.4 us -> 32.8 us  [exchange(): return lax.ppermute(face, AXES, pairs)]
    unnamed x12 -> x0, local copies, waits for them, and re-layouts: 5.92 us -> none
    pallas_call x6 -> x5, Pallas kernels: 9.78 us -> 5.49 us  [body(): pl.pallas_call(functools.partial(step_kernel, step, counts), out_shape=[f...]
    pallas_call x1 -> x2, Pallas kernels: 1.42 us -> 4.08 us  [the longest x1 3.17 us: body(): pl.pallas_call(first_kernel, out_shape=[face] * 3 + [like(operator), like...]
    ppermute x30, waiting for transfers between devices: 19.5 us -> 21.2 us  [exchange(): return lax.ppermute(face, AXES, pairs)]
  transfers between devices with their start and end apart: 30 -> 30, of which waited for: 11 -> 13; matrix products, arithmetic and copies ran while one was open for 0% -> 0% of each run, Pallas kernels for 0% -> 0%
where the time goes in v2:
time: 64.7 us; the launch traced here: 63.6 us
  starting transfers between devices  32.8 us (51%)
  waiting for transfers between devices  21.2 us (33%)
  Pallas kernels  9.57 us (15%)
    ppermute x30, starting transfers between devices, exchange(): return lax.ppermute(face, AXES, pairs)  32.8 us
    ppermute x30, waiting for transfers between devices, exchange(): return lax.ppermute(face, AXES, pairs)  21.2 us
    pallas_call x5, Pallas kernels, body(): pl.pallas_call(functools.partial(step_kernel, step, counts), out_shape=[f...  5.49 us
    pallas_call x1, Pallas kernels, body(): pl.pallas_call(first_kernel, out_shape=[face] * 3 + [like(operator), like...  3.17 us
  transfers between devices with their start and end apart: 30, of which 13 were waited for; matrix products, arithmetic and copies ran while one was open for 0% of the time, Pallas kernels for 0%

profile of v2, /device:TPU:1, one launch (start us, length us, event | category | flops | bytes accessed | tf_op | source)
XLA Modules:
  0.0 63.6 jit_solution(5005944742849577717)
XLA Ops:
  0.0 3.2 %first.1 = (bf16[384,256]{1,0:T(8,128)(2,1)S(1)}, bf16[384,256]{1,0:T(8,128)(2,1)S(1)}, bf16[384,256]{1,0:T(8,128)(2,1)S(1)}, bf16[1152,1152]{1,0:T(8,128)(2,1)S...) custom-call(bf16[1152,1152]{1,0:T(8,128)(2,1)} %bitcast.5, ...), custom_call_target="tpu_custom_call" | custom-call | tf_op jit(solution)/shard_map/first/pallas_call | solution.py:151
  3.2 2.1 %collective-permute-start.4 = (bf16[384,256]{1,0:T(8,128)(2,1)S(1)}, bf16[384,256]{1,0:T(8,128)(2,1)S(1)}, u32[]{:S(2)}, u32[]{:S(2)}) collective-permute-start(bf16[384,256]{1,0:T(8,128)(2,1)S(1)} %get-tuple-element.35), channel_id=1, source_target_pairs={{0,1},{1,0},{2,3},{3,2},{4,5},{5,4},{6,7},{7,6},{8,9},{9,8},{10,11... | collective-permute-start | bytes 589832 | tf_op jit(solution)/shard_map/ppermute | solution.py:44
  5.3 1.0 %collective-permute-start.1 = (bf16[384,256]{1,0:T(8,128)(2,1)S(1)}, bf16[384,256]{1,0:T(8,128)(2,1)S(1)}, u32[]{:S(2)}, u32[]{:S(2)}) collective-permute-start(bf16[384,256]{1,0:T(8,128)(2,1)S(1)} %get-tuple-element.33), channel_id=1, source_target_pairs={{0,2},{1,3},{2,0},{3,1},{4,6},{5,7},{6,4},{7,5},{8,16},{9,17},{10,... | collective-permute-start | bytes 589832 | tf_op jit(solution)/shard_map/ppermute | solution.py:44
  6.2 1.6 %collective-permute-start = (bf16[384,256]{1,0:T(8,128)(2,1)S(1)}, bf16[384,256]{1,0:T(8,128)(2,1)S(1)}, u32[]{:S(2)}, u32[]{:S(2)}) collective-permute-start(bf16[384,256]{1,0:T(8,128)(2,1)S(1)} %get-tuple-element.33), channel_id=1, source_target_pairs={{0,8},{1,9},{2,10},{3,11},{4,12},{5,13},{6,14},{7,15},{8,0},{9,1},... | collective-permute-start | bytes 589832 | tf_op jit(solution)/shard_map/ppermute | solution.py:44
  7.9 2.6 %collective-permute-start.3 = (bf16[384,256]{1,0:T(8,128)(2,1)S(1)}, bf16[384,256]{1,0:T(8,128)(2,1)S(1)}, u32[]{:S(2)}, u32[]{:S(2)}) collective-permute-start(bf16[384,256]{1,0:T(8,128)(2,1)S(1)} %get-tuple-element.34), channel_id=1, source_target_pairs={{0,1},{1,0},{2,4},{3,5},{4,2},{5,3},{6,7},{7,6},{8,9},{9,8},{10,12... | collective-permute-start | bytes 589832 | tf_op jit(solution)/shard_map/ppermute | solution.py:44
  10.5 1.4 %collective-permute-done.refs_0_ = bf16[384,256]{1,0:T(8,128)(2,1)S(1)} collective-permute-done((bf16[384,256]{1,0:T(8,128)(2,1)S(1)}, bf16[384,256]{1,0:T(8,128)(2,1)S(1)}, u32[]{:S(2)}, u32[]{:S(2)}) %collective-permute-start) | collective-permute-done | bytes 196640 | tf_op jit(solution)/shard_map/ppermute | solution.py:44
  11.9 2.2 %collective-permute-done.3.refs_3_ = bf16[384,256]{1,0:T(8,128)(2,1)S(1)} collective-permute-done((bf16[384,256]{1,0:T(8,128)(2,1)S(1)}, bf16[384,256]{1,0:T(8,128)(2,1)S(1)}, u32[]{:S(2)}, u32[]{:S(2)}) %collective-permute-start.3) | collective-permute-done | bytes 196640 | tf_op jit(solution)/shard_map/ppermute | solution.py:44
  14.2 1.1 %step1.1 = (bf16[384,256]{1,0:T(8,128)(2,1)S(1)}, bf16[384,256]{1,0:T(8,128)(2,1)S(1)}, bf16[384,256]{1,0:T(8,128)(2,1)S(1)}) custom-call(bf16[1152,1152]{1,0:T(8,128)(2,1)S(1)} %get-tuple-element.29.operator, bf16[1152,128]{1,0:T(8,128)(2,1)S(1)} %get-tuple-element.30.lift, bf16[128,256]{1,0:T(8,128)(2,1)S(1)} %get-tuple-element.31.source, ...), custom_call_target="tpu_custom_call" | custom-call | tf_op jit(solution)/shard_map/step1/pallas_call | solution.py:167
  15.6 1.2 %collective-permute-start.6 = (bf16[384,256]{1,0:T(8,128)(2,1)S(1)}, bf16[384,256]{1,0:T(8,128)(2,1)S(1)}, u32[]{:S(2)}, u32[]{:S(2)}) collective-permute-start(bf16[384,256]{1,0:T(8,128)(2,1)S(1)} %get-tuple-element.36), channel_id=1, source_target_pairs={{0,2},{1,3},{2,0},{3,1},{4,6},{5,7},{6,4},{7,5},{8,16},{9,17},{10,... | collective-permute-start | bytes 589832 | tf_op jit(solution)/shard_map/ppermute | solution.py:44
  16.9 2.5 %collective-permute-start.8 = (bf16[384,256]{1,0:T(8,128)(2,1)S(1)}, bf16[384,256]{1,0:T(8,128)(2,1)S(1)}, u32[]{:S(2)}, u32[]{:S(2)}) collective-permute-start(bf16[384,256]{1,0:T(8,128)(2,1)S(1)} %get-tuple-element.37), channel_id=1, source_target_pairs={{0,1},{1,0},{2,4},{3,5},{4,2},{5,3},{6,7},{7,6},{8,9},{9,8},{10,12... | collective-permute-start | bytes 589832 | tf_op jit(solution)/shard_map/ppermute | solution.py:44
  19.8 1.0 %collective-permute-done.9.refs_4_ = bf16[384,256]{1,0:T(8,128)(2,1)S(1)} collective-permute-done((bf16[384,256]{1,0:T(8,128)(2,1)S(1)}, bf16[384,256]{1,0:T(8,128)(2,1)S(1)}, u32[]{:S(2)}, u32[]{:S(2)}) %collective-permute-start.9) | collective-permute-done | bytes 196640 | tf_op jit(solution)/shard_map/ppermute | solution.py:44
  20.9 1.8 %collective-permute-done.5.refs_0_ = bf16[384,256]{1,0:T(8,128)(2,1)S(1)} collective-permute-done((bf16[384,256]{1,0:T(8,128)(2,1)S(1)}, bf16[384,256]{1,0:T(8,128)(2,1)S(1)}, u32[]{:S(2)}, u32[]{:S(2)}) %collective-permute-start.5) | collective-permute-done | bytes 196640 | tf_op jit(solution)/shard_map/ppermute | solution.py:44
  23.1 1.1 %step2.1 = (bf16[384,256]{1,0:T(8,128)(2,1)S(1)}, bf16[384,256]{1,0:T(8,128)(2,1)S(1)}, bf16[384,256]{1,0:T(8,128)(2,1)S(1)}) custom-call(bf16[1152,1152]{1,0:T(8,128)(2,1)S(1)} %get-tuple-element.29.operator, bf16[1152,128]{1,0:T(8,128)(2,1)S(1)} %get-tuple-element.30.lift, bf16[128,256]{1,0:T(8,128)(2,1)S(1)} %get-tuple-element.31.source, ...), custom_call_target="tpu_custom_call" | custom-call | tf_op jit(solution)/shard_map/step2/pallas_call | solution.py:167
  24.2 1.4 %collective-permute-start.14 = (bf16[384,256]{1,0:T(8,128)(2,1)S(1)}, bf16[384,256]{1,0:T(8,128)(2,1)S(1)}, u32[]{:S(2)}, u32[]{:S(2)}) collective-permute-start(bf16[384,256]{1,0:T(8,128)(2,1)S(1)} %get-tuple-element.41), channel_id=1, source_target_pairs={{0,1},{1,0},{2,3},{3,2},{4,5},{5,4},{6,7},{7,6},{8,9},{9,8},{10,11... | collective-permute-start | bytes 589832 | tf_op jit(solution)/shard_map/ppermute | solution.py:44
  25.6 1.1 %collective-permute-start.11 = (bf16[384,256]{1,0:T(8,128)(2,1)S(1)}, bf16[384,256]{1,0:T(8,128)(2,1)S(1)}, u32[]{:S(2)}, u32[]{:S(2)}) collective-permute-start(bf16[384,256]{1,0:T(8,128)(2,1)S(1)} %get-tuple-element.39), channel_id=1, source_target_pairs={{0,2},{1,3},{2,0},{3,1},{4,6},{5,7},{6,4},{7,5},{8,16},{9,17},{10,... | collective-permute-start | bytes 589832 | tf_op jit(solution)/shard_map/ppermute | solution.py:44
  26.9 2.4 %collective-permute-start.13 = (bf16[384,256]{1,0:T(8,128)(2,1)S(1)}, bf16[384,256]{1,0:T(8,128)(2,1)S(1)}, u32[]{:S(2)}, u32[]{:S(2)}) collective-permute-start(bf16[384,256]{1,0:T(8,128)(2,1)S(1)} %get-tuple-element.40), channel_id=1, source_target_pairs={{0,1},{1,0},{2,4},{3,5},{4,2},{5,3},{6,7},{7,6},{8,9},{9,8},{10,12... | collective-permute-start | bytes 589832 | tf_op jit(solution)/shard_map/ppermute | solution.py:44
  29.9 3.3 %collective-permute-done.10.refs_0_ = bf16[384,256]{1,0:T(8,128)(2,1)S(1)} collective-permute-done((bf16[384,256]{1,0:T(8,128)(2,1)S(1)}, bf16[384,256]{1,0:T(8,128)(2,1)S(1)}, u32[]{:S(2)}, u32[]{:S(2)}) %collective-permute-start.10) | collective-permute-done | bytes 196640 | tf_op jit(solution)/shard_map/ppermute | solution.py:44
  33.2 1.1 %step3.1 = (bf16[384,256]{1,0:T(8,128)(2,1)S(1)}, bf16[384,256]{1,0:T(8,128)(2,1)S(1)}, bf16[384,256]{1,0:T(8,128)(2,1)S(1)}) custom-call(bf16[1152,1152]{1,0:T(8,128)(2,1)S(1)} %get-tuple-element.29.operator, bf16[1152,128]{1,0:T(8,128)(2,1)S(1)} %get-tuple-element.30.lift, bf16[128,256]{1,0:T(8,128)(2,1)S(1)} %get-tuple-element.31.source, ...), custom_call_target="tpu_custom_call" | custom-call | tf_op jit(solution)/shard_map/step3/pallas_call | solution.py:167
  34.3 1.2 %collective-permute-start.19 = (bf16[384,256]{1,0:T(8,128)(2,1)S(1)}, bf16[384,256]{1,0:T(8,128)(2,1)S(1)}, u32[]{:S(2)}, u32[]{:S(2)}) collective-permute-start(bf16[384,256]{1,0:T(8,128)(2,1)S(1)} %get-tuple-element.44), channel_id=1, source_target_pairs={{0,1},{1,0},{2,3},{3,2},{4,5},{5,4},{6,7},{7,6},{8,9},{9,8},{10,11... | collective-permute-start | bytes 589832 | tf_op jit(solution)/shard_map/ppermute | solution.py:44
  35.5 1.2 %collective-permute-start.16 = (bf16[384,256]{1,0:T(8,128)(2,1)S(1)}, bf16[384,256]{1,0:T(8,128)(2,1)S(1)}, u32[]{:S(2)}, u32[]{:S(2)}) collective-permute-start(bf16[384,256]{1,0:T(8,128)(2,1)S(1)} %get-tuple-element.42), channel_id=1, source_target_pairs={{0,2},{1,3},{2,0},{3,1},{4,6},{5,7},{6,4},{7,5},{8,16},{9,17},{10,... | collective-permute-start | bytes 589832 | tf_op jit(solution)/shard_map/ppermute | solution.py:44
  36.8 2.3 %collective-permute-start.18 = (bf16[384,256]{1,0:T(8,128)(2,1)S(1)}, bf16[384,256]{1,0:T(8,128)(2,1)S(1)}, u32[]{:S(2)}, u32[]{:S(2)}) collective-permute-start(bf16[384,256]{1,0:T(8,128)(2,1)S(1)} %get-tuple-element.43), channel_id=1, source_target_pairs={{0,1},{1,0},{2,4},{3,5},{4,2},{5,3},{6,7},{7,6},{8,9},{9,8},{10,12... | collective-permute-start | bytes 589832 | tf_op jit(solution)/shard_map/ppermute | solution.py:44
  40.0 3.2 %collective-permute-done.15.refs_0_ = bf16[384,256]{1,0:T(8,128)(2,1)S(1)} collective-permute-done((bf16[384,256]{1,0:T(8,128)(2,1)S(1)}, bf16[384,256]{1,0:T(8,128)(2,1)S(1)}, u32[]{:S(2)}, u32[]{:S(2)}) %collective-permute-start.15) | collective-permute-done | bytes 196640 | tf_op jit(solution)/shard_map/ppermute | solution.py:44
  43.2 1.1 %step4.1 = (bf16[384,256]{1,0:T(8,128)(2,1)S(1)}, bf16[384,256]{1,0:T(8,128)(2,1)S(1)}, bf16[384,256]{1,0:T(8,128)(2,1)S(1)}) custom-call(bf16[1152,1152]{1,0:T(8,128)(2,1)S(1)} %get-tuple-element.29.operator, bf16[1152,128]{1,0:T(8,128)(2,1)S(1)} %get-tuple-element.30.lift, bf16[128,256]{1,0:T(8,128)(2,1)S(1)} %get-tuple-element.31.source, ...), custom_call_target="tpu_custom_call" | custom-call | tf_op jit(solution)/shard_map/step4/pallas_call | solution.py:167
  44.6 2.0 %collective-permute-start.21 = (bf16[384,256]{1,0:T(8,128)(2,1)S(1)}, bf16[384,256]{1,0:T(8,128)(2,1)S(1)}, u32[]{:S(2)}, u32[]{:S(2)}) collective-permute-start(bf16[384,256]{1,0:T(8,128)(2,1)S(1)} %get-tuple-element.45), channel_id=1, source_target_pairs={{0,2},{1,3},{2,0},{3,1},{4,6},{5,7},{6,4},{7,5},{8,16},{9,17},{10,... | collective-permute-start | bytes 589832 | tf_op jit(solution)/shard_map/ppermute | solution.py:44
  46.6 2.5 %collective-permute-start.23 = (bf16[384,256]{1,0:T(8,128)(2,1)S(1)}, bf16[384,256]{1,0:T(8,128)(2,1)S(1)}, u32[]{:S(2)}, u32[]{:S(2)}) collective-permute-start(bf16[384,256]{1,0:T(8,128)(2,1)S(1)} %get-tuple-element.46), channel_id=1, source_target_pairs={{0,1},{1,0},{2,4},{3,5},{4,2},{5,3},{6,7},{7,6},{8,9},{9,8},{10,12... | collective-permute-start | bytes 589832 | tf_op jit(solution)/shard_map/ppermute | solution.py:44
  49.9 3.1 %collective-permute-done.20.refs_0_ = bf16[384,256]{1,0:T(8,128)(2,1)S(1)} collective-permute-done((bf16[384,256]{1,0:T(8,128)(2,1)S(1)}, bf16[384,256]{1,0:T(8,128)(2,1)S(1)}, u32[]{:S(2)}, u32[]{:S(2)}) %collective-permute-start.20) | collective-permute-done | bytes 196640 | tf_op jit(solution)/shard_map/ppermute | solution.py:44
  53.1 1.1 %step5.1 = (bf16[384,256]{1,0:T(8,128)(2,1)S(1)}, bf16[384,256]{1,0:T(8,128)(2,1)S(1)}, bf16[384,256]{1,0:T(8,128)(2,1)S(1)}) custom-call(bf16[1152,1152]{1,0:T(8,128)(2,1)S(1)} %get-tuple-element.29.operator, bf16[1152,128]{1,0:T(8,128)(2,1)S(1)} %get-tuple-element.30.lift, bf16[128,256]{1,0:T(8,128)(2,1)S(1)} %get-tuple-element.31.source, ...), custom_call_target="tpu_custom_call" | custom-call | tf_op jit(solution)/shard_map/step5/pallas_call | solution.py:167
  54.6 1.2 %collective-permute-start.26 = (bf16[384,256]{1,0:T(8,128)(2,1)S(1)}, bf16[384,256]{1,0:T(8,128)(2,1)S(1)}, u32[]{:S(2)}, u32[]{:S(2)}) collective-permute-start(bf16[384,256]{1,0:T(8,128)(2,1)S(1)} %get-tuple-element.48), channel_id=1, source_target_pairs={{0,2},{1,3},{2,0},{3,1},{4,6},{5,7},{6,4},{7,5},{8,16},{9,17},{10,... | collective-permute-start | bytes 589832 | tf_op jit(solution)/shard_map/ppermute | solution.py:44
  56.1 3.0 %collective-permute-start.28 = (bf16[384,256]{1,0:T(8,128)(2,1)S(1)}, bf16[384,256]{1,0:T(8,128)(2,1)S(1)}, u32[]{:S(2)}, u32[]{:S(2)}) collective-permute-start(bf16[384,256]{1,0:T(8,128)(2,1)S(1)} %get-tuple-element.49), channel_id=1, source_target_pairs={{0,1},{1,0},{2,4},{3,5},{4,2},{5,3},{6,7},{7,6},{8,9},{9,8},{10,12... | collective-permute-start | bytes 589832 | tf_op jit(solution)/shard_map/ppermute | solution.py:44
  59.1 0.8 %collective-permute-done.29.refs_4_ = bf16[384,256]{1,0:T(8,128)(2,1)S(1)} collective-permute-done((bf16[384,256]{1,0:T(8,128)(2,1)S(1)}, bf16[384,256]{1,0:T(8,128)(2,1)S(1)}, u32[]{:S(2)}, u32[]{:S(2)}) %collective-permute-start.29) | collective-permute-done | bytes 196640 | tf_op jit(solution)/shard_map/ppermute | solution.py:44
  59.9 2.1 %collective-permute-done.25.refs_0_ = bf16[384,256]{1,0:T(8,128)(2,1)S(1)} collective-permute-done((bf16[384,256]{1,0:T(8,128)(2,1)S(1)}, bf16[384,256]{1,0:T(8,128)(2,1)S(1)}, u32[]{:S(2)}, u32[]{:S(2)}) %collective-permute-start.25) | collective-permute-done | bytes 196640 | tf_op jit(solution)/shard_map/ppermute | solution.py:44
  62.7 0.9 %last.1 = bf16[1152,256]{1,0:T(8,128)(2,1)} custom-call(bf16[16,256]{1,0:T(8,128)(2,1)S(1)} %get-tuple-element.28.direction, bf16[384,256]{1,0:T(8,128)(2,1)S(1)} %collective-permute-done.25.refs_0_, bf16[384,256]{1,0:T(8,128)(2,1)S(1)} %collective-permute-done.26.refs_1_, bf16[384,256]{1,0:T(8,128)(2,1)S(1)} %collective-permute-done.27.refs_2_, ...), custom_call_target="tpu_custom_call" | custom-call | tf_op jit(solution)/shard_map/last/pallas_call | solution.py:177
  (35 shorter events, 5.6 us)
Async XLA Ops:
  3.2 7.3 %collective-permute-start.4 = (bf16[384,256]{1,0:T(8,128)(2,1)S(1)}, bf16[384,256]{1,0:T(8,128)(2,1)S(1)}, u32[]{:S(2)}, u32[]{:S(2)}) collective-permute-start(bf16[384,256]{1,0:T(8,128)(2,1)S(1)} %get-tuple-element.35), channel_id=1, source_target_pairs={{0,1},{1,0},{2,3},{3,2},{4,5},{5,4},{6,7},{7,6},{8,9},{9,8},{10,11... | collective-permute-start | bytes 589832 | tf_op jit(solution)/shard_map/ppermute | solution.py:44
  5.3 5.2 %collective-permute-start.1 = (bf16[384,256]{1,0:T(8,128)(2,1)S(1)}, bf16[384,256]{1,0:T(8,128)(2,1)S(1)}, u32[]{:S(2)}, u32[]{:S(2)}) collective-permute-start(bf16[384,256]{1,0:T(8,128)(2,1)S(1)} %get-tuple-element.33), channel_id=1, source_target_pairs={{0,2},{1,3},{2,0},{3,1},{4,6},{5,7},{6,4},{7,5},{8,16},{9,17},{10,... | collective-permute-start | bytes 589832 | tf_op jit(solution)/shard_map/ppermute | solution.py:44
  6.2 5.7 %collective-permute-start = (bf16[384,256]{1,0:T(8,128)(2,1)S(1)}, bf16[384,256]{1,0:T(8,128)(2,1)S(1)}, u32[]{:S(2)}, u32[]{:S(2)}) collective-permute-start(bf16[384,256]{1,0:T(8,128)(2,1)S(1)} %get-tuple-element.33), channel_id=1, source_target_pairs={{0,8},{1,9},{2,10},{3,11},{4,12},{5,13},{6,14},{7,15},{8,0},{9,1},... | collective-permute-start | bytes 589832 | tf_op jit(solution)/shard_map/ppermute | solution.py:44
  7.9 6.3 %collective-permute-start.3 = (bf16[384,256]{1,0:T(8,128)(2,1)S(1)}, bf16[384,256]{1,0:T(8,128)(2,1)S(1)}, u32[]{:S(2)}, u32[]{:S(2)}) collective-permute-start(bf16[384,256]{1,0:T(8,128)(2,1)S(1)} %get-tuple-element.34), channel_id=1, source_target_pairs={{0,1},{1,0},{2,4},{3,5},{4,2},{5,3},{6,7},{7,6},{8,9},{9,8},{10,12... | collective-permute-start | bytes 589832 | tf_op jit(solution)/shard_map/ppermute | solution.py:44
  10.5 3.6 %collective-permute-start.2 = (bf16[384,256]{1,0:T(8,128)(2,1)S(1)}, bf16[384,256]{1,0:T(8,128)(2,1)S(1)}, u32[]{:S(2)}, u32[]{:S(2)}) collective-permute-start(bf16[384,256]{1,0:T(8,128)(2,1)S(1)} %get-tuple-element.34), channel_id=1, source_target_pairs={{0,2},{1,3},{2,0},{3,1},{4,6},{5,7},{6,4},{7,5},{8,10},{9,11},{10,... | collective-permute-start | bytes 589832 | tf_op jit(solution)/shard_map/ppermute | solution.py:44
  15.3 5.6 %collective-permute-start.9 = (bf16[384,256]{1,0:T(8,128)(2,1)S(1)}, bf16[384,256]{1,0:T(8,128)(2,1)S(1)}, u32[]{:S(2)}, u32[]{:S(2)}) collective-permute-start(bf16[384,256]{1,0:T(8,128)(2,1)S(1)} %get-tuple-element.38), channel_id=1, source_target_pairs={{0,1},{1,0},{2,3},{3,2},{4,5},{5,4},{6,7},{7,6},{8,9},{9,8},{10,11... | collective-permute-start | bytes 589832 | tf_op jit(solution)/shard_map/ppermute | solution.py:44
  15.6 5.3 %collective-permute-start.6 = (bf16[384,256]{1,0:T(8,128)(2,1)S(1)}, bf16[384,256]{1,0:T(8,128)(2,1)S(1)}, u32[]{:S(2)}, u32[]{:S(2)}) collective-permute-start(bf16[384,256]{1,0:T(8,128)(2,1)S(1)} %get-tuple-element.36), channel_id=1, source_target_pairs={{0,2},{1,3},{2,0},{3,1},{4,6},{5,7},{6,4},{7,5},{8,16},{9,17},{10,... | collective-permute-start | bytes 589832 | tf_op jit(solution)/shard_map/ppermute | solution.py:44
  16.8 5.9 %collective-permute-start.5 = (bf16[384,256]{1,0:T(8,128)(2,1)S(1)}, bf16[384,256]{1,0:T(8,128)(2,1)S(1)}, u32[]{:S(2)}, u32[]{:S(2)}) collective-permute-start(bf16[384,256]{1,0:T(8,128)(2,1)S(1)} %get-tuple-element.36), channel_id=1, source_target_pairs={{0,8},{1,9},{2,10},{3,11},{4,12},{5,13},{6,14},{7,15},{8,0},{9,1},... | collective-permute-start | bytes 589832 | tf_op jit(solution)/shard_map/ppermute | solution.py:44
  16.9 6.2 %collective-permute-start.8 = (bf16[384,256]{1,0:T(8,128)(2,1)S(1)}, bf16[384,256]{1,0:T(8,128)(2,1)S(1)}, u32[]{:S(2)}, u32[]{:S(2)}) collective-permute-start(bf16[384,256]{1,0:T(8,128)(2,1)S(1)} %get-tuple-element.37), channel_id=1, source_target_pairs={{0,1},{1,0},{2,4},{3,5},{4,2},{5,3},{6,7},{7,6},{8,9},{9,8},{10,12... | collective-permute-start | bytes 589832 | tf_op jit(solution)/shard_map/ppermute | solution.py:44
  19.5 3.6 %collective-permute-start.7 = (bf16[384,256]{1,0:T(8,128)(2,1)S(1)}, bf16[384,256]{1,0:T(8,128)(2,1)S(1)}, u32[]{:S(2)}, u32[]{:S(2)}) collective-permute-start(bf16[384,256]{1,0:T(8,128)(2,1)S(1)} %get-tuple-element.37), channel_id=1, source_target_pairs={{0,2},{1,3},{2,0},{3,1},{4,6},{5,7},{6,4},{7,5},{8,10},{9,11},{10,... | collective-permute-start | bytes 589832 | tf_op jit(solution)/shard_map/ppermute | solution.py:44
  24.2 5.6 %collective-permute-start.14 = (bf16[384,256]{1,0:T(8,128)(2,1)S(1)}, bf16[384,256]{1,0:T(8,128)(2,1)S(1)}, u32[]{:S(2)}, u32[]{:S(2)}) collective-permute-start(bf16[384,256]{1,0:T(8,128)(2,1)S(1)} %get-tuple-element.41), channel_id=1, source_target_pairs={{0,1},{1,0},{2,3},{3,2},{4,5},{5,4},{6,7},{7,6},{8,9},{9,8},{10,11... | collective-permute-start | bytes 589832 | tf_op jit(solution)/shard_map/ppermute | solution.py:44
  25.6 4.3 %collective-permute-start.11 = (bf16[384,256]{1,0:T(8,128)(2,1)S(1)}, bf16[384,256]{1,0:T(8,128)(2,1)S(1)}, u32[]{:S(2)}, u32[]{:S(2)}) collective-permute-start(bf16[384,256]{1,0:T(8,128)(2,1)S(1)} %get-tuple-element.39), channel_id=1, source_target_pairs={{0,2},{1,3},{2,0},{3,1},{4,6},{5,7},{6,4},{7,5},{8,16},{9,17},{10,... | collective-permute-start | bytes 589832 | tf_op jit(solution)/shard_map/ppermute | solution.py:44
  26.7 6.5 %collective-permute-start.10 = (bf16[384,256]{1,0:T(8,128)(2,1)S(1)}, bf16[384,256]{1,0:T(8,128)(2,1)S(1)}, u32[]{:S(2)}, u32[]{:S(2)}) collective-permute-start(bf16[384,256]{1,0:T(8,128)(2,1)S(1)} %get-tuple-element.39), channel_id=1, source_target_pairs={{0,8},{1,9},{2,10},{3,11},{4,12},{5,13},{6,14},{7,15},{8,0},{9,1},... | collective-permute-start | bytes 589832 | tf_op jit(solution)/shard_map/ppermute | solution.py:44
  26.9 6.3 %collective-permute-start.13 = (bf16[384,256]{1,0:T(8,128)(2,1)S(1)}, bf16[384,256]{1,0:T(8,128)(2,1)S(1)}, u32[]{:S(2)}, u32[]{:S(2)}) collective-permute-start(bf16[384,256]{1,0:T(8,128)(2,1)S(1)} %get-tuple-element.40), channel_id=1, source_target_pairs={{0,1},{1,0},{2,4},{3,5},{4,2},{5,3},{6,7},{7,6},{8,9},{9,8},{10,12... | collective-permute-start | bytes 589832 | tf_op jit(solution)/shard_map/ppermute | solution.py:44
  29.4 3.9 %collective-permute-start.12 = (bf16[384,256]{1,0:T(8,128)(2,1)S(1)}, bf16[384,256]{1,0:T(8,128)(2,1)S(1)}, u32[]{:S(2)}, u32[]{:S(2)}) collective-permute-start(bf16[384,256]{1,0:T(8,128)(2,1)S(1)} %get-tuple-element.40), channel_id=1, source_target_pairs={{0,2},{1,3},{2,0},{3,1},{4,6},{5,7},{6,4},{7,5},{8,10},{9,11},{10,... | collective-permute-start | bytes 589832 | tf_op jit(solution)/shard_map/ppermute | solution.py:44
  34.3 5.7 %collective-permute-start.19 = (bf16[384,256]{1,0:T(8,128)(2,1)S(1)}, bf16[384,256]{1,0:T(8,128)(2,1)S(1)}, u32[]{:S(2)}, u32[]{:S(2)}) collective-permute-start(bf16[384,256]{1,0:T(8,128)(2,1)S(1)} %get-tuple-element.44), channel_id=1, source_target_pairs={{0,1},{1,0},{2,3},{3,2},{4,5},{5,4},{6,7},{7,6},{8,9},{9,8},{10,11... | collective-permute-start | bytes 589832 | tf_op jit(solution)/shard_map/ppermute | solution.py:44
  35.5 4.5 %collective-permute-start.16 = (bf16[384,256]{1,0:T(8,128)(2,1)S(1)}, bf16[384,256]{1,0:T(8,128)(2,1)S(1)}, u32[]{:S(2)}, u32[]{:S(2)}) collective-permute-start(bf16[384,256]{1,0:T(8,128)(2,1)S(1)} %get-tuple-element.42), channel_id=1, source_target_pairs={{0,2},{1,3},{2,0},{3,1},{4,6},{5,7},{6,4},{7,5},{8,16},{9,17},{10,... | collective-permute-start | bytes 589832 | tf_op jit(solution)/shard_map/ppermute | solution.py:44
  36.7 6.5 %collective-permute-start.15 = (bf16[384,256]{1,0:T(8,128)(2,1)S(1)}, bf16[384,256]{1,0:T(8,128)(2,1)S(1)}, u32[]{:S(2)}, u32[]{:S(2)}) collective-permute-start(bf16[384,256]{1,0:T(8,128)(2,1)S(1)} %get-tuple-element.42), channel_id=1, source_target_pairs={{0,8},{1,9},{2,10},{3,11},{4,12},{5,13},{6,14},{7,15},{8,0},{9,1},... | collective-permute-start | bytes 589832 | tf_op jit(solution)/shard_map/ppermute | solution.py:44
  36.8 6.3 %collective-permute-start.18 = (bf16[384,256]{1,0:T(8,128)(2,1)S(1)}, bf16[384,256]{1,0:T(8,128)(2,1)S(1)}, u32[]{:S(2)}, u32[]{:S(2)}) collective-permute-start(bf16[384,256]{1,0:T(8,128)(2,1)S(1)} %get-tuple-element.43), channel_id=1, source_target_pairs={{0,1},{1,0},{2,4},{3,5},{4,2},{5,3},{6,7},{7,6},{8,9},{9,8},{10,12... | collective-permute-start | bytes 589832 | tf_op jit(solution)/shard_map/ppermute | solution.py:44
  39.2 4.0 %collective-permute-start.17 = (bf16[384,256]{1,0:T(8,128)(2,1)S(1)}, bf16[384,256]{1,0:T(8,128)(2,1)S(1)}, u32[]{:S(2)}, u32[]{:S(2)}) collective-permute-start(bf16[384,256]{1,0:T(8,128)(2,1)S(1)} %get-tuple-element.43), channel_id=1, source_target_pairs={{0,2},{1,3},{2,0},{3,1},{4,6},{5,7},{6,4},{7,5},{8,10},{9,11},{10,... | collective-permute-start | bytes 589832 | tf_op jit(solution)/shard_map/ppermute | solution.py:44
  44.3 5.7 %collective-permute-start.24 = (bf16[384,256]{1,0:T(8,128)(2,1)S(1)}, bf16[384,256]{1,0:T(8,128)(2,1)S(1)}, u32[]{:S(2)}, u32[]{:S(2)}) collective-permute-start(bf16[384,256]{1,0:T(8,128)(2,1)S(1)} %get-tuple-element.47), channel_id=1, source_target_pairs={{0,1},{1,0},{2,3},{3,2},{4,5},{5,4},{6,7},{7,6},{8,9},{9,8},{10,11... | collective-permute-start | bytes 589832 | tf_op jit(solution)/shard_map/ppermute | solution.py:44
  44.6 5.4 %collective-permute-start.21 = (bf16[384,256]{1,0:T(8,128)(2,1)S(1)}, bf16[384,256]{1,0:T(8,128)(2,1)S(1)}, u32[]{:S(2)}, u32[]{:S(2)}) collective-permute-start(bf16[384,256]{1,0:T(8,128)(2,1)S(1)} %get-tuple-element.45), channel_id=1, source_target_pairs={{0,2},{1,3},{2,0},{3,1},{4,6},{5,7},{6,4},{7,5},{8,16},{9,17},{10,... | collective-permute-start | bytes 589832 | tf_op jit(solution)/shard_map/ppermute | solution.py:44
  46.6 6.5 %collective-permute-start.20 = (bf16[384,256]{1,0:T(8,128)(2,1)S(1)}, bf16[384,256]{1,0:T(8,128)(2,1)S(1)}, u32[]{:S(2)}, u32[]{:S(2)}) collective-permute-start(bf16[384,256]{1,0:T(8,128)(2,1)S(1)} %get-tuple-element.45), channel_id=1, source_target_pairs={{0,8},{1,9},{2,10},{3,11},{4,12},{5,13},{6,14},{7,15},{8,0},{9,1},... | collective-permute-start | bytes 589832 | tf_op jit(solution)/shard_map/ppermute | solution.py:44
  46.6 6.5 %collective-permute-start.23 = (bf16[384,256]{1,0:T(8,128)(2,1)S(1)}, bf16[384,256]{1,0:T(8,128)(2,1)S(1)}, u32[]{:S(2)}, u32[]{:S(2)}) collective-permute-start(bf16[384,256]{1,0:T(8,128)(2,1)S(1)} %get-tuple-element.46), channel_id=1, source_target_pairs={{0,1},{1,0},{2,4},{3,5},{4,2},{5,3},{6,7},{7,6},{8,9},{9,8},{10,12... | collective-permute-start | bytes 589832 | tf_op jit(solution)/shard_map/ppermute | solution.py:44
  49.2 3.9 %collective-permute-start.22 = (bf16[384,256]{1,0:T(8,128)(2,1)S(1)}, bf16[384,256]{1,0:T(8,128)(2,1)S(1)}, u32[]{:S(2)}, u32[]{:S(2)}) collective-permute-start(bf16[384,256]{1,0:T(8,128)(2,1)S(1)} %get-tuple-element.46), channel_id=1, source_target_pairs={{0,2},{1,3},{2,0},{3,1},{4,6},{5,7},{6,4},{7,5},{8,10},{9,11},{10,... | collective-permute-start | bytes 589832 | tf_op jit(solution)/shard_map/ppermute | solution.py:44
  54.2 5.7 %collective-permute-start.29 = (bf16[384,256]{1,0:T(8,128)(2,1)S(1)}, bf16[384,256]{1,0:T(8,128)(2,1)S(1)}, u32[]{:S(2)}, u32[]{:S(2)}) collective-permute-start(bf16[384,256]{1,0:T(8,128)(2,1)S(1)} %get-tuple-element.50), channel_id=1, source_target_pairs={{0,1},{1,0},{2,3},{3,2},{4,5},{5,4},{6,7},{7,6},{8,9},{9,8},{10,11... | collective-permute-start | bytes 589832 | tf_op jit(solution)/shard_map/ppermute | solution.py:44
  54.6 5.3 %collective-permute-start.26 = (bf16[384,256]{1,0:T(8,128)(2,1)S(1)}, bf16[384,256]{1,0:T(8,128)(2,1)S(1)}, u32[]{:S(2)}, u32[]{:S(2)}) collective-permute-start(bf16[384,256]{1,0:T(8,128)(2,1)S(1)} %get-tuple-element.48), channel_id=1, source_target_pairs={{0,2},{1,3},{2,0},{3,1},{4,6},{5,7},{6,4},{7,5},{8,16},{9,17},{10,... | collective-permute-start | bytes 589832 | tf_op jit(solution)/shard_map/ppermute | solution.py:44
  55.7 6.2 %collective-permute-start.25 = (bf16[384,256]{1,0:T(8,128)(2,1)S(1)}, bf16[384,256]{1,0:T(8,128)(2,1)S(1)}, u32[]{:S(2)}, u32[]{:S(2)}) collective-permute-start(bf16[384,256]{1,0:T(8,128)(2,1)S(1)} %get-tuple-element.48), channel_id=1, source_target_pairs={{0,8},{1,9},{2,10},{3,11},{4,12},{5,13},{6,14},{7,15},{8,0},{9,1},... | collective-permute-start | bytes 589832 | tf_op jit(solution)/shard_map/ppermute | solution.py:44
  56.1 6.6 %collective-permute-start.28 = (bf16[384,256]{1,0:T(8,128)(2,1)S(1)}, bf16[384,256]{1,0:T(8,128)(2,1)S(1)}, u32[]{:S(2)}, u32[]{:S(2)}) collective-permute-start(bf16[384,256]{1,0:T(8,128)(2,1)S(1)} %get-tuple-element.49), channel_id=1, source_target_pairs={{0,1},{1,0},{2,4},{3,5},{4,2},{5,3},{6,7},{7,6},{8,9},{9,8},{10,12... | collective-permute-start | bytes 589832 | tf_op jit(solution)/shard_map/ppermute | solution.py:44
  59.1 3.6 %collective-permute-start.27 = (bf16[384,256]{1,0:T(8,128)(2,1)S(1)}, bf16[384,256]{1,0:T(8,128)(2,1)S(1)}, u32[]{:S(2)}, u32[]{:S(2)}) collective-permute-start(bf16[384,256]{1,0:T(8,128)(2,1)S(1)} %get-tuple-element.49), channel_id=1, source_target_pairs={{0,2},{1,3},{2,0},{3,1},{4,6},{5,7},{6,4},{7,5},{8,10},{9,11},{10,... | collective-permute-start | bytes 589832 | tf_op jit(solution)/shard_map/ppermute | solution.py:44

commit v3 on v2

--- a/solution.py
+++ b/solution.py
@@ -9,7 +9,7 @@
 
 STEPS = 6
 AXES = ("gx", "gy", "gz")
-FILL = {"gx": "gy", "gy": "gz", "gz": "gy"}
+FILL = {"gx": "gy", "gy": "gy", "gz": "gy"}
 TILE = 16
 VMEM = pl.BlockSpec(memory_space=pltpu.VMEM)
 HBM = pl.BlockSpec(memory_space=pltpu.HBM)
@@ -35,10 +35,17 @@
     return dict(position, **{axis: j}) if first <= min(i, j) and max(i, j) < lax.axis_size(axis) else None
 
 
+def filler(position, axis):
+    if FILL[axis] == axis:
+        other = lax.axis_size(axis) - 1 - position[axis]
+        return dict(position, **{axis: other}) if lax.axis_size(axis) % 2 == 0 else None
+    return swapped(position, FILL[axis], 0)
+
+
 def exchange(face, axis, first):
     pairs = []
     for position in devices():
-        partner = swapped(position, axis, first) or swapped(position, FILL[axis], 0)
+        partner = swapped(position, axis, first) or filler(position, axis)
         if partner is not None:
             pairs.append((device(position), device(partner)))
     return lax.ppermute(face, AXES, pairs)

time: 64.7 us -> 69.7 us (1.077)
  waiting for transfers between devices: 21.2 us -> 32.9 us
  starting transfers between devices: 32.8 us -> 26.2 us
    ppermute x30, waiting for transfers between devices: 21.2 us -> 32.9 us  [exchange(): return lax.ppermute(face, AXES, pairs)]
    ppermute x30, starting transfers between devices: 32.8 us -> 26.2 us  [exchange(): return lax.ppermute(face, AXES, pairs)]
  transfers between devices with their start and end apart: 30 -> 30, of which waited for: 13 -> 17; matrix products, arithmetic and copies ran while one was open for 0% -> 0% of each run, Pallas kernels for 0% -> 0%
where the time goes in v3:
time: 69.7 us; the launch traced here: 68.8 us
  waiting for transfers between devices  32.9 us (47%)
  starting transfers between devices  26.2 us (38%)
  Pallas kernels  9.57 us (14%)
    ppermute x30, waiting for transfers between devices, exchange(): return lax.ppermute(face, AXES, pairs)  32.9 us
    ppermute x30, starting transfers between devices, exchange(): return lax.ppermute(face, AXES, pairs)  26.2 us
    pallas_call x5, Pallas kernels, body(): pl.pallas_call(functools.partial(step_kernel, step, counts), out_shape=[f...  5.49 us
    pallas_call x1, Pallas kernels, body(): pl.pallas_call(first_kernel, out_shape=[face] * 3 + [like(operator), like...  3.17 us
  transfers between devices with their start and end apart: 30, of which 17 were waited for; matrix products, arithmetic and copies ran while one was open for 0% of the time, Pallas kernels for 0%

profile of v3, /device:TPU:1, one launch (start us, length us, event | category | flops | bytes accessed | tf_op | source)
XLA Modules:
  0.0 68.8 jit_solution(17581596426586944574)
XLA Ops:
  0.0 3.2 %first.1 = (bf16[384,256]{1,0:T(8,128)(2,1)S(1)}, bf16[384,256]{1,0:T(8,128)(2,1)S(1)}, bf16[384,256]{1,0:T(8,128)(2,1)S(1)}, bf16[1152,1152]{1,0:T(8,128)(2,1)S...) custom-call(bf16[1152,1152]{1,0:T(8,128)(2,1)} %bitcast.5, ...), custom_call_target="tpu_custom_call" | custom-call | tf_op jit(solution)/shard_map/first/pallas_call | solution.py:158
  3.2 2.1 %collective-permute-start.4 = (bf16[384,256]{1,0:T(8,128)(2,1)S(1)}, bf16[384,256]{1,0:T(8,128)(2,1)S(1)}, u32[]{:S(2)}, u32[]{:S(2)}) collective-permute-start(bf16[384,256]{1,0:T(8,128)(2,1)S(1)} %get-tuple-element.35), channel_id=1, source_target_pairs={{0,1},{1,0},{2,3},{3,2},{4,5},{5,4},{6,7},{7,6},{8,9},{9,8},{10,11... | collective-permute-start | bytes 589832 | tf_op jit(solution)/shard_map/ppermute | solution.py:51
  6.2 1.6 %collective-permute-start = (bf16[384,256]{1,0:T(8,128)(2,1)S(1)}, bf16[384,256]{1,0:T(8,128)(2,1)S(1)}, u32[]{:S(2)}, u32[]{:S(2)}) collective-permute-start(bf16[384,256]{1,0:T(8,128)(2,1)S(1)} %get-tuple-element.33), channel_id=1, source_target_pairs={{0,8},{1,9},{2,10},{3,11},{4,12},{5,13},{6,14},{7,15},{8,0},{9,1},... | collective-permute-start | bytes 589832 | tf_op jit(solution)/shard_map/ppermute | solution.py:51
  7.9 2.6 %collective-permute-start.3 = (bf16[384,256]{1,0:T(8,128)(2,1)S(1)}, bf16[384,256]{1,0:T(8,128)(2,1)S(1)}, u32[]{:S(2)}, u32[]{:S(2)}) collective-permute-start(bf16[384,256]{1,0:T(8,128)(2,1)S(1)} %get-tuple-element.34), channel_id=1, source_target_pairs={{0,6},{1,7},{2,4},{3,5},{4,2},{5,3},{6,0},{7,1},{8,14},{9,15},{10,... | collective-permute-start | bytes 589832 | tf_op jit(solution)/shard_map/ppermute | solution.py:51
  10.5 1.4 %collective-permute-done.refs_0_ = bf16[384,256]{1,0:T(8,128)(2,1)S(1)} collective-permute-done((bf16[384,256]{1,0:T(8,128)(2,1)S(1)}, bf16[384,256]{1,0:T(8,128)(2,1)S(1)}, u32[]{:S(2)}, u32[]{:S(2)}) %collective-permute-start) | collective-permute-done | bytes 196640 | tf_op jit(solution)/shard_map/ppermute | solution.py:51
  11.9 4.2 %collective-permute-done.3.refs_3_ = bf16[384,256]{1,0:T(8,128)(2,1)S(1)} collective-permute-done((bf16[384,256]{1,0:T(8,128)(2,1)S(1)}, bf16[384,256]{1,0:T(8,128)(2,1)S(1)}, u32[]{:S(2)}, u32[]{:S(2)}) %collective-permute-start.3) | collective-permute-done | bytes 196640 | tf_op jit(solution)/shard_map/ppermute | solution.py:51
  16.1 1.1 %step1.1 = (bf16[384,256]{1,0:T(8,128)(2,1)S(1)}, bf16[384,256]{1,0:T(8,128)(2,1)S(1)}, bf16[384,256]{1,0:T(8,128)(2,1)S(1)}) custom-call(bf16[1152,1152]{1,0:T(8,128)(2,1)S(1)} %get-tuple-element.29.operator, bf16[1152,128]{1,0:T(8,128)(2,1)S(1)} %get-tuple-element.30.lift, bf16[128,256]{1,0:T(8,128)(2,1)S(1)} %get-tuple-element.31.source, ...), custom_call_target="tpu_custom_call" | custom-call | tf_op jit(solution)/shard_map/step1/pallas_call | solution.py:174
  18.3 2.2 %collective-permute-start.8 = (bf16[384,256]{1,0:T(8,128)(2,1)S(1)}, bf16[384,256]{1,0:T(8,128)(2,1)S(1)}, u32[]{:S(2)}, u32[]{:S(2)}) collective-permute-start(bf16[384,256]{1,0:T(8,128)(2,1)S(1)} %get-tuple-element.37), channel_id=1, source_target_pairs={{0,6},{1,7},{2,4},{3,5},{4,2},{5,3},{6,0},{7,1},{8,14},{9,15},{10,... | collective-permute-start | bytes 589832 | tf_op jit(solution)/shard_map/ppermute | solution.py:51
  20.6 2.8 %collective-permute-done.9.refs_4_ = bf16[384,256]{1,0:T(8,128)(2,1)S(1)} collective-permute-done((bf16[384,256]{1,0:T(8,128)(2,1)S(1)}, bf16[384,256]{1,0:T(8,128)(2,1)S(1)}, u32[]{:S(2)}, u32[]{:S(2)}) %collective-permute-start.9) | collective-permute-done | bytes 196640 | tf_op jit(solution)/shard_map/ppermute | solution.py:51
  23.4 1.3 %collective-permute-done.5.refs_0_ = bf16[384,256]{1,0:T(8,128)(2,1)S(1)} collective-permute-done((bf16[384,256]{1,0:T(8,128)(2,1)S(1)}, bf16[384,256]{1,0:T(8,128)(2,1)S(1)}, u32[]{:S(2)}, u32[]{:S(2)}) %collective-permute-start.5) | collective-permute-done | bytes 196640 | tf_op jit(solution)/shard_map/ppermute | solution.py:51
  24.7 1.5 %collective-permute-done.8.refs_3_ = bf16[384,256]{1,0:T(8,128)(2,1)S(1)} collective-permute-done((bf16[384,256]{1,0:T(8,128)(2,1)S(1)}, bf16[384,256]{1,0:T(8,128)(2,1)S(1)}, u32[]{:S(2)}, u32[]{:S(2)}) %collective-permute-start.8) | collective-permute-done | bytes 196640 | tf_op jit(solution)/shard_map/ppermute | solution.py:51
  27.3 1.3 %collective-permute-start.14 = (bf16[384,256]{1,0:T(8,128)(2,1)S(1)}, bf16[384,256]{1,0:T(8,128)(2,1)S(1)}, u32[]{:S(2)}, u32[]{:S(2)}) collective-permute-start(bf16[384,256]{1,0:T(8,128)(2,1)S(1)} %get-tuple-element.41), channel_id=1, source_target_pairs={{0,1},{1,0},{2,3},{3,2},{4,5},{5,4},{6,7},{7,6},{8,9},{9,8},{10,11... | collective-permute-start | bytes 589832 | tf_op jit(solution)/shard_map/ppermute | solution.py:51
  29.3 1.9 %collective-permute-start.13 = (bf16[384,256]{1,0:T(8,128)(2,1)S(1)}, bf16[384,256]{1,0:T(8,128)(2,1)S(1)}, u32[]{:S(2)}, u32[]{:S(2)}) collective-permute-start(bf16[384,256]{1,0:T(8,128)(2,1)S(1)} %get-tuple-element.40), channel_id=1, source_target_pairs={{0,6},{1,7},{2,4},{3,5},{4,2},{5,3},{6,0},{7,1},{8,14},{9,15},{10,... | collective-permute-start | bytes 589832 | tf_op jit(solution)/shard_map/ppermute | solution.py:51
  31.1 2.3 %collective-permute-done.14.refs_4_ = bf16[384,256]{1,0:T(8,128)(2,1)S(1)} collective-permute-done((bf16[384,256]{1,0:T(8,128)(2,1)S(1)}, bf16[384,256]{1,0:T(8,128)(2,1)S(1)}, u32[]{:S(2)}, u32[]{:S(2)}) %collective-permute-start.14) | collective-permute-done | bytes 196640 | tf_op jit(solution)/shard_map/ppermute | solution.py:51
  33.4 2.3 %collective-permute-done.10.refs_0_ = bf16[384,256]{1,0:T(8,128)(2,1)S(1)} collective-permute-done((bf16[384,256]{1,0:T(8,128)(2,1)S(1)}, bf16[384,256]{1,0:T(8,128)(2,1)S(1)}, u32[]{:S(2)}, u32[]{:S(2)}) %collective-permute-start.10) | collective-permute-done | bytes 196640 | tf_op jit(solution)/shard_map/ppermute | solution.py:51
  35.7 1.1 %collective-permute-done.13.refs_3_ = bf16[384,256]{1,0:T(8,128)(2,1)S(1)} collective-permute-done((bf16[384,256]{1,0:T(8,128)(2,1)S(1)}, bf16[384,256]{1,0:T(8,128)(2,1)S(1)}, u32[]{:S(2)}, u32[]{:S(2)}) %collective-permute-start.13) | collective-permute-done | bytes 196640 | tf_op jit(solution)/shard_map/ppermute | solution.py:51
  36.8 1.1 %step3.1 = (bf16[384,256]{1,0:T(8,128)(2,1)S(1)}, bf16[384,256]{1,0:T(8,128)(2,1)S(1)}, bf16[384,256]{1,0:T(8,128)(2,1)S(1)}) custom-call(bf16[1152,1152]{1,0:T(8,128)(2,1)S(1)} %get-tuple-element.29.operator, bf16[1152,128]{1,0:T(8,128)(2,1)S(1)} %get-tuple-element.30.lift, bf16[128,256]{1,0:T(8,128)(2,1)S(1)} %get-tuple-element.31.source, ...), custom_call_target="tpu_custom_call" | custom-call | tf_op jit(solution)/shard_map/step3/pallas_call | solution.py:174
  39.1 1.7 %collective-permute-start.18 = (bf16[384,256]{1,0:T(8,128)(2,1)S(1)}, bf16[384,256]{1,0:T(8,128)(2,1)S(1)}, u32[]{:S(2)}, u32[]{:S(2)}) collective-permute-start(bf16[384,256]{1,0:T(8,128)(2,1)S(1)} %get-tuple-element.43), channel_id=1, source_target_pairs={{0,6},{1,7},{2,4},{3,5},{4,2},{5,3},{6,0},{7,1},{8,14},{9,15},{10,... | collective-permute-start | bytes 589832 | tf_op jit(solution)/shard_map/ppermute | solution.py:51
  40.8 3.2 %collective-permute-done.19.refs_4_ = bf16[384,256]{1,0:T(8,128)(2,1)S(1)} collective-permute-done((bf16[384,256]{1,0:T(8,128)(2,1)S(1)}, bf16[384,256]{1,0:T(8,128)(2,1)S(1)}, u32[]{:S(2)}, u32[]{:S(2)}) %collective-permute-start.19) | collective-permute-done | bytes 196640 | tf_op jit(solution)/shard_map/ppermute | solution.py:51
  44.0 1.4 %collective-permute-done.15.refs_0_ = bf16[384,256]{1,0:T(8,128)(2,1)S(1)} collective-permute-done((bf16[384,256]{1,0:T(8,128)(2,1)S(1)}, bf16[384,256]{1,0:T(8,128)(2,1)S(1)}, u32[]{:S(2)}, u32[]{:S(2)}) %collective-permute-start.15) | collective-permute-done | bytes 196640 | tf_op jit(solution)/shard_map/ppermute | solution.py:51
  46.2 1.1 %step4.1 = (bf16[384,256]{1,0:T(8,128)(2,1)S(1)}, bf16[384,256]{1,0:T(8,128)(2,1)S(1)}, bf16[384,256]{1,0:T(8,128)(2,1)S(1)}) custom-call(bf16[1152,1152]{1,0:T(8,128)(2,1)S(1)} %get-tuple-element.29.operator, bf16[1152,128]{1,0:T(8,128)(2,1)S(1)} %get-tuple-element.30.lift, bf16[128,256]{1,0:T(8,128)(2,1)S(1)} %get-tuple-element.31.source, ...), custom_call_target="tpu_custom_call" | custom-call | tf_op jit(solution)/shard_map/step4/pallas_call | solution.py:174
  47.3 1.3 %collective-permute-start.24 = (bf16[384,256]{1,0:T(8,128)(2,1)S(1)}, bf16[384,256]{1,0:T(8,128)(2,1)S(1)}, u32[]{:S(2)}, u32[]{:S(2)}) collective-permute-start(bf16[384,256]{1,0:T(8,128)(2,1)S(1)} %get-tuple-element.47), channel_id=1, source_target_pairs={{0,1},{1,0},{2,3},{3,2},{4,5},{5,4},{6,7},{7,6},{8,9},{9,8},{10,11... | collective-permute-start | bytes 589832 | tf_op jit(solution)/shard_map/ppermute | solution.py:51
  48.6 1.1 %collective-permute-start.21 = (bf16[384,256]{1,0:T(8,128)(2,1)S(1)}, bf16[384,256]{1,0:T(8,128)(2,1)S(1)}, u32[]{:S(2)}, u32[]{:S(2)}) collective-permute-start(bf16[384,256]{1,0:T(8,128)(2,1)S(1)} %get-tuple-element.45), channel_id=1, source_target_pairs={{0,2},{1,3},{2,0},{3,1},{4,6},{5,7},{6,4},{7,5},{8,16},{9,17},{10,... | collective-permute-start | bytes 589832 | tf_op jit(solution)/shard_map/ppermute | solution.py:51
  50.6 1.7 %collective-permute-start.23 = (bf16[384,256]{1,0:T(8,128)(2,1)S(1)}, bf16[384,256]{1,0:T(8,128)(2,1)S(1)}, u32[]{:S(2)}, u32[]{:S(2)}) collective-permute-start(bf16[384,256]{1,0:T(8,128)(2,1)S(1)} %get-tuple-element.46), channel_id=1, source_target_pairs={{0,6},{1,7},{2,4},{3,5},{4,2},{5,3},{6,0},{7,1},{8,14},{9,15},{10,... | collective-permute-start | bytes 589832 | tf_op jit(solution)/shard_map/ppermute | solution.py:51
  53.0 3.1 %collective-permute-done.20.refs_0_ = bf16[384,256]{1,0:T(8,128)(2,1)S(1)} collective-permute-done((bf16[384,256]{1,0:T(8,128)(2,1)S(1)}, bf16[384,256]{1,0:T(8,128)(2,1)S(1)}, u32[]{:S(2)}, u32[]{:S(2)}) %collective-permute-start.20) | collective-permute-done | bytes 196640 | tf_op jit(solution)/shard_map/ppermute | solution.py:51
  56.1 1.5 %collective-permute-done.23.refs_3_ = bf16[384,256]{1,0:T(8,128)(2,1)S(1)} collective-permute-done((bf16[384,256]{1,0:T(8,128)(2,1)S(1)}, bf16[384,256]{1,0:T(8,128)(2,1)S(1)}, u32[]{:S(2)}, u32[]{:S(2)}) %collective-permute-start.23) | collective-permute-done | bytes 196640 | tf_op jit(solution)/shard_map/ppermute | solution.py:51
  57.6 1.1 %step5.1 = (bf16[384,256]{1,0:T(8,128)(2,1)S(1)}, bf16[384,256]{1,0:T(8,128)(2,1)S(1)}, bf16[384,256]{1,0:T(8,128)(2,1)S(1)}) custom-call(bf16[1152,1152]{1,0:T(8,128)(2,1)S(1)} %get-tuple-element.29.operator, bf16[1152,128]{1,0:T(8,128)(2,1)S(1)} %get-tuple-element.30.lift, bf16[128,256]{1,0:T(8,128)(2,1)S(1)} %get-tuple-element.31.source, ...), custom_call_target="tpu_custom_call" | custom-call | tf_op jit(solution)/shard_map/step5/pallas_call | solution.py:174
  59.1 1.1 %collective-permute-start.26 = (bf16[384,256]{1,0:T(8,128)(2,1)S(1)}, bf16[384,256]{1,0:T(8,128)(2,1)S(1)}, u32[]{:S(2)}, u32[]{:S(2)}) collective-permute-start(bf16[384,256]{1,0:T(8,128)(2,1)S(1)} %get-tuple-element.48), channel_id=1, source_target_pairs={{0,2},{1,3},{2,0},{3,1},{4,6},{5,7},{6,4},{7,5},{8,16},{9,17},{10,... | collective-permute-start | bytes 589832 | tf_op jit(solution)/shard_map/ppermute | solution.py:51
  60.8 1.7 %collective-permute-start.28 = (bf16[384,256]{1,0:T(8,128)(2,1)S(1)}, bf16[384,256]{1,0:T(8,128)(2,1)S(1)}, u32[]{:S(2)}, u32[]{:S(2)}) collective-permute-start(bf16[384,256]{1,0:T(8,128)(2,1)S(1)} %get-tuple-element.49), channel_id=1, source_target_pairs={{0,6},{1,7},{2,4},{3,5},{4,2},{5,3},{6,0},{7,1},{8,14},{9,15},{10,... | collective-permute-start | bytes 589832 | tf_op jit(solution)/shard_map/ppermute | solution.py:51
  62.5 1.9 %collective-permute-done.29.refs_4_ = bf16[384,256]{1,0:T(8,128)(2,1)S(1)} collective-permute-done((bf16[384,256]{1,0:T(8,128)(2,1)S(1)}, bf16[384,256]{1,0:T(8,128)(2,1)S(1)}, u32[]{:S(2)}, u32[]{:S(2)}) %collective-permute-start.29) | collective-permute-done | bytes 196640 | tf_op jit(solution)/shard_map/ppermute | solution.py:51
  64.4 2.2 %collective-permute-done.25.refs_0_ = bf16[384,256]{1,0:T(8,128)(2,1)S(1)} collective-permute-done((bf16[384,256]{1,0:T(8,128)(2,1)S(1)}, bf16[384,256]{1,0:T(8,128)(2,1)S(1)}, u32[]{:S(2)}, u32[]{:S(2)}) %collective-permute-start.25) | collective-permute-done | bytes 196640 | tf_op jit(solution)/shard_map/ppermute | solution.py:51
  66.6 1.2 %collective-permute-done.28.refs_3_ = bf16[384,256]{1,0:T(8,128)(2,1)S(1)} collective-permute-done((bf16[384,256]{1,0:T(8,128)(2,1)S(1)}, bf16[384,256]{1,0:T(8,128)(2,1)S(1)}, u32[]{:S(2)}, u32[]{:S(2)}) %collective-permute-start.28) | collective-permute-done | bytes 196640 | tf_op jit(solution)/shard_map/ppermute | solution.py:51
  (35 shorter events, 9.2 us)
Async XLA Ops:
  3.2 7.3 %collective-permute-start.4 = (bf16[384,256]{1,0:T(8,128)(2,1)S(1)}, bf16[384,256]{1,0:T(8,128)(2,1)S(1)}, u32[]{:S(2)}, u32[]{:S(2)}) collective-permute-start(bf16[384,256]{1,0:T(8,128)(2,1)S(1)} %get-tuple-element.35), channel_id=1, source_target_pairs={{0,1},{1,0},{2,3},{3,2},{4,5},{5,4},{6,7},{7,6},{8,9},{9,8},{10,11... | collective-permute-start | bytes 589832 | tf_op jit(solution)/shard_map/ppermute | solution.py:51
  5.3 5.2 %collective-permute-start.1 = (bf16[384,256]{1,0:T(8,128)(2,1)S(1)}, bf16[384,256]{1,0:T(8,128)(2,1)S(1)}, u32[]{:S(2)}, u32[]{:S(2)}) collective-permute-start(bf16[384,256]{1,0:T(8,128)(2,1)S(1)} %get-tuple-element.33), channel_id=1, source_target_pairs={{0,2},{1,3},{2,0},{3,1},{4,6},{5,7},{6,4},{7,5},{8,16},{9,17},{10,... | collective-permute-start | bytes 589832 | tf_op jit(solution)/shard_map/ppermute | solution.py:51
  6.2 5.7 %collective-permute-start = (bf16[384,256]{1,0:T(8,128)(2,1)S(1)}, bf16[384,256]{1,0:T(8,128)(2,1)S(1)}, u32[]{:S(2)}, u32[]{:S(2)}) collective-permute-start(bf16[384,256]{1,0:T(8,128)(2,1)S(1)} %get-tuple-element.33), channel_id=1, source_target_pairs={{0,8},{1,9},{2,10},{3,11},{4,12},{5,13},{6,14},{7,15},{8,0},{9,1},... | collective-permute-start | bytes 589832 | tf_op jit(solution)/shard_map/ppermute | solution.py:51
  7.9 8.2 %collective-permute-start.3 = (bf16[384,256]{1,0:T(8,128)(2,1)S(1)}, bf16[384,256]{1,0:T(8,128)(2,1)S(1)}, u32[]{:S(2)}, u32[]{:S(2)}) collective-permute-start(bf16[384,256]{1,0:T(8,128)(2,1)S(1)} %get-tuple-element.34), channel_id=1, source_target_pairs={{0,6},{1,7},{2,4},{3,5},{4,2},{5,3},{6,0},{7,1},{8,14},{9,15},{10,... | collective-permute-start | bytes 589832 | tf_op jit(solution)/shard_map/ppermute | solution.py:51
  10.5 5.6 %collective-permute-start.2 = (bf16[384,256]{1,0:T(8,128)(2,1)S(1)}, bf16[384,256]{1,0:T(8,128)(2,1)S(1)}, u32[]{:S(2)}, u32[]{:S(2)}) collective-permute-start(bf16[384,256]{1,0:T(8,128)(2,1)S(1)} %get-tuple-element.34), channel_id=1, source_target_pairs={{0,2},{1,3},{2,0},{3,1},{4,6},{5,7},{6,4},{7,5},{8,10},{9,11},{10,... | collective-permute-start | bytes 589832 | tf_op jit(solution)/shard_map/ppermute | solution.py:51
  17.2 6.1 %collective-permute-start.9 = (bf16[384,256]{1,0:T(8,128)(2,1)S(1)}, bf16[384,256]{1,0:T(8,128)(2,1)S(1)}, u32[]{:S(2)}, u32[]{:S(2)}) collective-permute-start(bf16[384,256]{1,0:T(8,128)(2,1)S(1)} %get-tuple-element.38), channel_id=1, source_target_pairs={{0,1},{1,0},{2,3},{3,2},{4,5},{5,4},{6,7},{7,6},{8,9},{9,8},{10,11... | collective-permute-start | bytes 589832 | tf_op jit(solution)/shard_map/ppermute | solution.py:51
  17.5 5.8 %collective-permute-start.6 = (bf16[384,256]{1,0:T(8,128)(2,1)S(1)}, bf16[384,256]{1,0:T(8,128)(2,1)S(1)}, u32[]{:S(2)}, u32[]{:S(2)}) collective-permute-start(bf16[384,256]{1,0:T(8,128)(2,1)S(1)} %get-tuple-element.36), channel_id=1, source_target_pairs={{0,2},{1,3},{2,0},{3,1},{4,6},{5,7},{6,4},{7,5},{8,16},{9,17},{10,... | collective-permute-start | bytes 589832 | tf_op jit(solution)/shard_map/ppermute | solution.py:51
  18.2 6.5 %collective-permute-start.5 = (bf16[384,256]{1,0:T(8,128)(2,1)S(1)}, bf16[384,256]{1,0:T(8,128)(2,1)S(1)}, u32[]{:S(2)}, u32[]{:S(2)}) collective-permute-start(bf16[384,256]{1,0:T(8,128)(2,1)S(1)} %get-tuple-element.36), channel_id=1, source_target_pairs={{0,8},{1,9},{2,10},{3,11},{4,12},{5,13},{6,14},{7,15},{8,0},{9,1},... | collective-permute-start | bytes 589832 | tf_op jit(solution)/shard_map/ppermute | solution.py:51
  18.3 7.8 %collective-permute-start.8 = (bf16[384,256]{1,0:T(8,128)(2,1)S(1)}, bf16[384,256]{1,0:T(8,128)(2,1)S(1)}, u32[]{:S(2)}, u32[]{:S(2)}) collective-permute-start(bf16[384,256]{1,0:T(8,128)(2,1)S(1)} %get-tuple-element.37), channel_id=1, source_target_pairs={{0,6},{1,7},{2,4},{3,5},{4,2},{5,3},{6,0},{7,1},{8,14},{9,15},{10,... | collective-permute-start | bytes 589832 | tf_op jit(solution)/shard_map/ppermute | solution.py:51
  20.6 5.6 %collective-permute-start.7 = (bf16[384,256]{1,0:T(8,128)(2,1)S(1)}, bf16[384,256]{1,0:T(8,128)(2,1)S(1)}, u32[]{:S(2)}, u32[]{:S(2)}) collective-permute-start(bf16[384,256]{1,0:T(8,128)(2,1)S(1)} %get-tuple-element.37), channel_id=1, source_target_pairs={{0,2},{1,3},{2,0},{3,1},{4,6},{5,7},{6,4},{7,5},{8,10},{9,11},{10,... | collective-permute-start | bytes 589832 | tf_op jit(solution)/shard_map/ppermute | solution.py:51
  27.3 6.1 %collective-permute-start.14 = (bf16[384,256]{1,0:T(8,128)(2,1)S(1)}, bf16[384,256]{1,0:T(8,128)(2,1)S(1)}, u32[]{:S(2)}, u32[]{:S(2)}) collective-permute-start(bf16[384,256]{1,0:T(8,128)(2,1)S(1)} %get-tuple-element.41), channel_id=1, source_target_pairs={{0,1},{1,0},{2,3},{3,2},{4,5},{5,4},{6,7},{7,6},{8,9},{9,8},{10,11... | collective-permute-start | bytes 589832 | tf_op jit(solution)/shard_map/ppermute | solution.py:51
  28.6 4.9 %collective-permute-start.11 = (bf16[384,256]{1,0:T(8,128)(2,1)S(1)}, bf16[384,256]{1,0:T(8,128)(2,1)S(1)}, u32[]{:S(2)}, u32[]{:S(2)}) collective-permute-start(bf16[384,256]{1,0:T(8,128)(2,1)S(1)} %get-tuple-element.39), channel_id=1, source_target_pairs={{0,2},{1,3},{2,0},{3,1},{4,6},{5,7},{6,4},{7,5},{8,16},{9,17},{10,... | collective-permute-start | bytes 589832 | tf_op jit(solution)/shard_map/ppermute | solution.py:51
  29.3 6.5 %collective-permute-start.10 = (bf16[384,256]{1,0:T(8,128)(2,1)S(1)}, bf16[384,256]{1,0:T(8,128)(2,1)S(1)}, u32[]{:S(2)}, u32[]{:S(2)}) collective-permute-start(bf16[384,256]{1,0:T(8,128)(2,1)S(1)} %get-tuple-element.39), channel_id=1, source_target_pairs={{0,8},{1,9},{2,10},{3,11},{4,12},{5,13},{6,14},{7,15},{8,0},{9,1},... | collective-permute-start | bytes 589832 | tf_op jit(solution)/shard_map/ppermute | solution.py:51
  29.3 7.6 %collective-permute-start.13 = (bf16[384,256]{1,0:T(8,128)(2,1)S(1)}, bf16[384,256]{1,0:T(8,128)(2,1)S(1)}, u32[]{:S(2)}, u32[]{:S(2)}) collective-permute-start(bf16[384,256]{1,0:T(8,128)(2,1)S(1)} %get-tuple-element.40), channel_id=1, source_target_pairs={{0,6},{1,7},{2,4},{3,5},{4,2},{5,3},{6,0},{7,1},{8,14},{9,15},{10,... | collective-permute-start | bytes 589832 | tf_op jit(solution)/shard_map/ppermute | solution.py:51
  31.1 5.7 %collective-permute-start.12 = (bf16[384,256]{1,0:T(8,128)(2,1)S(1)}, bf16[384,256]{1,0:T(8,128)(2,1)S(1)}, u32[]{:S(2)}, u32[]{:S(2)}) collective-permute-start(bf16[384,256]{1,0:T(8,128)(2,1)S(1)} %get-tuple-element.40), channel_id=1, source_target_pairs={{0,2},{1,3},{2,0},{3,1},{4,6},{5,7},{6,4},{7,5},{8,10},{9,11},{10,... | collective-permute-start | bytes 589832 | tf_op jit(solution)/shard_map/ppermute | solution.py:51
  37.9 6.1 %collective-permute-start.19 = (bf16[384,256]{1,0:T(8,128)(2,1)S(1)}, bf16[384,256]{1,0:T(8,128)(2,1)S(1)}, u32[]{:S(2)}, u32[]{:S(2)}) collective-permute-start(bf16[384,256]{1,0:T(8,128)(2,1)S(1)} %get-tuple-element.44), channel_id=1, source_target_pairs={{0,1},{1,0},{2,3},{3,2},{4,5},{5,4},{6,7},{7,6},{8,9},{9,8},{10,11... | collective-permute-start | bytes 589832 | tf_op jit(solution)/shard_map/ppermute | solution.py:51
  38.3 5.8 %collective-permute-start.16 = (bf16[384,256]{1,0:T(8,128)(2,1)S(1)}, bf16[384,256]{1,0:T(8,128)(2,1)S(1)}, u32[]{:S(2)}, u32[]{:S(2)}) collective-permute-start(bf16[384,256]{1,0:T(8,128)(2,1)S(1)} %get-tuple-element.42), channel_id=1, source_target_pairs={{0,2},{1,3},{2,0},{3,1},{4,6},{5,7},{6,4},{7,5},{8,16},{9,17},{10,... | collective-permute-start | bytes 589832 | tf_op jit(solution)/shard_map/ppermute | solution.py:51
  39.0 6.5 %collective-permute-start.15 = (bf16[384,256]{1,0:T(8,128)(2,1)S(1)}, bf16[384,256]{1,0:T(8,128)(2,1)S(1)}, u32[]{:S(2)}, u32[]{:S(2)}) collective-permute-start(bf16[384,256]{1,0:T(8,128)(2,1)S(1)} %get-tuple-element.42), channel_id=1, source_target_pairs={{0,8},{1,9},{2,10},{3,11},{4,12},{5,13},{6,14},{7,15},{8,0},{9,1},... | collective-permute-start | bytes 589832 | tf_op jit(solution)/shard_map/ppermute | solution.py:51
  39.1 7.1 %collective-permute-start.18 = (bf16[384,256]{1,0:T(8,128)(2,1)S(1)}, bf16[384,256]{1,0:T(8,128)(2,1)S(1)}, u32[]{:S(2)}, u32[]{:S(2)}) collective-permute-start(bf16[384,256]{1,0:T(8,128)(2,1)S(1)} %get-tuple-element.43), channel_id=1, source_target_pairs={{0,6},{1,7},{2,4},{3,5},{4,2},{5,3},{6,0},{7,1},{8,14},{9,15},{10,... | collective-permute-start | bytes 589832 | tf_op jit(solution)/shard_map/ppermute | solution.py:51
  40.8 5.4 %collective-permute-start.17 = (bf16[384,256]{1,0:T(8,128)(2,1)S(1)}, bf16[384,256]{1,0:T(8,128)(2,1)S(1)}, u32[]{:S(2)}, u32[]{:S(2)}) collective-permute-start(bf16[384,256]{1,0:T(8,128)(2,1)S(1)} %get-tuple-element.43), channel_id=1, source_target_pairs={{0,2},{1,3},{2,0},{3,1},{4,6},{5,7},{6,4},{7,5},{8,10},{9,11},{10,... | collective-permute-start | bytes 589832 | tf_op jit(solution)/shard_map/ppermute | solution.py:51
  47.3 5.7 %collective-permute-start.24 = (bf16[384,256]{1,0:T(8,128)(2,1)S(1)}, bf16[384,256]{1,0:T(8,128)(2,1)S(1)}, u32[]{:S(2)}, u32[]{:S(2)}) collective-permute-start(bf16[384,256]{1,0:T(8,128)(2,1)S(1)} %get-tuple-element.47), channel_id=1, source_target_pairs={{0,1},{1,0},{2,3},{3,2},{4,5},{5,4},{6,7},{7,6},{8,9},{9,8},{10,11... | collective-permute-start | bytes 589832 | tf_op jit(solution)/shard_map/ppermute | solution.py:51
  48.6 4.4 %collective-permute-start.21 = (bf16[384,256]{1,0:T(8,128)(2,1)S(1)}, bf16[384,256]{1,0:T(8,128)(2,1)S(1)}, u32[]{:S(2)}, u32[]{:S(2)}) collective-permute-start(bf16[384,256]{1,0:T(8,128)(2,1)S(1)} %get-tuple-element.45), channel_id=1, source_target_pairs={{0,2},{1,3},{2,0},{3,1},{4,6},{5,7},{6,4},{7,5},{8,16},{9,17},{10,... | collective-permute-start | bytes 589832 | tf_op jit(solution)/shard_map/ppermute | solution.py:51
  49.7 6.5 %collective-permute-start.20 = (bf16[384,256]{1,0:T(8,128)(2,1)S(1)}, bf16[384,256]{1,0:T(8,128)(2,1)S(1)}, u32[]{:S(2)}, u32[]{:S(2)}) collective-permute-start(bf16[384,256]{1,0:T(8,128)(2,1)S(1)} %get-tuple-element.45), channel_id=1, source_target_pairs={{0,8},{1,9},{2,10},{3,11},{4,12},{5,13},{6,14},{7,15},{8,0},{9,1},... | collective-permute-start | bytes 589832 | tf_op jit(solution)/shard_map/ppermute | solution.py:51
  50.6 7.1 %collective-permute-start.23 = (bf16[384,256]{1,0:T(8,128)(2,1)S(1)}, bf16[384,256]{1,0:T(8,128)(2,1)S(1)}, u32[]{:S(2)}, u32[]{:S(2)}) collective-permute-start(bf16[384,256]{1,0:T(8,128)(2,1)S(1)} %get-tuple-element.46), channel_id=1, source_target_pairs={{0,6},{1,7},{2,4},{3,5},{4,2},{5,3},{6,0},{7,1},{8,14},{9,15},{10,... | collective-permute-start | bytes 589832 | tf_op jit(solution)/shard_map/ppermute | solution.py:51
  52.3 5.3 %collective-permute-start.22 = (bf16[384,256]{1,0:T(8,128)(2,1)S(1)}, bf16[384,256]{1,0:T(8,128)(2,1)S(1)}, u32[]{:S(2)}, u32[]{:S(2)}) collective-permute-start(bf16[384,256]{1,0:T(8,128)(2,1)S(1)} %get-tuple-element.46), channel_id=1, source_target_pairs={{0,2},{1,3},{2,0},{3,1},{4,6},{5,7},{6,4},{7,5},{8,10},{9,11},{10,... | collective-permute-start | bytes 589832 | tf_op jit(solution)/shard_map/ppermute | solution.py:51
  58.7 5.7 %collective-permute-start.29 = (bf16[384,256]{1,0:T(8,128)(2,1)S(1)}, bf16[384,256]{1,0:T(8,128)(2,1)S(1)}, u32[]{:S(2)}, u32[]{:S(2)}) collective-permute-start(bf16[384,256]{1,0:T(8,128)(2,1)S(1)} %get-tuple-element.50), channel_id=1, source_target_pairs={{0,1},{1,0},{2,3},{3,2},{4,5},{5,4},{6,7},{7,6},{8,9},{9,8},{10,11... | collective-permute-start | bytes 589832 | tf_op jit(solution)/shard_map/ppermute | solution.py:51
  59.1 5.4 %collective-permute-start.26 = (bf16[384,256]{1,0:T(8,128)(2,1)S(1)}, bf16[384,256]{1,0:T(8,128)(2,1)S(1)}, u32[]{:S(2)}, u32[]{:S(2)}) collective-permute-start(bf16[384,256]{1,0:T(8,128)(2,1)S(1)} %get-tuple-element.48), channel_id=1, source_target_pairs={{0,2},{1,3},{2,0},{3,1},{4,6},{5,7},{6,4},{7,5},{8,16},{9,17},{10,... | collective-permute-start | bytes 589832 | tf_op jit(solution)/shard_map/ppermute | solution.py:51
  60.2 6.5 %collective-permute-start.25 = (bf16[384,256]{1,0:T(8,128)(2,1)S(1)}, bf16[384,256]{1,0:T(8,128)(2,1)S(1)}, u32[]{:S(2)}, u32[]{:S(2)}) collective-permute-start(bf16[384,256]{1,0:T(8,128)(2,1)S(1)} %get-tuple-element.48), channel_id=1, source_target_pairs={{0,8},{1,9},{2,10},{3,11},{4,12},{5,13},{6,14},{7,15},{8,0},{9,1},... | collective-permute-start | bytes 589832 | tf_op jit(solution)/shard_map/ppermute | solution.py:51
  60.8 7.1 %collective-permute-start.28 = (bf16[384,256]{1,0:T(8,128)(2,1)S(1)}, bf16[384,256]{1,0:T(8,128)(2,1)S(1)}, u32[]{:S(2)}, u32[]{:S(2)}) collective-permute-start(bf16[384,256]{1,0:T(8,128)(2,1)S(1)} %get-tuple-element.49), channel_id=1, source_target_pairs={{0,6},{1,7},{2,4},{3,5},{4,2},{5,3},{6,0},{7,1},{8,14},{9,15},{10,... | collective-permute-start | bytes 589832 | tf_op jit(solution)/shard_map/ppermute | solution.py:51
  62.5 5.3 %collective-permute-start.27 = (bf16[384,256]{1,0:T(8,128)(2,1)S(1)}, bf16[384,256]{1,0:T(8,128)(2,1)S(1)}, u32[]{:S(2)}, u32[]{:S(2)}) collective-permute-start(bf16[384,256]{1,0:T(8,128)(2,1)S(1)} %get-tuple-element.49), channel_id=1, source_target_pairs={{0,2},{1,3},{2,0},{3,1},{4,6},{5,7},{6,4},{7,5},{8,10},{9,11},{10,... | collective-permute-start | bytes 589832 | tf_op jit(solution)/shard_map/ppermute | solution.py:51

commit v4 on v0

v4 whole, which is shorter than its diff:
```python
import functools

import jax
import jax.numpy as jnp
from jax import lax
from jax.experimental import pallas as pl
from jax.experimental.pallas import tpu as pltpu
from jax.sharding import PartitionSpec as P

STEPS = 6
AXES = ("gx", "gy", "gz")
PAIR = "gy"
ORDER = ("gz", "gx", "gy")
LANES = 128
TILE = 16
VMEM = pl.BlockSpec(memory_space=pltpu.VMEM)
SMEM = pl.BlockSpec(memory_space=pltpu.SMEM)
HBM = pl.BlockSpec(memory_space=pltpu.HBM)


def device(position):
    at = 0
    for axis in AXES:
        at = at * lax.axis_size(axis) + position[axis]
    return at


def devices():
    positions = [{}]
    for axis in AXES:
        positions = [dict(p, **{axis: i}) for p in positions for i in range(lax.axis_size(axis))]
    return positions


def mate(position):
    return dict(position, **{PAIR: position[PAIR] ^ 1})


def onward(position, axis):
    step = (2 if axis == PAIR else 1) * (1 if position[PAIR] % 2 == 0 else -1)
    there = position[axis] + step
    return dict(position, **{axis: there}) if 0 <= there < lax.axis_size(axis) else mate(position)


def permute(value, target):
    return lax.ppermute(value, AXES, [(device(p), device(target(p))) for p in devices()])


def pass_on(payloads):
    pieces = {}
    for axis in ORDER:
        pieces[axis] = permute(payloads[AXES.index(axis)], functools.partial(onward, axis=axis))
    return [pieces[axis] for axis in AXES]


def behind(axis, dtype):
    at = lax.axis_index(axis)
    down = lax.rem(lax.axis_index(PAIR), 2)
    there = at - 1 + 2 * down
    return jnp.where((there >= 0) & (there < lax.axis_size(axis)), 1.0, 0.0).astype(dtype)


def inject(source, wait):
    gate = jnp.concatenate([wait[...]] * (source.shape[1] // LANES), axis=1)
    return jnp.where(gate <= 0, source[...], jnp.zeros_like(source[...]))


def across(a, b):
    return lax.dot_general(a, b, (((1,), (1,)), ((), ())), preferred_element_type=jnp.float32)


def spread(values, origins, out):
    batches = values.shape[0]
    block = out.shape[0] // batches
    for place in range(batches):
        number = values[origins[place]].astype(jnp.float32)
        out[place * block : (place + 1) * block, :] = jnp.full((block, out.shape[1]), number).astype(out.dtype)


def first_kernel(held, *refs):
    operator_h, lift_h, *inputs = refs[:6]
    outgoing, operator, lift, source, wait, direction, sorting, level = refs[6:14]
    stack, raw, raw_source, depth_s, direction_s, origins_s, sems = refs[14:]
    order, width = raw.shape
    rows = order // len(AXES)
    dtype = stack.dtype
    parts = [slice(n * rows, (n + 1) * rows) for n in range(len(AXES))]
    moves = list(zip(inputs[::-1], (direction_s, depth_s, raw, raw_source)))
    for part in parts:
        moves.append((operator_h.at[part, :], operator.at[part, :]))
        moves.append((lift_h.at[part, :], lift.at[part, :]))
    copies = [pltpu.make_async_copy(a, b, sems.at[n]) for n, (a, b) in enumerate(moves)]
    for copy in copies:
        copy.start()
    copies[0].wait()
    copies[1].wait()
    batches = depth_s.shape[0]
    downs = sum(direction_s[b] for b in range(batches))
    most = jnp.maximum(downs, batches - downs)
    level[0] = sum((most > size).astype(jnp.int32) for size in held[:-1])
    seen = [jnp.int32(0), batches - downs]
    for b in range(batches):
        down = direction_s[b]
        origins_s[jnp.where(down == 1, seen[1], seen[0])] = b
        seen = [seen[0] + 1 - down, seen[1] + down]
    spread(depth_s, origins_s, wait)
    spread(direction_s, origins_s, direction)
    block = width // batches
    ahead = lax.broadcasted_iota(jnp.int32, (block, width), 1) - lax.broadcasted_iota(jnp.int32, (block, width), 0)
    for place in range(batches):
        picked = jnp.where(ahead == origins_s[place] * block, 1.0, 0.0)
        sorting[place * block : (place + 1) * block, :] = picked.astype(dtype)
    copies[2].wait()
    stack[:, :order] = across(sorting[...], raw[...]).astype(dtype)
    copies[3].wait()
    source[...] = across(sorting[...], raw_source[...]).astype(dtype)
    stack[:, order:] = inject(source, wait)
    for n, part in enumerate(parts):
        copies[4 + 2 * n].wait()
        copies[5 + 2 * n].wait()
        total = across(stack[:, :order], operator[part, :]) + across(stack[:, order:], lift[part, :])
        outgoing[:, part] = total.astype(dtype)


def store(own, other, payloads, keep):
    height, rows = keep.shape
    for n, axis in enumerate(AXES):
        part = slice(n * rows, (n + 1) * rows)
        if axis == PAIR:
            keep[...] = own[:, part]
            payloads[n][...] = other[:, part]
        else:
            payloads[n][:height, :] = own[:, part]
            payloads[n][height:, :] = other[:, part]


def second_kernel(outgoing, operator, lift, raw_source, raw, sorting, source, wait, *refs):
    payloads, (keep, source_own, source_other, left) = refs[:3], refs[3:]
    height, width = keep.shape[0], outgoing.shape[0]
    dtype = outgoing.dtype
    start = lax.rem(lax.axis_index(PAIR), 2) * (width - height)
    mine = pl.ds(pl.multiple_of(start, TILE), height)
    picked = sorting[mine, :]
    state = across(picked, raw[...]).astype(dtype)
    source_own[...] = source[mine, :]
    source_other[...] = across(picked, raw_source[...]).astype(dtype)
    left[...] = wait[mine, :]
    other = across(state, operator[...]) + across(inject(source_other, left), lift[...])
    left[...] = left[...] - 1
    store(outgoing[mine, :], other.astype(dtype), payloads, keep)


def early_kernel(own_operator, own_lift, other_operator, other_lift, own_source, other_source, wait, keep, y, z, *refs):
    own_total, other_total, left = refs
    height, rows = keep.shape
    dtype = keep.dtype
    y_in = y[...] * behind("gy", dtype)
    near = behind("gz", dtype)
    for total, operator, lift, source, first, at in (
        (own_total, own_operator, own_lift, own_source, y_in, 0),
        (other_total, other_operator, other_lift, other_source, keep[...], height),
    ):
        stack = jnp.concatenate([first, z[at : at + height, :] * near], axis=1)
        total[...] = across(stack, operator[:, rows:]) + across(inject(source, wait), lift[...])
    left[...] = wait[...] - 1


def late_kernel(own_operator, other_operator, own_total, other_total, x, *refs):
    payloads, keep = refs[:3], refs[3]
    height, rows = keep.shape
    dtype = keep.dtype
    near = behind("gx", dtype)
    outgoing = []
    for total, operator, at in ((own_total, own_operator, 0), (other_total, other_operator, height)):
        share = across(x[at : at + height, :] * near, operator[:, :rows])
        outgoing.append((total[...] + share).astype(dtype))
    store(*outgoing, payloads, keep)


def other_kernel(keep, x, z, out):
    height, rows = keep.shape
    dtype = keep.dtype
    out[:, :rows] = x[height:, :] * behind("gx", dtype)
    out[:, rows : 2 * rows] = keep[...]
    out[:, 2 * rows :] = z[height:, :] * behind("gz", dtype)


def last_kernel(direction, sorting, x, y, z, given, target, stack, out, sems):
    width, order = stack.shape
    height, rows = given.shape[0], order // len(AXES)
    start = width - height
    dtype = stack.dtype
    upward = lax.rem(lax.axis_index(PAIR), 2) == 0
    copies = []
    for n, (axis, face) in enumerate(zip(AXES, (x, y, z))):
        part = slice(n * rows, (n + 1) * rows)
        near = behind(axis, dtype)

        def assemble(low, high, part=part):
            if start:
                stack[:start, part] = low(0, start)
                stack[height:, part] = high(height - start, height)
            if height > start:
                down = jnp.concatenate([direction[start:height, :]] * (rows // LANES), axis=1) > 0
                stack[start:height, part] = jnp.where(down, high(0, height - start), low(start, height))

        own = lambda a, b, face=face, near=near: face[a:b, :] * near
        mates = lambda a, b, part=part: given[a:b, part]
        pl.when(upward)(functools.partial(assemble, own, mates))
        pl.when(jnp.logical_not(upward))(functools.partial(assemble, mates, own))
        back = lax.dot_general(stack[:, part], sorting[...], (((0,), (0,)), ((), ())), preferred_element_type=jnp.float32)
        out[part, :] = back.astype(dtype)
        copies.append(pltpu.make_async_copy(out.at[part, :], target.at[part, :], sems.at[n]))
        copies[-1].start()
    for copy in copies:
        copy.wait()


def shaped(dtype):
    return lambda *dims: jax.ShapeDtypeStruct(dims, dtype)


def call(kernel, outputs, operands, scratch=(), specs=None, sources=None):
    return pl.pallas_call(
        kernel,
        out_shape=outputs,
        in_specs=sources or [VMEM] * len(operands),
        out_specs=specs or [VMEM] * len(outputs),
        scratch_shapes=list(scratch),
        compiler_params=pltpu.CompilerParams(vmem_limit_bytes=16 * 2**20),
    )(*operands)


def begin(arguments, held):
    operator, lift, source, state, depth, direction = arguments
    order, width = state.shape
    inner = order + source.shape[0]
    dtype = state.dtype
    shape = shaped(dtype)
    return call(
        functools.partial(first_kernel, held),
        [shape(width, order), shape(*operator.shape), shape(*lift.shape), shape(width, source.shape[0])]
        + [shape(width, LANES)] * 2
        + [shape(width, width), jax.ShapeDtypeStruct((1,), jnp.int32)],
        [pltpu.with_memory_space_constraint(value, pltpu.HBM) for value in arguments],
        [
            pltpu.VMEM((width, inner), dtype),
            pltpu.VMEM(state.shape, dtype),
            pltpu.VMEM(source.shape, dtype),
            pltpu.SMEM(depth.shape, depth.dtype),
            pltpu.SMEM(direction.shape, direction.dtype),
            pltpu.SMEM(direction.shape, direction.dtype),
            pltpu.SemaphoreType.DMA((4 + 2 * len(AXES),)),
        ],
        [VMEM] * 7 + [SMEM],
        [HBM] * 6,
    )


def finish(height, kept, others):
    outgoing, operator, lift, source, wait, direction, sorting = kept
    other_operator, other_lift, other_source, other_state = others
    width, order = outgoing.shape
    rows, inner = order // len(AXES), source.shape[1]
    dtype = operator.dtype
    shape = shaped(dtype)
    payloads = [shape(height if axis == PAIR else 2 * height, rows) for axis in AXES]
    keep, thin, row = shape(height, rows), shape(height, inner), shape(height, LANES)
    total = jax.ShapeDtypeStruct((height, order), jnp.float32)
    *outs, keep_now, source, other_source, wait = call(
        second_kernel,
        payloads + [keep, thin, thin, row],
        [outgoing, other_operator, other_lift, other_source, other_state, sorting, source, wait],
    )
    for _ in range(1, STEPS):
        x, y, z = pass_on(outs)
        own_total, other_total, wait = call(
            early_kernel,
            [total, total, row],
            [operator, lift, other_operator, other_lift, source, other_source, wait, keep_now, y, z],
        )
        *outs, keep_now = call(late_kernel, payloads + [keep], [operator, other_operator, own_total, other_total, x])
    x, y, z = pass_on(outs)
    (given,) = call(other_kernel, [shape(height, order)], [keep_now, x, z])
    given = permute(given, mate)
    (state,) = call(
        last_kernel,
        [pltpu.HBM((order, width), dtype)],
        [direction, sorting, x, y, z, given],
        [
            pltpu.VMEM((width, order), dtype),
            pltpu.VMEM((order, width), dtype),
            pltpu.SemaphoreType.DMA((len(AXES),)),
        ],
        [HBM],
    )
    return state


def levels(batches):
    extra = [1]
    while extra[-1] < batches // 2:
        extra.append(2 * extra[-1])
    return [batches - batches // 2 + e for e in extra]


def body(operator, lift, source, traces_in, depth, direction):
    batches, width = direction.shape[0], traces_in.shape[-1]
    held = levels(batches)
    own = [value[0, 0, 0] for value in (operator, lift, source, traces_in)]
    others = [permute(value, mate) for value in own]
    *kept, level = begin([*own, depth, direction], held)
    branches = [functools.partial(finish, size * (width // batches)) for size in held]
    return lax.switch(level[0], branches, kept, others).reshape(traces_in.shape)


def solution(mesh):
    placed = P("gx", "gy", "gz", None, None)
    return jax.shard_map(
        body,
        mesh=mesh,
        in_specs=(placed, placed, placed, placed, P(), P()),
        out_specs=placed,
        check_vma=False,
    )
```

time: 149 us -> 70.2 us (0.47)
  starting transfers between devices: 110 us -> 27.5 us
  Pallas kernels: 0 us -> 18.9 us
  other arithmetic: 8.42 us -> 0 us
  matrix products: 6.94 us -> 0 us
  waiting for transfers between devices: 18.9 us -> 21.2 us
    ppermute x36 -> x23, starting transfers between devices: 110 us -> 27.5 us  [permute(): lax.ppermute(value, AXES, [(device(p), device(target(p))) for p in device...]
    pallas_call x0 -> x14, Pallas kernels: none -> 18.9 us  [call(): pl.pallas_call(kernel, out_shape=outputs, in_specs=sources or [VMEM] * le...]
    dot_general x7 -> x0, matrix products: 6.94 us -> none  [the longest x6 5.65 us: body(): jnp.dot(matrix, state, preferred_element_type=jnp.float32) + gate * lifted]
    select_n x6 -> x0, other arithmetic: 6.76 us -> none  [body(): face_x = jnp.where(backward, near_x[2], near_x[0])]
    ppermute x36 -> x23, waiting for transfers between devices: 18.9 us -> 21.2 us  [permute(): lax.ppermute(value, AXES, [(device(p), device(target(p))) for p in device...]
  transfers between devices with their start and end apart: 36 -> 23, of which waited for: 12 -> 9; matrix products, arithmetic and copies ran while one was open for 1% -> 0% of each run, Pallas kernels for 0% -> 17%
where the time goes in v4:
time: 70.2 us; the launch traced here: 69.2 us
  starting transfers between devices  27.5 us (39%)
  waiting for transfers between devices  21.2 us (30%)
  Pallas kernels  18.9 us (27%)
  between operations  0.87 us (1%)
  loops' own time  0.8 us (1%)
    ppermute x23, starting transfers between devices, permute(): lax.ppermute(value, AXES, [(device(p), device(target(p))) for p in device...  27.5 us
    ppermute x23, waiting for transfers between devices, permute(): lax.ppermute(value, AXES, [(device(p), device(target(p))) for p in device...  21.2 us
    pallas_call x14, Pallas kernels, call(): pl.pallas_call(kernel, out_shape=outputs, in_specs=sources or [VMEM] * le...  18.9 us
  transfers between devices with their start and end apart: 23, of which 9 were waited for; matrix products, arithmetic and copies ran while one was open for 0% of the time, Pallas kernels for 17%

profile of v4, /device:TPU:1, one launch (start us, length us, event | category | flops | bytes accessed | tf_op | source)
XLA Modules:
  0.0 69.2 jit_solution(7863574103718413800)
XLA Ops:
  1.0 3.8 %shard_map.67 = (bf16[256,1152]{1,0:T(8,128)(2,1)S(1)}, bf16[1152,1152]{1,0:T(8,128)(2,1)S(1)}, bf16[1152,128]{1,0:T(8,128)(2,1)S(1)}, bf16[256,128]{1,0:T(8,128...) custom-call(bf16[1152,1152]{1,0:T(8,128)(2,1)} %bitcast.9, ...), custom_call_target="tpu_custom_call" | custom-call | tf_op jit(solution)/shard_map/pallas_call | solution.py:224
  5.5 1.0 %collective-permute-done.59 = bf16[128,256]{1,0:T(8,128)(2,1)S(1)} collective-permute-done((bf16[128,256]{1,0:T(8,128)(2,1)}, bf16[128,256]{1,0:T(8,128)(2,1)S(1)}, u32[]{:S(2)}, u32[]{:S(2)}) %collective-permute-start.59) | collective-permute-done | bytes 65568 | tf_op jit(solution)/shard_map/ppermute | solution.py:46
  6.5 62.4 %conditional.1 = (bf16[1,1,1,1152,256]{4,3,2,1,0:T(8,128)(2,1)}) conditional(s32[]{:T(128)} %bitcast.7, (bf16[256,1152]{1,0:T(8,128)(2,1)S(1)}, bf16[1152,1152]{1,0:T(8,128)(2,1)S(1)}, bf16[1152,128]{1,0:T(8,128)(2,1)S(1)}, bf16[128,256]{1,0:T(8,128)(2,1)S(1)}, bf16[1152,256]{1,0:T(8,128)(2,1)S(1)}, ...), branch_computations={%region_0.0_spmd, %region_1.0_spmd, %region_2.0_spmd} | conditional | bytes 25953024 | solution.py:314
  6.7 1.5 %branch_1_fun.13 = (bf16[384,384]{1,0:T(8,128)(2,1)S(1)}, bf16[192,384]{1,0:T(8,128)(2,1)S(1)}, bf16[384,384]{1,0:T(8,128)(2,1)S(1)}, bf16[192,384]{1,0:T(8,128)...) custom-call(bf16[256,1152]{1,0:T(8,128)(2,1)S(1)} %get-tuple-element.134.outgoin, ...), custom_call_target="tpu_custom_call" | custom-call | tf_op jit(solution)/shard_map/cond/branch_1_fun/pallas_call | solution.py:224
  8.4 2.8 %collective-permute-start.21 = (bf16[384,384]{1,0:T(8,128)(2,1)S(1)}, bf16[384,384]{1,0:T(8,128)(2,1)S(1)}, u32[]{:S(2)}, u32[]{:S(2)}) collective-permute-start(bf16[384,384]{1,0:T(8,128)(2,1)S(1)} %get-tuple-element.148), channel_id=1, source_target_pairs={{0,8},{1,9},{2,0},{3,1},{4,12},{5,13},{6,4},{7,5},{8,16},{9,17},{1... | collective-permute-start | bytes 884744 | tf_op jit(solution)/shard_map/cond/branch_1_fun/ppermute | solution.py:46
  11.3 1.6 %collective-permute-start.19 = (bf16[192,384]{1,0:T(8,128)(2,1)S(1)}, bf16[192,384]{1,0:T(8,128)(2,1)S(1)}, u32[]{:S(2)}, u32[]{:S(2)}) collective-permute-start(bf16[192,384]{1,0:T(8,128)(2,1)S(1)} %get-tuple-element.143), channel_id=1, source_target_pairs={{0,4},{1,5},{2,0},{3,1},{4,6},{5,7},{6,2},{7,3},{8,12},{9,13},{10,... | collective-permute-start | bytes 442376 | tf_op jit(solution)/shard_map/cond/branch_1_fun/ppermute | solution.py:46
  12.9 2.4 %collective-permute-done.19.y = bf16[192,384]{1,0:T(8,128)(2,1)S(1)} collective-permute-done((bf16[192,384]{1,0:T(8,128)(2,1)S(1)}, bf16[192,384]{1,0:T(8,128)(2,1)S(1)}, u32[]{:S(2)}, u32[]{:S(2)}) %collective-permute-start.19) | collective-permute-done | bytes 147488 | tf_op jit(solution)/shard_map/cond/branch_1_fun/ppermute | solution.py:46
  15.3 1.4 %branch_1_fun.14 = (f32[192,1152]{1,0:T(8,128)S(1)}, f32[192,1152]{1,0:T(8,128)S(1)}, bf16[192,128]{1,0:T(8,128)(2,1)S(1)}) custom-call(bf16[1152,1152]{1,0:T(8,128)(2,1)S(1)} %get-tuple-element.130.own_operator, bf16[1152,128]{1,0:T(8,128)(2,1)S(1)} %get-tuple-element.132.own_lift, bf16[1152,1152]{1,0:T(8,128)(2,1)S(1)} %get-tuple-element.131.operator.other_operator, ...), custom_call_target="tpu_custom_call" | custom-call | tf_op jit(solution)/shard_map/cond/branch_1_fun/pallas_call | solution.py:224
  17.6 1.8 %collective-permute-start.23 = (bf16[384,384]{1,0:T(8,128)(2,1)S(1)}, bf16[384,384]{1,0:T(8,128)(2,1)S(1)}, u32[]{:S(2)}, u32[]{:S(2)}) collective-permute-start(bf16[384,384]{1,0:T(8,128)(2,1)S(1)} %get-tuple-element.151), channel_id=1, source_target_pairs={{0,1},{1,3},{2,0},{3,2},{4,5},{5,7},{6,4},{7,6},{8,9},{9,11},{10,8... | collective-permute-start | bytes 884744 | tf_op jit(solution)/shard_map/cond/branch_1_fun/ppermute | solution.py:46
  19.4 1.0 %collective-permute-start.24 = (bf16[384,384]{1,0:T(8,128)(2,1)S(1)}, bf16[384,384]{1,0:T(8,128)(2,1)S(1)}, u32[]{:S(2)}, u32[]{:S(2)}) collective-permute-start(bf16[384,384]{1,0:T(8,128)(2,1)S(1)} %get-tuple-element.155), channel_id=1, source_target_pairs={{0,8},{1,9},{2,0},{3,1},{4,12},{5,13},{6,4},{7,5},{8,16},{9,17},{1... | collective-permute-start | bytes 884744 | tf_op jit(solution)/shard_map/cond/branch_1_fun/ppermute | solution.py:46
  20.3 1.6 %collective-permute-start.22 = (bf16[192,384]{1,0:T(8,128)(2,1)S(1)}, bf16[192,384]{1,0:T(8,128)(2,1)S(1)}, u32[]{:S(2)}, u32[]{:S(2)}) collective-permute-start(bf16[192,384]{1,0:T(8,128)(2,1)S(1)} %get-tuple-element.150), channel_id=1, source_target_pairs={{0,4},{1,5},{2,0},{3,1},{4,6},{5,7},{6,2},{7,3},{8,12},{9,13},{10,... | collective-permute-start | bytes 442376 | tf_op jit(solution)/shard_map/cond/branch_1_fun/ppermute | solution.py:46
  21.9 2.4 %collective-permute-done.22.y = bf16[192,384]{1,0:T(8,128)(2,1)S(1)} collective-permute-done((bf16[192,384]{1,0:T(8,128)(2,1)S(1)}, bf16[192,384]{1,0:T(8,128)(2,1)S(1)}, u32[]{:S(2)}, u32[]{:S(2)}) %collective-permute-start.22) | collective-permute-done | bytes 147488 | tf_op jit(solution)/shard_map/cond/branch_1_fun/ppermute | solution.py:46
  24.3 1.4 %branch_1_fun.16 = (f32[192,1152]{1,0:T(8,128)S(1)}, f32[192,1152]{1,0:T(8,128)S(1)}, bf16[192,128]{1,0:T(8,128)(2,1)S(1)}) custom-call(bf16[1152,1152]{1,0:T(8,128)(2,1)S(1)} %get-tuple-element.130.own_operator, bf16[1152,128]{1,0:T(8,128)(2,1)S(1)} %get-tuple-element.132.own_lift, bf16[1152,1152]{1,0:T(8,128)(2,1)S(1)} %get-tuple-element.131.operator.other_operator, ...), custom_call_target="tpu_custom_call" | custom-call | tf_op jit(solution)/shard_map/cond/branch_1_fun/pallas_call | solution.py:224
  26.6 1.9 %collective-permute-start.26 = (bf16[384,384]{1,0:T(8,128)(2,1)S(1)}, bf16[384,384]{1,0:T(8,128)(2,1)S(1)}, u32[]{:S(2)}, u32[]{:S(2)}) collective-permute-start(bf16[384,384]{1,0:T(8,128)(2,1)S(1)} %get-tuple-element.158), channel_id=1, source_target_pairs={{0,1},{1,3},{2,0},{3,2},{4,5},{5,7},{6,4},{7,6},{8,9},{9,11},{10,8... | collective-permute-start | bytes 884744 | tf_op jit(solution)/shard_map/cond/branch_1_fun/ppermute | solution.py:46
  29.3 1.6 %collective-permute-start.25 = (bf16[192,384]{1,0:T(8,128)(2,1)S(1)}, bf16[192,384]{1,0:T(8,128)(2,1)S(1)}, u32[]{:S(2)}, u32[]{:S(2)}) collective-permute-start(bf16[192,384]{1,0:T(8,128)(2,1)S(1)} %get-tuple-element.157), channel_id=1, source_target_pairs={{0,4},{1,5},{2,0},{3,1},{4,6},{5,7},{6,2},{7,3},{8,12},{9,13},{10,... | collective-permute-start | bytes 442376 | tf_op jit(solution)/shard_map/cond/branch_1_fun/ppermute | solution.py:46
  30.9 2.4 %collective-permute-done.25.y = bf16[192,384]{1,0:T(8,128)(2,1)S(1)} collective-permute-done((bf16[192,384]{1,0:T(8,128)(2,1)S(1)}, bf16[192,384]{1,0:T(8,128)(2,1)S(1)}, u32[]{:S(2)}, u32[]{:S(2)}) %collective-permute-start.25) | collective-permute-done | bytes 147488 | tf_op jit(solution)/shard_map/cond/branch_1_fun/ppermute | solution.py:46
  33.3 1.4 %branch_1_fun.18 = (f32[192,1152]{1,0:T(8,128)S(1)}, f32[192,1152]{1,0:T(8,128)S(1)}, bf16[192,128]{1,0:T(8,128)(2,1)S(1)}) custom-call(bf16[1152,1152]{1,0:T(8,128)(2,1)S(1)} %get-tuple-element.130.own_operator, bf16[1152,128]{1,0:T(8,128)(2,1)S(1)} %get-tuple-element.132.own_lift, bf16[1152,1152]{1,0:T(8,128)(2,1)S(1)} %get-tuple-element.131.operator.other_operator, ...), custom_call_target="tpu_custom_call" | custom-call | tf_op jit(solution)/shard_map/cond/branch_1_fun/pallas_call | solution.py:224
  35.6 2.0 %collective-permute-start.29 = (bf16[384,384]{1,0:T(8,128)(2,1)S(1)}, bf16[384,384]{1,0:T(8,128)(2,1)S(1)}, u32[]{:S(2)}, u32[]{:S(2)}) collective-permute-start(bf16[384,384]{1,0:T(8,128)(2,1)S(1)} %get-tuple-element.165), channel_id=1, source_target_pairs={{0,1},{1,3},{2,0},{3,2},{4,5},{5,7},{6,4},{7,6},{8,9},{9,11},{10,8... | collective-permute-start | bytes 884744 | tf_op jit(solution)/shard_map/cond/branch_1_fun/ppermute | solution.py:46
  38.4 1.6 %collective-permute-start.28 = (bf16[192,384]{1,0:T(8,128)(2,1)S(1)}, bf16[192,384]{1,0:T(8,128)(2,1)S(1)}, u32[]{:S(2)}, u32[]{:S(2)}) collective-permute-start(bf16[192,384]{1,0:T(8,128)(2,1)S(1)} %get-tuple-element.164), channel_id=1, source_target_pairs={{0,4},{1,5},{2,0},{3,1},{4,6},{5,7},{6,2},{7,3},{8,12},{9,13},{10,... | collective-permute-start | bytes 442376 | tf_op jit(solution)/shard_map/cond/branch_1_fun/ppermute | solution.py:46
  39.9 2.4 %collective-permute-done.28.y = bf16[192,384]{1,0:T(8,128)(2,1)S(1)} collective-permute-done((bf16[192,384]{1,0:T(8,128)(2,1)S(1)}, bf16[192,384]{1,0:T(8,128)(2,1)S(1)}, u32[]{:S(2)}, u32[]{:S(2)}) %collective-permute-start.28) | collective-permute-done | bytes 147488 | tf_op jit(solution)/shard_map/cond/branch_1_fun/ppermute | solution.py:46
  42.4 1.4 %branch_1_fun.20 = (f32[192,1152]{1,0:T(8,128)S(1)}, f32[192,1152]{1,0:T(8,128)S(1)}, bf16[192,128]{1,0:T(8,128)(2,1)S(1)}) custom-call(bf16[1152,1152]{1,0:T(8,128)(2,1)S(1)} %get-tuple-element.130.own_operator, bf16[1152,128]{1,0:T(8,128)(2,1)S(1)} %get-tuple-element.132.own_lift, bf16[1152,1152]{1,0:T(8,128)(2,1)S(1)} %get-tuple-element.131.operator.other_operator, ...), custom_call_target="tpu_custom_call" | custom-call | tf_op jit(solution)/shard_map/cond/branch_1_fun/pallas_call | solution.py:224
  44.6 2.0 %collective-permute-start.32 = (bf16[384,384]{1,0:T(8,128)(2,1)S(1)}, bf16[384,384]{1,0:T(8,128)(2,1)S(1)}, u32[]{:S(2)}, u32[]{:S(2)}) collective-permute-start(bf16[384,384]{1,0:T(8,128)(2,1)S(1)} %get-tuple-element.172), channel_id=1, source_target_pairs={{0,1},{1,3},{2,0},{3,2},{4,5},{5,7},{6,4},{7,6},{8,9},{9,11},{10,8... | collective-permute-start | bytes 884744 | tf_op jit(solution)/shard_map/cond/branch_1_fun/ppermute | solution.py:46
  47.4 1.6 %collective-permute-start.31 = (bf16[192,384]{1,0:T(8,128)(2,1)S(1)}, bf16[192,384]{1,0:T(8,128)(2,1)S(1)}, u32[]{:S(2)}, u32[]{:S(2)}) collective-permute-start(bf16[192,384]{1,0:T(8,128)(2,1)S(1)} %get-tuple-element.171), channel_id=1, source_target_pairs={{0,4},{1,5},{2,0},{3,1},{4,6},{5,7},{6,2},{7,3},{8,12},{9,13},{10,... | collective-permute-start | bytes 442376 | tf_op jit(solution)/shard_map/cond/branch_1_fun/ppermute | solution.py:46
  49.0 2.4 %collective-permute-done.31.y = bf16[192,384]{1,0:T(8,128)(2,1)S(1)} collective-permute-done((bf16[192,384]{1,0:T(8,128)(2,1)S(1)}, bf16[192,384]{1,0:T(8,128)(2,1)S(1)}, u32[]{:S(2)}, u32[]{:S(2)}) %collective-permute-start.31) | collective-permute-done | bytes 147488 | tf_op jit(solution)/shard_map/cond/branch_1_fun/ppermute | solution.py:46
  51.4 2.0 %branch_1_fun.22 = (f32[192,1152]{1,0:T(8,128)S(1)}, f32[192,1152]{1,0:T(8,128)S(1)}, bf16[192,128]{1,0:T(8,128)(2,1)}) custom-call(bf16[1152,1152]{1,0:T(8,128)(2,1)S(1)} %get-tuple-element.130.own_operator, bf16[1152,128]{1,0:T(8,128)(2,1)S(1)} %get-tuple-element.132.own_lift, bf16[1152,1152]{1,0:T(8,128)(2,1)S(1)} %get-tuple-element.131.operator.other_operator, ...), custom_call_target="tpu_custom_call" | custom-call | tf_op jit(solution)/shard_map/cond/branch_1_fun/pallas_call | solution.py:224
  54.2 2.0 %collective-permute-start.34 = (bf16[384,384]{1,0:T(8,128)(2,1)S(1)}, bf16[384,384]{1,0:T(8,128)(2,1)S(1)}, u32[]{:S(2)}, u32[]{:S(2)}) collective-permute-start(bf16[384,384]{1,0:T(8,128)(2,1)S(1)} %get-tuple-element.176), channel_id=1, source_target_pairs={{0,8},{1,9},{2,0},{3,1},{4,12},{5,13},{6,4},{7,5},{8,16},{9,17},{1... | collective-permute-start | bytes 884744 | tf_op jit(solution)/shard_map/cond/branch_1_fun/ppermute | solution.py:46
  56.2 1.5 %collective-permute-start.36 = (bf16[384,384]{1,0:T(8,128)(2,1)S(1)}, bf16[384,384]{1,0:T(8,128)(2,1)S(1)}, u32[]{:S(2)}, u32[]{:S(2)}) collective-permute-start(bf16[384,384]{1,0:T(8,128)(2,1)S(1)} %get-tuple-element.178), channel_id=1, source_target_pairs={{0,1},{1,3},{2,0},{3,2},{4,5},{5,7},{6,4},{7,6},{8,9},{9,11},{10,8... | collective-permute-start | bytes 884744 | tf_op jit(solution)/shard_map/cond/branch_1_fun/ppermute | solution.py:46
  57.7 2.3 %collective-permute-done.34.x = bf16[384,384]{1,0:T(8,128)(2,1)S(1)} collective-permute-done((bf16[384,384]{1,0:T(8,128)(2,1)S(1)}, bf16[384,384]{1,0:T(8,128)(2,1)S(1)}, u32[]{:S(2)}, u32[]{:S(2)}) %collective-permute-start.34) | collective-permute-done | bytes 294944 | tf_op jit(solution)/shard_map/cond/branch_1_fun/ppermute | solution.py:46
  60.1 1.7 %collective-permute-done.36.z = bf16[384,384]{1,0:T(8,128)(2,1)S(1)} collective-permute-done((bf16[384,384]{1,0:T(8,128)(2,1)S(1)}, bf16[384,384]{1,0:T(8,128)(2,1)S(1)}, u32[]{:S(2)}, u32[]{:S(2)}) %collective-permute-start.36) | collective-permute-done | bytes 294944 | tf_op jit(solution)/shard_map/cond/branch_1_fun/ppermute | solution.py:46
  61.8 1.1 %collective-permute-start.37 = (bf16[192,1152]{1,0:T(8,128)(2,1)S(1)}, bf16[192,1152]{1,0:T(8,128)(2,1)S(1)}, u32[]{:S(2)}, u32[]{:S(2)}) collective-permute-start(bf16[192,1152]{1,0:T(8,128)(2,1)S(1)} %branch_1_fun.24), channel_id=1, source_target_pairs={{0,2},{1,3},{2,0},{3,1},{4,6},{5,7},{6,4},{7,5},{8,10},{9,11},{10,... | collective-permute-start | bytes 1327112 | tf_op jit(solution)/shard_map/cond/branch_1_fun/ppermute | solution.py:46
  62.9 4.0 %collective-permute-done.35.y = bf16[192,384]{1,0:T(8,128)(2,1)S(1)} collective-permute-done((bf16[192,384]{1,0:T(8,128)(2,1)S(1)}, bf16[192,384]{1,0:T(8,128)(2,1)S(1)}, u32[]{:S(2)}, u32[]{:S(2)}) %collective-permute-start.35) | collective-permute-done | bytes 147488 | tf_op jit(solution)/shard_map/cond/branch_1_fun/ppermute | solution.py:46
  66.9 1.6 %branch_1_fun.25 = bf16[1152,256]{1,0:T(8,128)(2,1)} custom-call(bf16[256,128]{1,0:T(8,128)(2,1)S(1)} %get-tuple-element.128.direction, bf16[256,256]{1,0:T(8,128)(2,1)S(1)} %get-tuple-element.129.sorting, bf16[384,384]{1,0:T(8,128)(2,1)S(1)} %collective-permute-done.34.x, bf16[192,384]{1,0:T(8,128)(2,1)S(1)} %collective-permute-done.35.y, ...), custom_call_target="tpu_custom_call" | custom-call | tf_op jit(solution)/shard_map/cond/branch_1_fun/pallas_call | solution.py:224
  (29 shorter events, 7.7 us)
Async XLA Ops:
  0.0 6.5 %collective-permute-start.57 = (bf16[1152,1152]{1,0:T(8,128)(2,1)}, bf16[1152,1152]{1,0:T(8,128)(2,1)S(1)}, u32[]{:S(2)}, u32[]{:S(2)}) collective-permute-start(bf16[1152,1152]{1,0:T(8,128)(2,1)} %bitcast.8), channel_id=1, source_target_pairs={{0,2},{1,3},{2,0},{3,1},{4,6},{5,7},{6,4},{7,5},{8,10},{9,11},{10,... | collective-permute-start | bytes 7962632 | tf_op jit(solution)/shard_map/ppermute | solution.py:46
  0.0 6.5 %collective-permute-start.60 = (bf16[1152,256]{1,0:T(8,128)(2,1)}, bf16[1152,256]{1,0:T(8,128)(2,1)S(1)}, u32[]{:S(2)}, u32[]{:S(2)}) collective-permute-start(bf16[1152,256]{1,0:T(8,128)(2,1)} %bitcast.13), channel_id=1, source_target_pairs={{0,2},{1,3},{2,0},{3,1},{4,6},{5,7},{6,4},{7,5},{8,10},{9,11},{10,... | collective-permute-start | bytes 1769480 | tf_op jit(solution)/shard_map/ppermute | solution.py:46
  0.5 6.0 %collective-permute-start.58 = (bf16[1152,128]{1,0:T(8,128)(2,1)}, bf16[1152,128]{1,0:T(8,128)(2,1)S(1)}, u32[]{:S(2)}, u32[]{:S(2)}) collective-permute-start(bf16[1152,128]{1,0:T(8,128)(2,1)} %bitcast.15), channel_id=1, source_target_pairs={{0,2},{1,3},{2,0},{3,1},{4,6},{5,7},{6,4},{7,5},{8,10},{9,11},{10,... | collective-permute-start | bytes 884744 | tf_op jit(solution)/shard_map/ppermute | solution.py:46
  0.5 6.0 %collective-permute-start.59 = (bf16[128,256]{1,0:T(8,128)(2,1)}, bf16[128,256]{1,0:T(8,128)(2,1)S(1)}, u32[]{:S(2)}, u32[]{:S(2)}) collective-permute-start(bf16[128,256]{1,0:T(8,128)(2,1)} %bitcast.17), channel_id=1, source_target_pairs={{0,2},{1,3},{2,0},{3,1},{4,6},{5,7},{6,4},{7,5},{8,10},{9,11},{10,... | collective-permute-start | bytes 196616 | tf_op jit(solution)/shard_map/ppermute | solution.py:46
  8.3 7.0 %collective-permute-start.20 = (bf16[384,384]{1,0:T(8,128)(2,1)S(1)}, bf16[384,384]{1,0:T(8,128)(2,1)S(1)}, u32[]{:S(2)}, u32[]{:S(2)}) collective-permute-start(bf16[384,384]{1,0:T(8,128)(2,1)S(1)} %get-tuple-element.144), channel_id=1, source_target_pairs={{0,1},{1,3},{2,0},{3,2},{4,5},{5,7},{6,4},{7,6},{8,9},{9,11},{10,8... | collective-permute-start | bytes 884744 | tf_op jit(solution)/shard_map/cond/branch_1_fun/ppermute | solution.py:46
  8.4 8.3 %collective-permute-start.21 = (bf16[384,384]{1,0:T(8,128)(2,1)S(1)}, bf16[384,384]{1,0:T(8,128)(2,1)S(1)}, u32[]{:S(2)}, u32[]{:S(2)}) collective-permute-start(bf16[384,384]{1,0:T(8,128)(2,1)S(1)} %get-tuple-element.148), channel_id=1, source_target_pairs={{0,8},{1,9},{2,0},{3,1},{4,12},{5,13},{6,4},{7,5},{8,16},{9,17},{1... | collective-permute-start | bytes 884744 | tf_op jit(solution)/shard_map/cond/branch_1_fun/ppermute | solution.py:46
  11.3 4.0 %collective-permute-start.19 = (bf16[192,384]{1,0:T(8,128)(2,1)S(1)}, bf16[192,384]{1,0:T(8,128)(2,1)S(1)}, u32[]{:S(2)}, u32[]{:S(2)}) collective-permute-start(bf16[192,384]{1,0:T(8,128)(2,1)S(1)} %get-tuple-element.143), channel_id=1, source_target_pairs={{0,4},{1,5},{2,0},{3,1},{4,6},{5,7},{6,2},{7,3},{8,12},{9,13},{10,... | collective-permute-start | bytes 442376 | tf_op jit(solution)/shard_map/cond/branch_1_fun/ppermute | solution.py:46
  17.6 6.7 %collective-permute-start.23 = (bf16[384,384]{1,0:T(8,128)(2,1)S(1)}, bf16[384,384]{1,0:T(8,128)(2,1)S(1)}, u32[]{:S(2)}, u32[]{:S(2)}) collective-permute-start(bf16[384,384]{1,0:T(8,128)(2,1)S(1)} %get-tuple-element.151), channel_id=1, source_target_pairs={{0,1},{1,3},{2,0},{3,2},{4,5},{5,7},{6,4},{7,6},{8,9},{9,11},{10,8... | collective-permute-start | bytes 884744 | tf_op jit(solution)/shard_map/cond/branch_1_fun/ppermute | solution.py:46
  19.4 6.4 %collective-permute-start.24 = (bf16[384,384]{1,0:T(8,128)(2,1)S(1)}, bf16[384,384]{1,0:T(8,128)(2,1)S(1)}, u32[]{:S(2)}, u32[]{:S(2)}) collective-permute-start(bf16[384,384]{1,0:T(8,128)(2,1)S(1)} %get-tuple-element.155), channel_id=1, source_target_pairs={{0,8},{1,9},{2,0},{3,1},{4,12},{5,13},{6,4},{7,5},{8,16},{9,17},{1... | collective-permute-start | bytes 884744 | tf_op jit(solution)/shard_map/cond/branch_1_fun/ppermute | solution.py:46
  20.3 4.0 %collective-permute-start.22 = (bf16[192,384]{1,0:T(8,128)(2,1)S(1)}, bf16[192,384]{1,0:T(8,128)(2,1)S(1)}, u32[]{:S(2)}, u32[]{:S(2)}) collective-permute-start(bf16[192,384]{1,0:T(8,128)(2,1)S(1)} %get-tuple-element.150), channel_id=1, source_target_pairs={{0,4},{1,5},{2,0},{3,1},{4,6},{5,7},{6,2},{7,3},{8,12},{9,13},{10,... | collective-permute-start | bytes 442376 | tf_op jit(solution)/shard_map/cond/branch_1_fun/ppermute | solution.py:46
  26.6 6.7 %collective-permute-start.26 = (bf16[384,384]{1,0:T(8,128)(2,1)S(1)}, bf16[384,384]{1,0:T(8,128)(2,1)S(1)}, u32[]{:S(2)}, u32[]{:S(2)}) collective-permute-start(bf16[384,384]{1,0:T(8,128)(2,1)S(1)} %get-tuple-element.158), channel_id=1, source_target_pairs={{0,1},{1,3},{2,0},{3,2},{4,5},{5,7},{6,4},{7,6},{8,9},{9,11},{10,8... | collective-permute-start | bytes 884744 | tf_op jit(solution)/shard_map/cond/branch_1_fun/ppermute | solution.py:46
  28.5 6.3 %collective-permute-start.27 = (bf16[384,384]{1,0:T(8,128)(2,1)S(1)}, bf16[384,384]{1,0:T(8,128)(2,1)S(1)}, u32[]{:S(2)}, u32[]{:S(2)}) collective-permute-start(bf16[384,384]{1,0:T(8,128)(2,1)S(1)} %get-tuple-element.162), channel_id=1, source_target_pairs={{0,8},{1,9},{2,0},{3,1},{4,12},{5,13},{6,4},{7,5},{8,16},{9,17},{1... | collective-permute-start | bytes 884744 | tf_op jit(solution)/shard_map/cond/branch_1_fun/ppermute | solution.py:46
  29.3 4.0 %collective-permute-start.25 = (bf16[192,384]{1,0:T(8,128)(2,1)S(1)}, bf16[192,384]{1,0:T(8,128)(2,1)S(1)}, u32[]{:S(2)}, u32[]{:S(2)}) collective-permute-start(bf16[192,384]{1,0:T(8,128)(2,1)S(1)} %get-tuple-element.157), channel_id=1, source_target_pairs={{0,4},{1,5},{2,0},{3,1},{4,6},{5,7},{6,2},{7,3},{8,12},{9,13},{10,... | collective-permute-start | bytes 442376 | tf_op jit(solution)/shard_map/cond/branch_1_fun/ppermute | solution.py:46
  35.6 6.7 %collective-permute-start.29 = (bf16[384,384]{1,0:T(8,128)(2,1)S(1)}, bf16[384,384]{1,0:T(8,128)(2,1)S(1)}, u32[]{:S(2)}, u32[]{:S(2)}) collective-permute-start(bf16[384,384]{1,0:T(8,128)(2,1)S(1)} %get-tuple-element.165), channel_id=1, source_target_pairs={{0,1},{1,3},{2,0},{3,2},{4,5},{5,7},{6,4},{7,6},{8,9},{9,11},{10,8... | collective-permute-start | bytes 884744 | tf_op jit(solution)/shard_map/cond/branch_1_fun/ppermute | solution.py:46
  37.6 6.2 %collective-permute-start.30 = (bf16[384,384]{1,0:T(8,128)(2,1)S(1)}, bf16[384,384]{1,0:T(8,128)(2,1)S(1)}, u32[]{:S(2)}, u32[]{:S(2)}) collective-permute-start(bf16[384,384]{1,0:T(8,128)(2,1)S(1)} %get-tuple-element.169), channel_id=1, source_target_pairs={{0,8},{1,9},{2,0},{3,1},{4,12},{5,13},{6,4},{7,5},{8,16},{9,17},{1... | collective-permute-start | bytes 884744 | tf_op jit(solution)/shard_map/cond/branch_1_fun/ppermute | solution.py:46
  38.4 4.0 %collective-permute-start.28 = (bf16[192,384]{1,0:T(8,128)(2,1)S(1)}, bf16[192,384]{1,0:T(8,128)(2,1)S(1)}, u32[]{:S(2)}, u32[]{:S(2)}) collective-permute-start(bf16[192,384]{1,0:T(8,128)(2,1)S(1)} %get-tuple-element.164), channel_id=1, source_target_pairs={{0,4},{1,5},{2,0},{3,1},{4,6},{5,7},{6,2},{7,3},{8,12},{9,13},{10,... | collective-permute-start | bytes 442376 | tf_op jit(solution)/shard_map/cond/branch_1_fun/ppermute | solution.py:46
  44.6 6.7 %collective-permute-start.32 = (bf16[384,384]{1,0:T(8,128)(2,1)S(1)}, bf16[384,384]{1,0:T(8,128)(2,1)S(1)}, u32[]{:S(2)}, u32[]{:S(2)}) collective-permute-start(bf16[384,384]{1,0:T(8,128)(2,1)S(1)} %get-tuple-element.172), channel_id=1, source_target_pairs={{0,1},{1,3},{2,0},{3,2},{4,5},{5,7},{6,4},{7,6},{8,9},{9,11},{10,8... | collective-permute-start | bytes 884744 | tf_op jit(solution)/shard_map/cond/branch_1_fun/ppermute | solution.py:46
  46.6 6.8 %collective-permute-start.33 = (bf16[384,384]{1,0:T(8,128)(2,1)S(1)}, bf16[384,384]{1,0:T(8,128)(2,1)S(1)}, u32[]{:S(2)}, u32[]{:S(2)}) collective-permute-start(bf16[384,384]{1,0:T(8,128)(2,1)S(1)} %get-tuple-element.175), channel_id=1, source_target_pairs={{0,8},{1,9},{2,0},{3,1},{4,12},{5,13},{6,4},{7,5},{8,16},{9,17},{1... | collective-permute-start | bytes 884744 | tf_op jit(solution)/shard_map/cond/branch_1_fun/ppermute | solution.py:46
  47.4 4.0 %collective-permute-start.31 = (bf16[192,384]{1,0:T(8,128)(2,1)S(1)}, bf16[192,384]{1,0:T(8,128)(2,1)S(1)}, u32[]{:S(2)}, u32[]{:S(2)}) collective-permute-start(bf16[192,384]{1,0:T(8,128)(2,1)S(1)} %get-tuple-element.171), channel_id=1, source_target_pairs={{0,4},{1,5},{2,0},{3,1},{4,6},{5,7},{6,2},{7,3},{8,12},{9,13},{10,... | collective-permute-start | bytes 442376 | tf_op jit(solution)/shard_map/cond/branch_1_fun/ppermute | solution.py:46
  54.2 5.9 %collective-permute-start.34 = (bf16[384,384]{1,0:T(8,128)(2,1)S(1)}, bf16[384,384]{1,0:T(8,128)(2,1)S(1)}, u32[]{:S(2)}, u32[]{:S(2)}) collective-permute-start(bf16[384,384]{1,0:T(8,128)(2,1)S(1)} %get-tuple-element.176), channel_id=1, source_target_pairs={{0,8},{1,9},{2,0},{3,1},{4,12},{5,13},{6,4},{7,5},{8,16},{9,17},{1... | collective-permute-start | bytes 884744 | tf_op jit(solution)/shard_map/cond/branch_1_fun/ppermute | solution.py:46
  56.2 5.6 %collective-permute-start.36 = (bf16[384,384]{1,0:T(8,128)(2,1)S(1)}, bf16[384,384]{1,0:T(8,128)(2,1)S(1)}, u32[]{:S(2)}, u32[]{:S(2)}) collective-permute-start(bf16[384,384]{1,0:T(8,128)(2,1)S(1)} %get-tuple-element.178), channel_id=1, source_target_pairs={{0,1},{1,3},{2,0},{3,2},{4,5},{5,7},{6,4},{7,6},{8,9},{9,11},{10,8... | collective-permute-start | bytes 884744 | tf_op jit(solution)/shard_map/cond/branch_1_fun/ppermute | solution.py:46
  61.8 5.1 %collective-permute-start.37 = (bf16[192,1152]{1,0:T(8,128)(2,1)S(1)}, bf16[192,1152]{1,0:T(8,128)(2,1)S(1)}, u32[]{:S(2)}, u32[]{:S(2)}) collective-permute-start(bf16[192,1152]{1,0:T(8,128)(2,1)S(1)} %branch_1_fun.24), channel_id=1, source_target_pairs={{0,2},{1,3},{2,0},{3,1},{4,6},{5,7},{6,4},{7,5},{8,10},{9,11},{10,... | collective-permute-start | bytes 1327112 | tf_op jit(solution)/shard_map/cond/branch_1_fun/ppermute | solution.py:46
  62.9 4.0 %collective-permute-start.35 = (bf16[192,384]{1,0:T(8,128)(2,1)S(1)}, bf16[192,384]{1,0:T(8,128)(2,1)S(1)}, u32[]{:S(2)}, u32[]{:S(2)}) collective-permute-start(bf16[192,384]{1,0:T(8,128)(2,1)S(1)} %get-tuple-element.177), channel_id=1, source_target_pairs={{0,4},{1,5},{2,0},{3,1},{4,6},{5,7},{6,2},{7,3},{8,12},{9,13},{10,... | collective-permute-start | bytes 442376 | tf_op jit(solution)/shard_map/cond/branch_1_fun/ppermute | solution.py:46
